TPU v7x, 32 devices: a whole 2x2x4 slice. The times are simulated.
32 devices in a mesh: dp: 4 (over y, x), row: 4 (over z), col: 2 (over core).
Axes of the slice: x: 2, y: 2, z: 4, core: 2. Of those that a mesh axis runs over, the one named last changes fastest.
Arguments:
- hidden: bfloat16 [4096, 2048], P(('dp', 'row'), 'col'), may hold values from -6 to 6
- norm_before: float32 [2048], P('col'), may hold values from 0.1 to 1.9
- query_weight: bfloat16 [2048, 2048], P('col', 'row'), may hold values from -0.125 to 0.125
- key_matrix: bfloat16 [2048, 1024], P('col', 'row'), may hold values from -0.125 to 0.125
- value_matrix: bfloat16 [2048, 1024], P('col', 'row'), may hold values from -0.125 to 0.125
- query_gain: float32 [128], replicated, may hold values from 0.5 to 2
- key_gain: float32 [128], replicated, may hold values from 0.5 to 2
- output_weight: bfloat16 [2048, 2048], P('row', 'col'), may hold values from -1 to 1
- norm_after: float32 [2048], P('col'), may hold values from 0.1 to 1.9
- gate_weight: bfloat16 [2048, 6144], P('col', 'row'), may hold values from -0.125 to 0.125
- up_weight: bfloat16 [2048, 6144], P('col', 'row'), may hold values from -0.125 to 0.125
- down_weight: bfloat16 [6144, 2048], P('row', 'col'), may hold values from -0.078125 to 0.078125
- cotangent: bfloat16 [4096, 2048], P(('dp', 'row'), 'col'), may hold values from -6 to 6
Outputs:
- layer_out: bfloat16 [4096, 2048], P(('dp', 'row'), 'col')
- hidden_grad: float32 [4096, 2048], P(('dp', 'row'), 'col')
- before_grad: float32 [2048], P('col')
- query_grad: float32 [2048, 2048], P('col', 'row')
- key_grad: float32 [2048, 1024], P('col', 'row')
- value_grad: float32 [2048, 1024], P('col', 'row')
- gain_query: float32 [128], replicated
- gain_key: float32 [128], replicated
- output_grad: float32 [2048, 2048], P('row', 'col')
- after_grad: float32 [2048], P('col')
- gate_grad: float32 [2048, 6144], P('col', 'row')
- up_grad: float32 [2048, 6144], P('col', 'row')
- down_grad: float32 [6144, 2048], P('row', 'col')
All inputs are finite; a program needn't handle non-finite values.
Results may differ from a plain program's by a relative error of at most 0.017.
Values may be sent and summed in bfloat16 or wider, within the bound.
No kernel may reach another device: no remote copies, remote signals or barrier semaphores. Data moves between devices by JAX's collectives and lax.ppermute only.
A program may use at most 192 MiB of HBM per device.

v0:
```python
import math

import jax
import jax.numpy as jnp
from jax import lax
from jax.sharding import PartitionSpec as P

MODEL_WIDTH = 2048
QUERY_HEADS = 16
KEY_VALUE_HEADS = 8
HEAD_SIZE = 128
SEQUENCE_LENGTH = 1024


EPS = 1e-06
THETA = 1000000.0


def width_sum(value_rows):
    return lax.psum(value_rows, "col")


def gather_rows(value_rows):
    return lax.all_gather(value_rows, "row", axis=0, tiled=True)


def reduce_rows(value_rows):
    return lax.psum_scatter(value_rows, "row", scatter_dimension=0, tiled=True)


def gather_share(value_rows):
    return lax.all_gather(value_rows, "col", axis=1, tiled=True)


def reduce_share(value_rows):
    return lax.psum_scatter(value_rows, "col", scatter_dimension=1, tiled=True)


def every_gains(leading_part, second, third, fourth):
    return lax.psum((leading_part, second, third, fourth), ("dp", "row", "col"))


def norm_forward(value_rows, gain):
    total = width_sum(jnp.sum(value_rows * value_rows, axis=1))
    factor = lax.rsqrt(total / MODEL_WIDTH + EPS)
    unit = value_rows * factor[:, None]
    return (unit, factor, (unit * gain).astype(jnp.bfloat16))


def norm_backward(grad, unit, factor, gain):
    scaled = grad * gain
    inner = width_sum(jnp.sum(scaled * unit, axis=1)) / MODEL_WIDTH
    return (factor[:, None] * (scaled - unit * inner[:, None]), jnp.sum(grad * unit, axis=0))


def head_norm(value_rows, gain):
    factor = lax.rsqrt(jnp.mean(value_rows * value_rows, axis=-1, keepdims=True) + EPS)
    unit = value_rows * factor
    return (unit, factor, unit * gain)


def head_norm_back(grad, unit, factor, gain):
    scaled = grad * gain
    inner = jnp.mean(scaled * unit, axis=-1, keepdims=True)
    return (factor * (scaled - unit * inner), jnp.sum(grad * unit, axis=(0, 1, 2)))


def rope_tables():
    half = HEAD_SIZE // 2
    freq = THETA ** (-(jnp.arange(half, dtype=jnp.float32) * 2.0) / HEAD_SIZE)
    angle = jnp.arange(SEQUENCE_LENGTH, dtype=jnp.float32)[:, None] * freq[None, :]
    cosine = jnp.cos(angle)
    sine = jnp.sin(angle)
    return (jnp.concatenate([cosine, cosine], 1), jnp.concatenate([-sine, sine], 1))


def rotate(value_rows, cosine, sine):
    return (
        value_rows * cosine[None, :, None, :]
        + jnp.roll(value_rows, HEAD_SIZE // 2, axis=3) * sine[None, :, None, :]
    )


def unrotate(grad, cosine, sine):
    return grad * cosine[None, :, None, :] + jnp.roll(
        grad * sine[None, :, None, :], HEAD_SIZE // 2, axis=3
    )


def masked_scores(query, key):
    raw = jnp.einsum("qhgd,phd->hgqp", query, key, preferred_element_type=jnp.float32)
    places = jnp.arange(SEQUENCE_LENGTH)
    causal = (places[:, None] >= places[None, :])[None, None]
    return jnp.where(causal, raw * (1.0 / math.sqrt(HEAD_SIZE)), -1e30)


def attend(blocks):
    query, key, value_tensor = blocks
    scores = masked_scores(query, key)
    top = jnp.max(scores, axis=3, keepdims=True)
    expo = jnp.exp(scores - top)
    total = jnp.sum(expo, axis=3, keepdims=True)
    prob = (expo / total).astype(jnp.bfloat16)
    result = jnp.einsum("hgqp,phd->qhgd", prob, value_tensor, preferred_element_type=jnp.float32)
    return (result, (top + jnp.log(total))[..., 0])


def attend_back(blocks):
    query, key, value_tensor, logsum, grad_out = blocks
    scores = masked_scores(query, key)
    prob = jnp.exp(scores - logsum[..., None])
    dprob = jnp.einsum("qhgd,phd->hgqp", grad_out, value_tensor, preferred_element_type=jnp.float32)
    delta = jnp.sum(prob * dprob, axis=3, keepdims=True)
    dscore = (1.0 / math.sqrt(HEAD_SIZE) * prob * (dprob - delta)).astype(jnp.bfloat16)
    grad_query = jnp.einsum("hgqp,phd->qhgd", dscore, key, preferred_element_type=jnp.float32)
    grad_key = jnp.einsum("hgqp,qhgd->phd", dscore, query, preferred_element_type=jnp.float32)
    grad_value = jnp.einsum(
        "hgqp,qhgd->phd", prob.astype(jnp.bfloat16), grad_out, preferred_element_type=jnp.float32
    )
    return (grad_query, grad_key, grad_value)


def product(left, right, form):
    return jnp.einsum(form, left, right, preferred_element_type=jnp.float32)


def on_device(
    hidden,
    norm_before,
    query_weight,
    key_matrix,
    value_matrix,
    query_gain,
    key_gain,
    output_weight,
    norm_after,
    gate_weight,
    up_weight,
    down_weight,
    cotangent,
):
    head_group = QUERY_HEADS // KEY_VALUE_HEADS
    cosine, sine = rope_tables()
    resid = hidden.astype(jnp.float32)
    unit_one, factor_one, sent_one = norm_forward(resid, norm_before)
    full_one = gather_rows(sent_one)
    query_part = product(full_one, query_weight, "td,dq->tq")
    key_part = product(full_one, key_matrix, "td,dq->tq")
    value_part = product(full_one, value_matrix, "td,dq->tq")
    query_raw, key_unnormed, value_raw = (
        lax.psum_scatter(query_part, "col", scatter_dimension=1, tiled=True),
        lax.psum_scatter(key_part, "col", scatter_dimension=1, tiled=True),
        lax.psum_scatter(value_part, "col", scatter_dimension=1, tiled=True),
    )
    tokens = query_raw.shape[0]
    seqs = tokens // SEQUENCE_LENGTH
    q_heads = query_raw.shape[1] // HEAD_SIZE
    kv_heads = key_unnormed.shape[1] // HEAD_SIZE
    q_unit, q_factor, q_gained = head_norm(
        query_raw.reshape(seqs, SEQUENCE_LENGTH, q_heads, HEAD_SIZE), query_gain
    )
    k_unit, k_factor, k_gained = head_norm(
        key_unnormed.reshape(seqs, SEQUENCE_LENGTH, kv_heads, HEAD_SIZE), key_gain
    )
    query = (
        rotate(q_gained, cosine, sine)
        .astype(jnp.bfloat16)
        .reshape(seqs, SEQUENCE_LENGTH, kv_heads, head_group, HEAD_SIZE)
    )
    key = rotate(k_gained, cosine, sine).astype(jnp.bfloat16)
    value_tensor = value_raw.astype(jnp.bfloat16).reshape(
        seqs, SEQUENCE_LENGTH, kv_heads, HEAD_SIZE
    )
    attended, logsum = lax.map(attend, (query, key, value_tensor))
    att_full = gather_share(attended.reshape(tokens, q_heads * HEAD_SIZE).astype(jnp.bfloat16))
    middle = resid + reduce_rows(product(att_full, output_weight, "tq,qd->td"))
    unit_two, factor_two, sent_two = norm_forward(middle, norm_after)
    full_two = gather_rows(sent_two)
    gate_part = product(full_two, gate_weight, "td,df->tf")
    up_part = product(full_two, up_weight, "td,df->tf")
    gate, upper = (
        lax.psum_scatter(gate_part, "col", scatter_dimension=1, tiled=True),
        lax.psum_scatter(up_part, "col", scatter_dimension=1, tiled=True),
    )
    activ = jax.nn.silu(gate)
    mixed_full = gather_share((activ * upper).astype(jnp.bfloat16))
    layer_out = (middle + reduce_rows(product(mixed_full, down_weight, "tf,fd->td"))).astype(
        jnp.bfloat16
    )
    grad_out = cotangent.astype(jnp.float32)
    grad_full = gather_rows(cotangent)
    down_local = product(mixed_full, grad_full, "tf,td->fd")
    dmixed = reduce_share(product(grad_full, down_weight, "td,fd->tf"))
    sigma = jax.nn.sigmoid(gate)
    dgate = (dmixed * upper * sigma * (1.0 + gate * (1.0 - sigma))).astype(jnp.bfloat16)
    dupper = (dmixed * activ).astype(jnp.bfloat16)
    dgate_full, dupper_full = (
        lax.all_gather(dgate, "col", axis=1, tiled=True),
        lax.all_gather(dupper, "col", axis=1, tiled=True),
    )
    gate_local = product(full_two, dgate_full, "td,tf->df")
    up_local = product(full_two, dupper_full, "td,tf->df")
    dsecond = reduce_rows(
        product(dgate_full, gate_weight, "tf,df->td") + product(dupper_full, up_weight, "tf,df->td")
    )
    dmid_norm, after_part = norm_backward(dsecond, unit_two, factor_two, norm_after)
    dmiddle = grad_out + dmid_norm
    dmid_full = gather_rows(dmiddle.astype(jnp.bfloat16))
    output_local = product(att_full, dmid_full, "tq,td->qd")
    datt = reduce_share(product(dmid_full, output_weight, "td,qd->tq"))
    datt_heads = datt.astype(jnp.bfloat16).reshape(
        seqs, SEQUENCE_LENGTH, kv_heads, head_group, HEAD_SIZE
    )
    dquery, dkey, dvalue = lax.map(attend_back, (query, key, value_tensor, logsum, datt_heads))
    dq_gained = unrotate(dquery.reshape(seqs, SEQUENCE_LENGTH, q_heads, HEAD_SIZE), cosine, sine)
    dk_gained = unrotate(dkey, cosine, sine)
    dq_raw, qgain_part = head_norm_back(dq_gained, q_unit, q_factor, query_gain)
    dk_raw, kgain_part = head_norm_back(dk_gained, k_unit, k_factor, key_gain)
    dq_full, dk_full, dv_full = (
        lax.all_gather(
            dq_raw.reshape(tokens, q_heads * HEAD_SIZE).astype(jnp.bfloat16),
            "col",
            axis=1,
            tiled=True,
        ),
        lax.all_gather(
            dk_raw.reshape(tokens, kv_heads * HEAD_SIZE).astype(jnp.bfloat16),
            "col",
            axis=1,
            tiled=True,
        ),
        lax.all_gather(
            dvalue.reshape(tokens, kv_heads * HEAD_SIZE).astype(jnp.bfloat16),
            "col",
            axis=1,
            tiled=True,
        ),
    )
    query_local = product(full_one, dq_full, "td,tq->dq")
    key_local = product(full_one, dk_full, "td,tq->dq")
    value_local = product(full_one, dv_full, "td,tq->dq")
    dfirst = reduce_rows(
        product(dq_full, query_weight, "tq,dq->td")
        + product(dk_full, key_matrix, "tq,dq->td")
        + product(dv_full, value_matrix, "tq,dq->td")
    )
    dres_norm, before_part = norm_backward(dfirst, unit_one, factor_one, norm_before)
    hidden_grad = dmiddle + dres_norm
    width = norm_before.shape[0]
    offset = lax.axis_index("col") * width
    before_wide = lax.dynamic_update_slice_in_dim(
        jnp.zeros((MODEL_WIDTH,), jnp.float32), before_part, offset, 0
    )
    after_wide = lax.dynamic_update_slice_in_dim(
        jnp.zeros((MODEL_WIDTH,), jnp.float32), after_part, offset, 0
    )
    summed = (
        lax.psum(query_local.astype(jnp.bfloat16), "dp").astype(jnp.float32),
        lax.psum(key_local.astype(jnp.bfloat16), "dp").astype(jnp.float32),
        lax.psum(value_local.astype(jnp.bfloat16), "dp").astype(jnp.float32),
        lax.psum(output_local.astype(jnp.bfloat16), "dp").astype(jnp.float32),
        lax.psum(gate_local.astype(jnp.bfloat16), "dp").astype(jnp.float32),
        lax.psum(up_local.astype(jnp.bfloat16), "dp").astype(jnp.float32),
        lax.psum(down_local.astype(jnp.bfloat16), "dp").astype(jnp.float32),
    )
    gains = every_gains(before_wide, after_wide, qgain_part, kgain_part)
    weights = (summed[0], summed[1], summed[2], summed[3], summed[4], summed[5], summed[6])
    before_grad = lax.dynamic_slice_in_dim(gains[0], offset, width, 0)
    after_grad = lax.dynamic_slice_in_dim(gains[1], offset, width, 0)
    return (
        layer_out,
        hidden_grad,
        before_grad,
        weights[0],
        weights[1],
        weights[2],
        gains[2],
        gains[3],
        weights[3],
        after_grad,
        weights[4],
        weights[5],
        weights[6],
    )


def solution(mesh):
    placed = (
        P(("dp", "row"), "col"),
        P("col"),
        P("col", "row"),
        P("col", "row"),
        P("col", "row"),
        P(),
        P(),
        P("row", "col"),
        P("col"),
        P("col", "row"),
        P("col", "row"),
        P("row", "col"),
        P(("dp", "row"), "col"),
    )
    return jax.shard_map(
        on_device,
        mesh=mesh,
        in_specs=placed,
        out_specs=(
            P(("dp", "row"), "col"),
            P(("dp", "row"), "col"),
            P("col"),
            P("col", "row"),
            P("col", "row"),
            P("col", "row"),
            P(),
            P(),
            P("row", "col"),
            P("col"),
            P("col", "row"),
            P("col", "row"),
            P("row", "col"),
        ),
        check_vma=False,
    )
```

profile of v0, /device:TPU:0, one launch (start us, length us, event | category | flops | bytes accessed | tf_op | source)
XLA Modules:
  0.0 1031.0 jit_solution(5193941451720121744)
XLA Ops:
  8.6 2.6 psum.105
  13.9 48.3 %all-gather.11.cloned.1.call-done = bf16[1024,1024]{1,0:T(8,128)(2,1)} async-done(((bf16[256,1024]{1,0:T(8,128)(2,1)}), bf16[1024,1024]{1,0:T(8,128)(2,1)}) %all-gather.11.cloned.1.call-update) | async-done | bytes 2097168 | tf_op jit(solution)/shard_map/all_gather | solution.py:24
  62.2 3.4 fusion.67
  65.7 4.4 fusion.68
  71.5 3.2 fusion.60
  90.0 2.7 reshape.472
  92.7 3.2 multiply_reduce_fusion.5
  108.3 3.5 fusion.40
  113.9 3.3 copy-done.2
  118.3 6.1 fusion.17
  124.4 8.1 all-gather.13.cloned.1.call-done
  132.5 4.8 fusion.69
  138.2 77.3 %reduce-scatter.18.cloned.1.call-done = f32[256,1024]{1,0:T(8,128)} async-done(((f32[1024,1024]{1,0:T(8,128)}), f32[256,1024]{1,0:T(8,128)}) %reduce-scatter.18.cloned.1.call-update) | async-done | bytes 1048592 | tf_op jit(solution)/shard_map/reduce_scatter | solution.py:28
  223.1 40.1 %all-gather.19.cloned.1.call-done = bf16[1024,1024]{1,0:T(8,128)(2,1)} async-done(((bf16[256,1024]{1,0:T(8,128)(2,1)}), bf16[1024,1024]{1,0:T(8,128)(2,1)}) %all-gather.19.cloned.1.call-update) | async-done | bytes 2097168 | tf_op jit(solution)/shard_map/all_gather | solution.py:24
  263.3 8.7 fusion.73
  272.0 37.9 %all-gather.15.cloned.1.call-done = bf16[1024,1024]{1,0:T(8,128)(2,1)} async-done(((bf16[256,1024]{1,0:T(8,128)(2,1)}), bf16[1024,1024]{1,0:T(8,128)(2,1)}) %all-gather.15.cloned.1.call-update) | async-done | bytes 2097168 | tf_op jit(solution)/shard_map/all_gather | solution.py:24
  309.9 6.9 fusion.70
  316.8 9.5 fusion.71
  326.4 17.0 %reduce-scatter.20.cloned.1.call-done = f32[1024,768]{1,0:T(8,128)} async-done(((f32[1024,1536]{1,0:T(8,128)}), f32[1024,768]{1,0:T(8,128)}) %reduce-scatter.20.cloned.1.call-update) | async-done | bytes 3145744 | tf_op jit(solution)/shard_map/reduce_scatter | solution.py:182
  343.3 18.0 %reduce-scatter.22.cloned.1.call-done = f32[1024,768]{1,0:T(8,128)} async-done(((f32[1024,1536]{1,0:T(8,128)}), f32[1024,768]{1,0:T(8,128)}) %reduce-scatter.22.cloned.1.call-update) | async-done | bytes 3145744 | tf_op jit(solution)/shard_map/reduce_scatter | solution.py:183
  361.4 6.1 multiply_convert_fusion
  368.3 12.8 %all-gather.21.cloned.1.call-done = bf16[1024,1536]{1,0:T(8,128)(2,1)} async-done(((bf16[1024,768]{1,0:T(8,128)(2,1)}), bf16[1024,1536]{1,0:T(8,128)(2,1)}) %all-gather.21.cloned.1.call-update) | async-done | bytes 3145744 | tf_op jit(solution)/shard_map/all_gather | solution.py:198
  381.0 6.9 fusion.74
  387.9 8.6 all-gather.23.cloned.1.call-done
  396.5 9.5 convolution_add_fusion
  406.1 78.1 %reduce-scatter.28.cloned.1.call-done = f32[256,1024]{1,0:T(8,128)} async-done(((f32[1024,1024]{1,0:T(8,128)}), f32[256,1024]{1,0:T(8,128)}) %reduce-scatter.28.cloned.1.call-update) | async-done | bytes 1048592 | tf_op jit(solution)/shard_map/reduce_scatter | solution.py:28
  490.8 46.1 %all-gather.25.cloned.1.call-done = bf16[1024,1024]{1,0:T(8,128)(2,1)} async-done(((bf16[256,1024]{1,0:T(8,128)(2,1)}), bf16[1024,1024]{1,0:T(8,128)(2,1)}) %all-gather.25.cloned.1.call-update) | async-done | bytes 2097168 | tf_op jit(solution)/shard_map/all_gather | solution.py:24
  536.9 4.2 fusion.75
  541.2 8.5 reduce-scatter.30.cloned.1.call-done
  551.2 5.3 fusion
  568.8 3.7 fusion.38
  575.3 4.3 maximum_multiply_fusion.2
  587.0 2.8 fusion.76
  589.7 2.8 fusion.47
  592.5 8.2 add_add_fusion
  600.8 8.4 fusion.72
  609.5 7.8 convolution_convert_fusion.1
  617.3 4.9 convolution_convert_fusion.2
  622.3 4.9 convolution_convert_fusion
  635.2 43.7 %reduce-scatter.32.cloned.1.call-done = f32[256,1024]{1,0:T(8,128)} async-done(((f32[1024,1024]{1,0:T(8,128)}), f32[256,1024]{1,0:T(8,128)}) %reduce-scatter.32.cloned.1.call-update) | async-done | bytes 1048592 | tf_op jit(solution)/shard_map/reduce_scatter | solution.py:28
  680.9 43.7 %all-reduce = (f32[2048]{0:T(1024)S(1)}, f32[128]{0:T(128)}, f32[128]{0:T(128)}, f32[2048]{0:T(1024)S(1)}) all-reduce(f32[2048]{0:T(1024)S(1)} %dynamic_update_slice.19, f32[128]{0:T(128)S(1)} %get-tuple-element.49, f32[128]{0:T(128)S(1)} %get-tuple-element.64, ...), channel_id=1, replica_groups=mesh['dp'=4,'row'=4,'col'=2] {'dp','row','col'}, use_global_device_ids=true, to_apply=%region_27.28 | all-reduce | flops 4352 | bytes 34816 | tf_op jit(solution)/shard_map/psum | solution.py:40
  725.8 2.7 psum.108
  728.5 31.5 %reduce-scatter.24.cloned.1.call-done = f32[256,1024]{1,0:T(8,128)} async-done(((f32[1024,1024]{1,0:T(8,128)}), f32[256,1024]{1,0:T(8,128)}) %reduce-scatter.24.cloned.1.call-update) | async-done | bytes 1048592 | tf_op jit(solution)/shard_map/reduce_scatter | solution.py:28
  760.0 3.2 fusion.33
  763.2 242.7 %all-reduce.4.cloned.1.call-done = (bf16[1024,512]{1,0:T(8,128)(2,1)}, bf16[1024,256]{1,0:T(8,128)(2,1)}, bf16[1024,256]{1,0:T(8,128)(2,1)}, bf16[512,1024]{1,0:...) async-done(((bf16[1024,512]{1,0:T(8,128)(2,1)}, bf16[1024,256]{1,0:T(8,128)(2,1)}, bf16[1024,256]{1,0:T(8,128)(2,1)}, ...) | async-done | bytes 12582928 | tf_op jit(solution)/shard_map/psum | solution.py:258
  1005.9 5.6 convert_element_type.171
  1011.5 3.6 convert_element_type.173
  1015.1 3.5 convert_element_type.175
  (228 shorter events, 93.0 us)
Async XLA Ops:
  7.2 302.7 %copy-start = (bf16[1024,1536]{1,0:T(8,128)(2,1)S(1)}, bf16[1024,1536]{1,0:T(8,128)(2,1)}, u32[]{:S(2)}) copy-start(bf16[1024,1536]{1,0:T(8,128)(2,1)} %param.22) | copy-start | bytes 9437188
  7.2 55.0 %all-gather.11.cloned.1.call-start = ((), (), s32[]{:S(2)}) async-start(), calls=%async_computation.11 | async-start | bytes 2621440 | tf_op jit(solution)/shard_map/all_gather | solution.py:24
  13.9 62.8 %reduce-scatter.14.cloned.1.call-start = ((), (), s32[]{:S(2)}) async-start(), calls=%async_computation.13 | async-start | bytes 1572864 | tf_op jit(solution)/shard_map/reduce_scatter | solution.py:152
  65.6 24.4 %reduce-scatter.16.cloned.1.call-start = ((), (), s32[]{:S(2)}) async-start(), calls=%async_computation.14 | async-start | bytes 3145728 | tf_op jit(solution)/shard_map/reduce_scatter | solution.py:151
  70.1 48.1 %reduce-scatter.12.cloned.1.call-start = ((), (), s32[]{:S(2)}) async-start(), calls=%async_computation.12 | async-start | bytes 1572864 | tf_op jit(solution)/shard_map/reduce_scatter | solution.py:153
  70.2 4.5 copy-start.32
  76.4 56.1 %all-gather.13.cloned.1.call-start = ((), (), s32[]{:S(2)}) async-start(), calls=%async_computation.15 | async-start | bytes 1572864 | tf_op jit(solution)/shard_map/all_gather | solution.py:32
  124.4 91.1 %reduce-scatter.18.cloned.1.call-start = ((), (), s32[]{:S(2)}) async-start(), calls=%async_computation.16 | async-start | bytes 5242880 | tf_op jit(solution)/shard_map/reduce_scatter | solution.py:28
  137.3 83.1 %copy-start.37 = (f32[1024]{0:T(1024)S(1)}, f32[1024]{0:T(1024)}, u32[]{:S(2)}) copy-start(f32[1024]{0:T(1024)} %param.21) | copy-start | bytes 12292
  137.4 125.9 %all-gather.19.cloned.1.call-start = ((), (), s32[]{:S(2)}) async-start(), calls=%async_computation.22 | async-start | bytes 2621440 | tf_op jit(solution)/shard_map/all_gather | solution.py:24
  138.1 171.8 %all-gather.15.cloned.1.call-start = ((), (), s32[]{:S(2)}) async-start(), calls=%async_computation.17 | async-start | bytes 2621440 | tf_op jit(solution)/shard_map/all_gather | solution.py:24
  222.7 103.7 %reduce-scatter.26.cloned.1.call-start = ((), (), s32[]{:S(2)}) async-start(), calls=%async_computation.23 | async-start | bytes 9437184 | tf_op jit(solution)/shard_map/reduce_scatter | solution.py:36
  272.0 71.4 %reduce-scatter.20.cloned.1.call-start = ((), (), s32[]{:S(2)}) async-start(), calls=%async_computation.18 | async-start | bytes 9437184 | tf_op jit(solution)/shard_map/reduce_scatter | solution.py:182
  316.8 44.6 %reduce-scatter.22.cloned.1.call-start = ((), (), s32[]{:S(2)}) async-start(), calls=%async_computation.19 | async-start | bytes 9437184 | tf_op jit(solution)/shard_map/reduce_scatter | solution.py:183
  326.3 54.7 %all-gather.21.cloned.1.call-start = ((), (), s32[]{:S(2)}) async-start(), calls=%async_computation.24 | async-start | bytes 4718592 | tf_op jit(solution)/shard_map/all_gather | solution.py:198
  367.5 29.0 %all-gather.23.cloned.1.call-start = ((), (), s32[]{:S(2)}) async-start(), calls=%async_computation.25 | async-start | bytes 4718592 | tf_op jit(solution)/shard_map/all_gather | solution.py:199
  368.2 115.9 %reduce-scatter.28.cloned.1.call-start = ((), (), s32[]{:S(2)}) async-start(), calls=%async_computation.26 | async-start | bytes 5242880 | tf_op jit(solution)/shard_map/reduce_scatter | solution.py:28
  406.0 78.2 %copy-start.4 = (f32[256,1024]{1,0:T(8,128)S(1)}, f32[256,1024]{1,0:T(8,128)}, u32[]{:S(2)}) copy-start(f32[256,1024]{1,0:T(8,128)} %get-tuple-element.79) | copy-start | bytes 3145732
  406.0 82.2 %copy-start.14 = (bf16[256,1024]{1,0:T(8,128)(2,1)S(1)}, bf16[256,1024]{1,0:T(8,128)(2,1)}, u32[]{:S(2)}) copy-start(bf16[256,1024]{1,0:T(8,128)(2,1)} %param.25) | copy-start | bytes 1572868
  406.0 130.9 %copy-start.30 = (bf16[512,1024]{1,0:T(8,128)(2,1)S(1)}, bf16[512,1024]{1,0:T(8,128)(2,1)}, u32[]{:S(2)}) copy-start(bf16[512,1024]{1,0:T(8,128)(2,1)} %param.20) | copy-start | bytes 3145732
  406.0 130.9 %all-gather.25.cloned.1.call-start = ((), (), s32[]{:S(2)}) async-start(), calls=%async_computation.27 | async-start | bytes 2621440 | tf_op jit(solution)/shard_map/all_gather | solution.py:24
  490.6 59.1 %reduce-scatter.30.cloned.1.call-start = ((), (), s32[]{:S(2)}) async-start(), calls=%async_computation.28 | async-start | bytes 3145728 | tf_op jit(solution)/shard_map/reduce_scatter | solution.py:36
  541.1 10.1 copy-start.34
  541.1 51.4 %all-gather.27.cloned.1.call-start = ((), (), s32[]{:S(2)}) async-start(), calls=%async_computation.29 | async-start | bytes 1572864 | tf_op jit(solution)/shard_map/all_gather | solution.py:220
  551.2 5.4 copy-start.18
  551.2 5.4 slice-start
  551.2 6.0 slice-start.1
  572.5 28.2 %all-gather.17.cloned.1.call-start = ((), (), s32[]{:S(2)}) async-start(), calls=%async_computation.20 | async-start | bytes 4718592 | tf_op jit(solution)/shard_map/all_gather | solution.py:32
  575.2 103.7 %reduce-scatter.32.cloned.1.call-start = ((), (), s32[]{:S(2)}) async-start(), calls=%async_computation.30 | async-start | bytes 5242880 | tf_op jit(solution)/shard_map/reduce_scatter | solution.py:28
  575.2 7.8 slice-start.2
  575.3 4.5 copy-start.8
  575.3 4.5 copy-start.17
  575.3 7.8 slice-start.3
  584.6 5.1 copy-start.33
  600.7 159.3 %reduce-scatter.24.cloned.1.call-start = ((), (), s32[]{:S(2)}) async-start(), calls=%async_computation.21 | async-start | bytes 5242880 | tf_op jit(solution)/shard_map/reduce_scatter | solution.py:28
  609.2 396.7 %all-reduce.4.cloned.1.call-start = ((), (), s32[]{:S(2)}) async-start(), calls=%async_computation.31 | async-start | bytes 25165824 | tf_op jit(solution)/shard_map/psum | solution.py:258
  609.5 7.8 copy-start.43
  609.5 7.8 copy-start.48
  617.3 5.0 copy-start.44
  617.3 4.9 copy-start.47
  622.3 4.9 copy-start.24
  622.3 4.9 copy-start.49
  634.8 44.1 %copy-start.5 = (bf16[256,1024]{1,0:T(8,128)(2,1)S(1)}, bf16[256,1024]{1,0:T(8,128)(2,1)}, u32[]{:S(2)}) copy-start(bf16[256,1024]{1,0:T(8,128)(2,1)} %param.13) | copy-start | bytes 1572868
  634.8 44.1 %copy-start.38 = (f32[1024]{0:T(1024)S(1)}, f32[1024]{0:T(1024)}, u32[]{:S(2)}) copy-start(f32[1024]{0:T(1024)} %param.14) | copy-start | bytes 12292
  634.8 44.1 %copy-start.40 = (f32[256]{0:T(256)S(1)}, f32[256]{0:T(256)}, u32[]{:S(2)}) copy-start(f32[256]{0:T(256)} %copy-done.39) | copy-start | bytes 3076
  634.8 125.2 %copy-start.10 = (f32[256,1024]{1,0:T(8,128)S(1)}, f32[256,1024]{1,0:T(8,128)}, u32[]{:S(2)}) copy-start(f32[256,1024]{1,0:T(8,128)} %reduce-scatter.28.cloned.1.call-done) | copy-start | bytes 3145732
  634.8 125.2 %copy-start.15 = (bf16[256,1024]{1,0:T(8,128)(2,1)S(1)}, bf16[256,1024]{1,0:T(8,128)(2,1)}, u32[]{:S(2)}) copy-start(bf16[256,1024]{1,0:T(8,128)(2,1)} %param.25) | copy-start | bytes 1572868
  1005.9 5.6 copy-start.21
  (27 other events, 73.7 us)
Sparse Core Ops, SparseCore 0:
  14.0 48.2 all-gather.10
  65.7 7.1 reduce-scatter.13
  75.8 10.7 reduce-scatter.15
  89.2 9.6 reduce-scatter.11
  124.5 7.9 all-gather.12
  137.5 77.9 reduce-scatter.17
  217.1 46.1 all-gather.18
  265.4 44.4 all-gather.14
  312.8 12.6 reduce-scatter.25
  328.2 15.1 reduce-scatter.19
  346.2 15.1 reduce-scatter.21
  367.6 13.3 all-gather.20
  383.1 13.2 all-gather.22
  406.1 77.9 reduce-scatter.27
  490.7 46.1 all-gather.24
  541.2 8.4 reduce-scatter.29
  572.6 10.0 all-gather.26
  584.7 13.3 all-gather.16
  600.9 77.9 reduce-scatter.31
  681.6 78.3 reduce-scatter.23
  765.9 240.0 all-reduce.3
where the time goes:
time: 1040 us; the launch traced here: 1030 us
  waiting for transfers between devices  720 us (69%)
  matrix products  127 us (12%)
  other arithmetic  69.6 us (7%)
  blocking collectives  58.5 us (6%)
  local copies, waits for them, and re-layouts  38.1 us (4%)
  between operations  15.2 us (1%)
    psum x1, waiting for transfers between devices, on_device(): lax.psum(query_local.astype(jnp.bfloat16), 'dp').astype(jnp.float32)  243 us
    reduce_scatter x4, waiting for transfers between devices, reduce_rows(): return lax.psum_scatter(value_rows, 'row', scatter_dimension=0, tiled=True)  231 us
    all_gather x4, waiting for transfers between devices, gather_rows(): return lax.all_gather(value_rows, 'row', axis=0, tiled=True)  172 us
    dot_general x21, matrix products, product(): return jnp.einsum(form, left, right, preferred_element_type=jnp.float32)  107 us
    psum x1, blocking collectives, every_gains(): return lax.psum((leading_part, second, third, fourth), ('dp', 'row', 'col'))  43.7 us
  transfers between devices with their start and end apart: 21, of which 15 were waited for; matrix products, arithmetic and copies ran while one was open for 14% of the time, Pallas kernels for 0%

commit v1 on v0

v1 whole, which is shorter than its diff:
```python
import functools
import math

import jax
import jax.numpy as jnp
from jax import lax
from jax.experimental import pallas as pl
from jax.experimental.pallas import tpu as pltpu
from jax.sharding import PartitionSpec as P

MODEL_WIDTH = 2048
HEAD_SIZE = 128
SEQUENCE_LENGTH = 1024
EPS = 1e-06
THETA = 1000000.0
ROWS = 4
BLOCK = SEQUENCE_LENGTH // ROWS
SCALE = 1.0 / math.sqrt(HEAD_SIZE)
LOG2 = SCALE * math.log2(math.e)

F32 = jnp.float32
BF16 = jnp.bfloat16


def swap(x):
    return lax.ppermute(x, "col", [(0, 1), (1, 0)])


def row_swap(x, mask):
    return lax.ppermute(x, "row", [(i, i ^ mask) for i in range(ROWS)])


def gather_slots(x):
    two = row_swap(x, 2)
    one = row_swap(x, 1)
    three = row_swap(two, 1)
    return [x, one, two, three]


def scatter_slots(own, one, two, three):
    got_three = row_swap(three.astype(BF16), 1)
    got_one = row_swap(one.astype(BF16), 1)
    got_two = row_swap((two + got_three.astype(F32)).astype(BF16), 2)
    return own + got_one.astype(F32) + got_two.astype(F32)


def dp_swap(x, mask, dp):
    return lax.ppermute(x, "dp", [(i, i ^ mask) for i in range(dp)])


def halving(part, bits, me, dp):
    first, second = bits
    v1, v2 = (me // first) % 2, (me // second) % 2
    half = part.shape[0] // 2
    kept = lax.dynamic_slice_in_dim(part, v1 * half, half, 0)
    sent = lax.dynamic_slice_in_dim(part, (1 - v1) * half, half, 0)
    total = (kept.astype(F32) + dp_swap(sent, first, dp).astype(F32)).astype(BF16)
    quarter = half // 2
    kept = lax.dynamic_slice_in_dim(total, v2 * quarter, quarter, 0)
    sent = lax.dynamic_slice_in_dim(total, (1 - v2) * quarter, quarter, 0)
    mine = (kept.astype(F32) + dp_swap(sent, second, dp).astype(F32)).astype(BF16)
    near = dp_swap(mine, second, dp)
    far = dp_swap(mine, first, dp)
    cross = dp_swap(near, first, dp)
    return [mine, near, far, cross]


def piece_rows(bits, me):
    first, second = bits
    rows = []
    for mask in (0, second, first, first + second):
        who = me ^ mask
        rows.append(((who // first) % 2) * 2 + (who // second) % 2)
    return rows


def assemble_kernel(spans, table_ref, *refs):
    pieces, outs = refs[:8], refs[8:]
    half, slot = pl.program_id(0), pl.program_id(1)
    for h in range(2):
        for s in range(4):

            @pl.when((half == h) & (slot == s))
            def _(piece=pieces[h * 4 + s]):
                for (lo, hi), out in zip(spans, outs):
                    out[...] = piece[:, lo:hi].astype(F32)


def assemble(pieces_a, pieces_b, me, core, widths, split):
    rows, columns = pieces_a[0].shape
    spans, at = [], 0
    for width in widths:
        spans.append((at, at + width))
        at += width
    block_rows, block_cols = [], []
    for half, bits in ((core, (1, 2)), (1 - core, (2, 1))):
        ids = piece_rows(bits, me)
        block_rows += [half * 4 + r if split == 0 else r for r in ids]
        block_cols.append(half if split == 1 else 0 * half)
    table = jnp.stack(block_rows + block_cols).astype(jnp.int32)
    full = [
        (rows * (8 if split == 0 else 4), width * (2 if split == 1 else 1)) for width in widths
    ]
    return pl.pallas_call(
        functools.partial(assemble_kernel, spans),
        out_shape=[jax.ShapeDtypeStruct(shape, F32) for shape in full],
        grid_spec=pltpu.PrefetchScalarGridSpec(
            num_scalar_prefetch=1,
            grid=(2, 4),
            in_specs=[pl.BlockSpec((rows, columns), lambda h, s, t: (0, 0))] * 8,
            out_specs=[
                pl.BlockSpec((rows, width), lambda h, s, t: (t[h * 4 + s], t[8 + h]))
                for width in widths
            ],
        ),
        cost_estimate=pl.CostEstimate(
            flops=0, transcendentals=0, bytes_accessed=8 * rows * columns * 6
        ),
    )(table, *pieces_a, *pieces_b)


def reduce_grads(part_a, part_b, me, core, dp, widths, split):
    if dp == 4:
        pieces_a = halving(part_a, (1, 2), me, dp)
        pieces_b = halving(part_b, (2, 1), me, dp)
        return assemble(pieces_a, pieces_b, me, core, widths, split)
    total_a, total_b = lax.psum(part_a, "dp"), lax.psum(part_b, "dp")
    outs, at = [], 0
    for width in widths:
        a, b = total_a[:, at : at + width], total_b[:, at : at + width]
        axis = split
        nat = jnp.where(core == 0, jnp.concatenate([a, b], axis), jnp.concatenate([b, a], axis))
        outs.append(nat.astype(F32))
        at += width
    return outs


def rope_tables():
    half = HEAD_SIZE // 2
    freq = THETA ** (-(jnp.arange(half, dtype=F32) * 2.0) / HEAD_SIZE)
    angle = jnp.arange(SEQUENCE_LENGTH, dtype=F32)[:, None] * freq[None, :]
    cosine = jnp.cos(angle)
    sine = jnp.sin(angle)
    return (jnp.concatenate([cosine, cosine], 1), jnp.concatenate([-sine, sine], 1))


def dot(a, b, dims):
    return lax.dot_general(a, b, (dims, ((), ())), preferred_element_type=F32)


NN = ((1,), (0,))
NT = ((1,), (1,))
TN = ((0,), (0,))


def unit_rows(x):
    factor = lax.rsqrt(jnp.mean(x * x, axis=1, keepdims=True) + EPS)
    return x * factor, factor


def raw_scores(query, key, block):
    scores = dot(query, key, NT)
    row = lax.broadcasted_iota(jnp.int32, scores.shape, 0) + block * BLOCK
    column = lax.broadcasted_iota(jnp.int32, scores.shape, 1)
    return jnp.where(row >= column, scores, -1e30)


def attend_kernel(groups, table, *refs):
    raws = refs[:ROWS]
    cosine, sine, q_gain, k_gain = refs[ROWS : ROWS + 4]
    att, lse, query, key, value = refs[ROWS + 4 :]
    width = HEAD_SIZE
    for s in range(ROWS):
        rows = pl.ds(pl.multiple_of(table[s] * BLOCK, BLOCK), BLOCK)
        cos, sin = cosine[rows, :], sine[rows, :]
        for h in range(groups + 1):
            unit, _ = unit_rows(raws[s][:, h * width : (h + 1) * width])
            gained = unit * (q_gain[...] if h < groups else k_gain[...])
            turned = gained * cos + pltpu.roll(gained, width // 2, 1) * sin
            if h < groups:
                query[rows, h * width : (h + 1) * width] = turned.astype(BF16)
            else:
                key[rows, :] = turned.astype(BF16)
        value[rows, :] = raws[s][:, (groups + 1) * width :].astype(BF16)
    for i in range(ROWS):
        span = (i + 1) * BLOCK
        slot = table[ROWS + i]
        rows = pl.ds(pl.multiple_of(slot * BLOCK, BLOCK), BLOCK)
        for h in range(groups):
            cols = slice(h * width, (h + 1) * width)
            scores = raw_scores(query[i * BLOCK : span, cols], key[:span, :], i)
            top = jnp.max(scores, axis=1, keepdims=True)
            expo = jnp.exp2((scores - top) * LOG2)
            total = jnp.sum(expo, axis=1, keepdims=True)
            prob = (expo * (1.0 / total)).astype(BF16)
            att[rows, cols] = dot(prob, value[:span, :], NN).astype(BF16)
            log = top * LOG2 + jnp.log2(total)
            lse[i * BLOCK : span, cols] = jnp.broadcast_to(log, (BLOCK, width))


def attend_back_kernel(groups, table, *refs):
    raws = refs[:ROWS]
    grads = refs[ROWS : 2 * ROWS]
    cosine, sine, q_gain, k_gain, query, key, value, lse = refs[2 * ROWS : 2 * ROWS + 8]
    out, gains, d_query, d_key, d_value, grad = refs[2 * ROWS + 8 :]
    width = HEAD_SIZE
    for s in range(ROWS):
        rows = pl.ds(pl.multiple_of(table[s] * BLOCK, BLOCK), BLOCK)
        grad[rows, :] = grads[s][...]
    d_key[...] = jnp.zeros_like(d_key)
    d_value[...] = jnp.zeros_like(d_value)
    for i in range(ROWS):
        span = (i + 1) * BLOCK
        for h in range(groups):
            cols = slice(h * width, (h + 1) * width)
            q = query[i * BLOCK : span, cols]
            g = grad[i * BLOCK : span, cols]
            scores = raw_scores(q, key[:span, :], i)
            log = lse[i * BLOCK : span, h * width : h * width + 1]
            prob = jnp.exp2(scores * LOG2 - log)
            dprob = dot(g, value[:span, :], NT)
            delta = jnp.sum(prob * dprob, axis=1, keepdims=True)
            dscore = (SCALE * prob * (dprob - delta)).astype(BF16)
            d_query[i * BLOCK : span, cols] = dot(dscore, key[:span, :], NN)
            d_key[:span, :] += dot(dscore, q, TN)
            d_value[:span, :] += dot(prob.astype(BF16), g, TN)
    gain_sums = [jnp.zeros((1, width), F32), jnp.zeros((1, width), F32)]
    for s in range(ROWS):
        rows = pl.ds(pl.multiple_of(table[s] * BLOCK, BLOCK), BLOCK)
        cos, sin = cosine[rows, :], sine[rows, :]
        for h in range(groups + 1):
            cols = slice(h * width, (h + 1) * width)
            unit, factor = unit_rows(raws[s][:, cols])
            turned = d_query[rows, cols] if h < groups else d_key[rows, :]
            back = turned * cos + pltpu.roll(turned * sin, width // 2, 1)
            scaled = back * (q_gain[...] if h < groups else k_gain[...])
            inner = jnp.mean(scaled * unit, axis=1, keepdims=True)
            which = 0 if h < groups else 1
            gain_sums[which] += jnp.sum(back * unit, axis=0, keepdims=True)
            out[s * BLOCK : (s + 1) * BLOCK, cols] = (factor * (scaled - unit * inner)).astype(BF16)
        out[s * BLOCK : (s + 1) * BLOCK, (groups + 1) * width :] = d_value[rows, :].astype(BF16)
    gains[0:1, :] = gain_sums[0]
    gains[1:2, :] = gain_sums[1]


SMEM = pl.BlockSpec(memory_space=pltpu.SMEM)
VMEM = pl.BlockSpec(memory_space=pltpu.VMEM)


def attention_cost(groups, products):
    area = groups * SEQUENCE_LENGTH * SEQUENCE_LENGTH * 5 // 8
    return pl.CostEstimate(
        flops=2 * products * area * HEAD_SIZE + 30 * area,
        transcendentals=area,
        bytes_accessed=SEQUENCE_LENGTH * HEAD_SIZE * 4 * (groups + 2) * 3,
    )


def attend(table, raws, cosine, sine, q_gain, k_gain, groups):
    wide = (SEQUENCE_LENGTH, groups * HEAD_SIZE)
    one = (SEQUENCE_LENGTH, HEAD_SIZE)
    return pl.pallas_call(
        functools.partial(attend_kernel, groups),
        out_shape=[
            jax.ShapeDtypeStruct(wide, BF16),
            jax.ShapeDtypeStruct(wide, F32),
            jax.ShapeDtypeStruct(wide, BF16),
            jax.ShapeDtypeStruct(one, BF16),
            jax.ShapeDtypeStruct(one, BF16),
        ],
        in_specs=[SMEM] + [VMEM] * (ROWS + 4),
        out_specs=[VMEM] * 5,
        cost_estimate=attention_cost(groups, 2),
    )(table, *raws, cosine, sine, q_gain[None], k_gain[None])


def attend_back(table, raws, grads, cosine, sine, q_gain, k_gain, saved, groups):
    query, key, value, lse = saved
    return pl.pallas_call(
        functools.partial(attend_back_kernel, groups),
        out_shape=[
            jax.ShapeDtypeStruct((SEQUENCE_LENGTH, (groups + 2) * HEAD_SIZE), BF16),
            jax.ShapeDtypeStruct((2, HEAD_SIZE), F32),
        ],
        in_specs=[SMEM] + [VMEM] * (2 * ROWS + 8),
        out_specs=[VMEM] * 2,
        scratch_shapes=[
            pltpu.VMEM((SEQUENCE_LENGTH, groups * HEAD_SIZE), F32),
            pltpu.VMEM((SEQUENCE_LENGTH, HEAD_SIZE), F32),
            pltpu.VMEM((SEQUENCE_LENGTH, HEAD_SIZE), F32),
            pltpu.VMEM((SEQUENCE_LENGTH, groups * HEAD_SIZE), BF16),
        ],
        cost_estimate=attention_cost(groups, 5),
    )(table, *raws, *grads, cosine, sine, q_gain[None], k_gain[None], query, key, value, lse)


def own_other(weight, core, axis):
    half = weight.shape[axis] // 2
    return (
        lax.dynamic_slice_in_dim(weight, core * half, half, axis),
        lax.dynamic_slice_in_dim(weight, (1 - core) * half, half, axis),
    )


def norm_stats(x):
    part = jnp.sum(x * x, axis=1)
    factor = lax.rsqrt((part + swap(part)) / MODEL_WIDTH + EPS)
    return x * factor[:, None], factor


def norm_backward(grad, unit, factor, gain):
    scaled = grad * gain
    part = jnp.sum(scaled * unit, axis=1)
    inner = (part + swap(part)) / MODEL_WIDTH
    return (factor[:, None] * (scaled - unit * inner[:, None]), jnp.sum(grad * unit, axis=0))


def cat(items, axis):
    return jnp.concatenate(items, axis)


def after(x, *others):
    return lax.optimization_barrier((x, *others))[0]


def on_device(
    hidden,
    norm_before,
    query_weight,
    key_matrix,
    value_matrix,
    query_gain,
    key_gain,
    output_weight,
    norm_after,
    gate_weight,
    up_weight,
    down_weight,
    cotangent,
):
    dp = lax.axis_size("dp")
    k, core, me = lax.axis_index("row"), lax.axis_index("col"), lax.axis_index("dp")
    table = jnp.stack([k ^ i for i in range(ROWS)] * 2).astype(jnp.int32)
    groups = query_weight.shape[1] // (2 * HEAD_SIZE)
    cosine, sine = rope_tables()

    q_own, q_oth = own_other(query_weight, core, 1)
    k_own, k_oth = own_other(key_matrix, core, 1)
    v_own, v_oth = own_other(value_matrix, core, 1)
    g_own, g_oth = own_other(gate_weight, core, 1)
    u_own, u_oth = own_other(up_weight, core, 1)
    down_own, down_oth = own_other(down_weight, core, 0)
    out_own, out_oth = own_other(output_weight, core, 0)
    qkv_own, qkv_oth = cat([q_own, k_own, v_own], 1), cat([q_oth, k_oth, v_oth], 1)
    gu_own, gu_oth = cat([g_own, u_own], 1), cat([g_oth, u_oth], 1)

    resid = hidden.astype(F32)
    unit_one, factor_one = norm_stats(resid)
    n1 = gather_slots((unit_one * norm_before).astype(BF16))
    qkv_full = cat([qkv_own, swap(qkv_oth)], 0)
    raws = [dot(cat([x, swap(x)], 1), qkv_full, NN) for x in n1]
    att, lse, query, key, value = attend(table, raws, cosine, sine, query_gain, key_gain, groups)

    cot = gather_slots(after(cotangent, n1[3]))
    gu_full = cat([gu_own, swap(gu_oth)], 0)
    down_full = cat([down_own, swap(down_oth)], 1)

    att_oth = swap(att)
    att_both = cat([att, att_oth], 1)
    out_both = cat([out_own, out_oth], 0)
    parts = [dot(att_both[s * BLOCK : (s + 1) * BLOCK], out_both, NN) for s in range(ROWS)]
    middle = resid + scatter_slots(*parts)

    unit_two, factor_two = norm_stats(middle)
    n2 = gather_slots((unit_two * norm_after).astype(BF16))
    ff = g_own.shape[1]
    g_mixed = [dot(cat([x, swap(x)], 1), down_full, NT) for x in cot]
    mixed, dgu, mixed_oth, dgu_oth = [], [], [], []
    for s in range(ROWS):
        both = dot(cat([n2[s], swap(n2[s])], 1), gu_full, NN)
        gate, upper = both[:, :ff], both[:, ff:]
        sigma = jax.nn.sigmoid(gate)
        activ = gate * sigma
        gm = g_mixed[s]
        packed = cat(
            [
                (activ * upper).astype(BF16),
                (gm * upper * sigma * (1.0 + gate * (1.0 - sigma))).astype(BF16),
                (gm * activ).astype(BF16),
            ],
            1,
        )
        other = swap(packed)
        mixed.append(packed[:, :ff])
        dgu.append(packed[:, ff:])
        mixed_oth.append(other[:, :ff])
        dgu_oth.append(other[:, ff:])
    gu_both = cat([gu_own, gu_oth], 1)
    parts = [dot(cat([dgu[s], dgu_oth[s]], 1), gu_both, NT) for s in range(ROWS)]
    dsecond = scatter_slots(*parts)

    cot_all = cat(cot, 0)
    mixed_all, mixed_oth_all = cat(mixed, 0), cat(mixed_oth, 0)
    (down_grad,) = reduce_grads(
        dot(mixed_all, cot_all, TN).astype(BF16),
        dot(mixed_oth_all, cot_all, TN).astype(BF16),
        me, core, dp, (down_weight.shape[1],), 0,
    )
    n2_all = cat(n2, 0)
    gate_grad, up_grad = reduce_grads(
        dot(n2_all, cat(dgu, 0), TN).astype(BF16),
        dot(n2_all, cat(dgu_oth, 0), TN).astype(BF16),
        me, core, dp, (ff, ff), 1,
    )

    dmid_norm, after_part = norm_backward(dsecond, unit_two, factor_two, norm_after)
    dmiddle = cotangent.astype(F32) + dmid_norm
    dmid = gather_slots(dmiddle.astype(BF16))

    down_both = cat([down_own, down_oth], 0)
    parts = [dot(cat([mixed[s], mixed_oth[s]], 1), down_both, NN) for s in range(ROWS)]
    parts[1], parts[3] = after(parts[1], dmid[3]), after(parts[3], dmid[3])
    layer_out = (middle + scatter_slots(*parts)).astype(BF16)

    datt = [
        (dot(x, out_own, NT) + swap(dot(x, out_oth, NT).astype(BF16)).astype(F32)).astype(BF16)
        for x in dmid
    ]
    dmid_all = cat(dmid, 0)
    (output_grad,) = reduce_grads(
        dot(att, dmid_all, TN).astype(BF16),
        dot(att_oth, dmid_all, TN).astype(BF16),
        me, core, dp, (output_weight.shape[1],), 0,
    )
    dqkv, gain_parts = attend_back(
        table, raws, datt, cosine, sine, query_gain, key_gain, (query, key, value, lse), groups
    )
    dqkv_oth = swap(dqkv)
    dqkv_both = cat([dqkv, dqkv_oth], 1)
    qkv_both = cat([qkv_own, qkv_oth], 1)
    parts = [dot(dqkv_both[s * BLOCK : (s + 1) * BLOCK], qkv_both, NT) for s in range(ROWS)]
    dfirst = scatter_slots(*parts)
    n1_all = cat(n1, 0)
    query_grad, key_grad, value_grad = reduce_grads(
        dot(n1_all, dqkv, TN).astype(BF16),
        dot(n1_all, dqkv_oth, TN).astype(BF16),
        me, core, dp, (q_own.shape[1], k_own.shape[1], v_own.shape[1]), 1,
    )
    dres_norm, before_part = norm_backward(dfirst, unit_one, factor_one, norm_before)
    hidden_grad = dmiddle + dres_norm

    before_grad, after_grad = lax.psum((before_part, after_part), ("dp", "row"))
    gain_query, gain_key = lax.psum((gain_parts[0], gain_parts[1]), ("dp", "row", "col"))
    return (
        layer_out,
        hidden_grad,
        before_grad,
        query_grad,
        key_grad,
        value_grad,
        gain_query,
        gain_key,
        output_grad,
        after_grad,
        gate_grad,
        up_grad,
        down_grad,
    )


def solution(mesh):
    placed = (
        P(("dp", "row"), "col"),
        P("col"),
        P("col", "row"),
        P("col", "row"),
        P("col", "row"),
        P(),
        P(),
        P("row", "col"),
        P("col"),
        P("col", "row"),
        P("col", "row"),
        P("row", "col"),
        P(("dp", "row"), "col"),
    )
    return jax.shard_map(
        on_device,
        mesh=mesh,
        in_specs=placed,
        out_specs=(
            P(("dp", "row"), "col"),
            P(("dp", "row"), "col"),
            P("col"),
            P("col", "row"),
            P("col", "row"),
            P("col", "row"),
            P(),
            P(),
            P("row", "col"),
            P("col"),
            P("col", "row"),
            P("col", "row"),
            P("row", "col"),
        ),
        check_vma=False,
    )
```

time: 1040 us -> 690 us (0.66)
  waiting for transfers between devices: 720 us -> 266 us
  starting transfers between devices: 1.83 us -> 87.1 us
  other arithmetic: 69.6 us -> 22.9 us
  Pallas kernels: 0 us -> 45.1 us
  blocking collectives: 58.5 us -> 79.4 us
  matrix products: 127 us -> 147 us
  between operations: 15.2 us -> 3.01 us
    reduce_scatter x11 -> x0, waiting for transfers between devices: 274 us -> none  [the longest x4 231 us: reduce_rows(): return lax.psum_scatter(value_rows, 'row', scatter_dimension=0, tiled=True)]
    ppermute x0 -> x93, waiting for transfers between devices: none -> 266 us  [the longest x24 164 us: row_swap(): return lax.ppermute(x, 'row', [(i, i ^ mask) for i in range(ROWS)])]
    psum x1 -> x0, waiting for transfers between devices: 243 us -> none  [on_device(): lax.psum(query_local.astype(jnp.bfloat16), 'dp').astype(jnp.float32)]
    all_gather x9 -> x0, waiting for transfers between devices: 202 us -> none  [the longest x4 172 us: gather_rows(): return lax.all_gather(value_rows, 'row', axis=0, tiled=True)]
    ppermute x0 -> x93, starting transfers between devices: none -> 87.1 us  [the longest x40 47.3 us: dp_swap(): return lax.ppermute(x, 'dp', [(i, i ^ mask) for i in range(dp)])]
    pallas_call x0 -> x6, Pallas kernels: none -> 45.1 us  [the longest x4 26.9 us: assemble(): pl.pallas_call(functools.partial(assemble_kernel, spans), out_shape=[jax....]
    convert_element_type x15 -> x19, other arithmetic: 37.4 us -> 10.7 us  [the longest x8 4.62 us: halving(): (kept.astype(F32) + dp_swap(sent, second, dp).astype(F32)).astype(BF16)]
    psum x5 -> x2, blocking collectives: 54 us -> 79.4 us  [the longest x1 41.2 us: on_device(): before_grad, after_grad = lax.psum((before_part, after_part), ('dp', 'row'))]
  transfers between devices with their start and end apart: 21 -> 93, of which waited for: 15 -> 31; matrix products, arithmetic and copies ran while one was open for 14% -> 28% of each run, Pallas kernels for 0% -> 5%
where the time goes in v1:
time: 690 us; the launch traced here: 680 us
  waiting for transfers between devices  266 us (39%)
  matrix products  147 us (21%)
  starting transfers between devices  87.1 us (13%)
  blocking collectives  79.4 us (12%)
  Pallas kernels  45.1 us (7%)
  local copies, waits for them, and re-layouts  29 us (4%)
  other arithmetic  22.9 us (3%)
    ppermute x24, waiting for transfers between devices, row_swap(): return lax.ppermute(x, 'row', [(i, i ^ mask) for i in range(ROWS)])  164 us
    dot_general x44, matrix products, dot(): return lax.dot_general(a, b, (dims, ((), ())), preferred_element_type=F32)  147 us
    ppermute x40, waiting for transfers between devices, dp_swap(): return lax.ppermute(x, 'dp', [(i, i ^ mask) for i in range(dp)])  101 us
    ppermute x40, starting transfers between devices, dp_swap(): return lax.ppermute(x, 'dp', [(i, i ^ mask) for i in range(dp)])  47.3 us
    psum x1, blocking collectives, on_device(): before_grad, after_grad = lax.psum((before_part, after_part), ('dp', 'row'))  41.2 us
    psum x1, blocking collectives, on_device(): lax.psum((gain_parts[0], gain_parts[1]), ('dp', 'row', 'col'))  38.2 us
    ppermute x24, starting transfers between devices, row_swap(): return lax.ppermute(x, 'row', [(i, i ^ mask) for i in range(ROWS)])  34.5 us
    pallas_call x4, Pallas kernels, assemble(): pl.pallas_call(functools.partial(assemble_kernel, spans), out_shape=[jax....  26.9 us
  transfers between devices with their start and end apart: 93, of which 31 were waited for; matrix products, arithmetic and copies ran while one was open for 28% of the time, Pallas kernels for 5%

profile of v1, /device:TPU:0, one launch (start us, length us, event | category | flops | bytes accessed | tf_op | source)
XLA Modules:
  0.0 680.2 jit_solution(13538725127749770876)
XLA Ops:
  8.0 4.1 collective-permute-start.5
  17.6 18.2 %collective-permute-done.5 = bf16[256,1024]{1,0:T(8,128)(2,1)} collective-permute-done((bf16[256,1024]{1,0:T(8,128)(2,1)}, bf16[256,1024]{1,0:T(8,128)(2,1)}, u32[]{:S(2)}, u32[]{:S(2)}) %collective-permute-start.5) | collective-permute-done | bytes 524320 | tf_op jit(solution)/shard_map/ppermute | solution.py:30
  36.5 4.9 constant_dynamic-slice_fusion.20
  41.9 3.7 fusion.100.refs_0_
  45.6 3.7 collective-permute-done.7
  49.3 3.1 fusion.104.refs_1_
  58.1 8.1 %shard_map.228 = (bf16[1024,256]{1,0:T(8,128)(2,1)}, f32[1024,256]{1,0:T(8,128)}, bf16[1024,256]{1,0:T(8,128)(2,1)}, bf16[1024,128]{1,0:T(8,128)(2,1)}, bf16[1024,128]{1,0:T(8,128)(2,1)}) custom-call(s32[8]{0:T(128)} %stack.103.table, f32[256,512]{1,0:T(8,128)} %fusion.100.refs_0_, f32[256,512]{1,0:T(8,128)} %fusion.104.refs_1_, ...), custom_call_target="tpu_custom_call" | custom-call | flops 710410240 | bytes 6291456 | tf_op jit(solution)/shard_map/pallas_call | solution.py:262
  72.9 12.0 %collective-permute-done.11 = bf16[256,1024]{1,0:T(8,128)(2,1)S(1)} collective-permute-done((bf16[256,1024]{1,0:T(8,128)(2,1)S(1)}, bf16[256,1024]{1,0:T(8,128)(2,1)S(1)}, u32[]{:S(2)}, u32[]{:S(2)}) %collective-permute-start.11) | collective-permute-done | bytes 524320 | tf_op jit(solution)/shard_map/ppermute | solution.py:30
  88.4 16.9 %collective-permute-done.10 = bf16[256,1024]{1,0:T(8,128)(2,1)S(1)} collective-permute-done((bf16[256,1024]{1,0:T(8,128)(2,1)S(1)}, bf16[256,1024]{1,0:T(8,128)(2,1)S(1)}, u32[]{:S(2)}, u32[]{:S(2)}) %collective-permute-start.10) | collective-permute-done | bytes 524320 | tf_op jit(solution)/shard_map/ppermute | solution.py:30
  105.3 18.3 %collective-permute-done.12 = bf16[256,1024]{1,0:T(8,128)(2,1)S(1)} collective-permute-done((bf16[256,1024]{1,0:T(8,128)(2,1)S(1)}, bf16[256,1024]{1,0:T(8,128)(2,1)S(1)}, u32[]{:S(2)}, u32[]{:S(2)}) %collective-permute-start.12) | collective-permute-done | bytes 524320 | tf_op jit(solution)/shard_map/ppermute | solution.py:30
  128.0 4.8 collective-permute-done.25
  136.1 8.1 %collective-permute-done.21 = bf16[256,1024]{1,0:T(8,128)(2,1)} collective-permute-done((bf16[256,1024]{1,0:T(8,128)(2,1)S(1)}, bf16[256,1024]{1,0:T(8,128)(2,1)}, u32[]{:S(2)}, u32[]{:S(2)}) %collective-permute-start.21) | collective-permute-done | bytes 524320 | tf_op jit(solution)/shard_map/ppermute | solution.py:30
  145.3 10.0 %collective-permute-done.30 = bf16[256,1024]{1,0:T(8,128)(2,1)} collective-permute-done((bf16[256,1024]{1,0:T(8,128)(2,1)S(1)}, bf16[256,1024]{1,0:T(8,128)(2,1)}, u32[]{:S(2)}, u32[]{:S(2)}) %collective-permute-start.30) | collective-permute-done | bytes 524320 | tf_op jit(solution)/shard_map/ppermute | solution.py:30
  157.0 13.9 %fusion.116 = f32[256,1536]{1,0:T(8,128)S(1)} fusion(bf16[256,1024]{1,0:T(8,128)(2,1)} %collective-permute-done.14, bf16[256,1024]{1,0:T(8,128)(2,1)} %multiply_convert_fusion, bf16[1024,1536]{1,0:T(8,128)(2,1)} %collective-permute-done.15, bf16[1024,768]{1,0:T(8,128)(2,1)S(1)} %copy-done.17, bf16[1024,768]{1,0:T(8,128)(2,1)S(1)} %copy-done.18), kind=kOutput, calls=%fused_computation.153 | convolution fusion | flops 1631584256 | bytes 8912896 | tf_op jit(solution)/shard_map/dot_general | solution.py:148
  171.5 3.9 collective-permute-start.27
  178.4 20.7 %collective-permute-done.27 = bf16[256,1024]{1,0:T(8,128)(2,1)S(1)} collective-permute-done((bf16[256,1024]{1,0:T(8,128)(2,1)}, bf16[256,1024]{1,0:T(8,128)(2,1)S(1)}, u32[]{:S(2)}, u32[]{:S(2)}) %collective-permute-start.27) | collective-permute-done | bytes 524320 | tf_op jit(solution)/shard_map/ppermute | solution.py:30
  199.2 13.9 %fusion.124 = f32[256,1536]{1,0:T(8,128)S(1)} fusion(bf16[256,1024]{1,0:T(8,128)(2,1)S(1)} %collective-permute-done.20, bf16[256,1024]{1,0:T(8,128)(2,1)S(1)} %collective-permute-done.19, bf16[1024,1536]{1,0:T(8,128)(2,1)} %collective-permute-done.15, bf16[1024,768]{1,0:T(8,128)(2,1)S(1)} %copy-done.17, bf16[1024,768]{1,0:T(8,128)(2,1)S(1)} %copy-done.18), kind=kOutput, calls=%fused_computation.161 | convolution fusion | flops 1631584256 | bytes 8912896 | tf_op jit(solution)/shard_map/dot_general | solution.py:148
  217.2 13.7 %fusion.136 = f32[256,1536]{1,0:T(8,128)S(1)} fusion(bf16[256,1024]{1,0:T(8,128)(2,1)S(1)} %collective-permute-done.28, bf16[256,1024]{1,0:T(8,128)(2,1)S(1)} %collective-permute-done.27, bf16[1024,1536]{1,0:T(8,128)(2,1)} %collective-permute-done.15, bf16[1024,768]{1,0:T(8,128)(2,1)S(1)} %copy-done.17, bf16[1024,768]{1,0:T(8,128)(2,1)S(1)} %copy-done.18), kind=kOutput, calls=%fused_computation.173 | convolution fusion | flops 1631584256 | bytes 8912896 | tf_op jit(solution)/shard_map/dot_general | solution.py:148
  233.8 14.1 %fusion.144 = f32[256,1536]{1,0:T(8,128)S(1)} fusion(bf16[256,1024]{1,0:T(8,128)(2,1)S(1)} %collective-permute-done.33, bf16[256,1024]{1,0:T(8,128)(2,1)S(1)} %collective-permute-done.32, bf16[1024,1536]{1,0:T(8,128)(2,1)} %collective-permute-done.15, bf16[1024,768]{1,0:T(8,128)(2,1)S(1)} %copy-done.17, bf16[1024,768]{1,0:T(8,128)(2,1)S(1)} %copy-done.18), kind=kOutput, calls=%fused_computation.181 | convolution fusion | flops 1631584256 | bytes 8912896 | tf_op jit(solution)/shard_map/dot_general | solution.py:148
  256.5 5.1 convolution_convert_fusion.1
  264.1 10.2 %collective-permute-done.83 = bf16[384,1024]{1,0:T(8,128)(2,1)S(1)} collective-permute-done((bf16[384,1024]{1,0:T(8,128)(2,1)}, bf16[384,1024]{1,0:T(8,128)(2,1)S(1)}, u32[]{:S(2)}, u32[]{:S(2)}) %collective-permute-start.83) | collective-permute-done | bytes 786464 | tf_op jit(solution)/shard_map/ppermute | solution.py:48
  281.0 3.3 fusion.151
  293.4 4.8 convolution_convert_fusion
  298.3 3.2 fusion.158
  315.6 17.5 %collective-permute-done.36 = bf16[256,1024]{1,0:T(8,128)(2,1)S(1)} collective-permute-done((bf16[256,1024]{1,0:T(8,128)(2,1)S(1)}, bf16[256,1024]{1,0:T(8,128)(2,1)S(1)}, u32[]{:S(2)}, u32[]{:S(2)}) %collective-permute-start.36) | collective-permute-done | bytes 524320 | tf_op jit(solution)/shard_map/ppermute | solution.py:30
  333.0 3.1 multiply_reduce_fusion
  338.6 23.1 %collective-permute-done.74 = bf16[256,1536]{1,0:T(8,128)(2,1)S(1)} collective-permute-done((bf16[256,1536]{1,0:T(8,128)(2,1)S(1)}, bf16[256,1536]{1,0:T(8,128)(2,1)S(1)}, u32[]{:S(2)}, u32[]{:S(2)}) %collective-permute-start.74) | collective-permute-done | bytes 786464 | tf_op jit(solution)/shard_map/ppermute | solution.py:48
  369.4 16.4 %collective-permute-done.38 = bf16[256,1024]{1,0:T(8,128)(2,1)} collective-permute-done((bf16[256,1024]{1,0:T(8,128)(2,1)S(1)}, bf16[256,1024]{1,0:T(8,128)(2,1)}, u32[]{:S(2)}, u32[]{:S(2)}) %collective-permute-start.38) | collective-permute-done | bytes 524320 | tf_op jit(solution)/shard_map/ppermute | solution.py:30
  395.4 4.9 collective-permute-done.86.refs_2_
  401.2 7.0 %collective-permute-done.87.refs_3_ = bf16[192,1024]{1,0:T(8,128)(2,1)S(1)} collective-permute-done((bf16[192,1024]{1,0:T(8,128)(2,1)S(1)}, bf16[192,1024]{1,0:T(8,128)(2,1)S(1)}, u32[]{:S(2)}, u32[]{:S(2)}) %collective-permute-start.87) | collective-permute-done | bytes 393248 | tf_op jit(solution)/shard_map/ppermute | solution.py:48
  411.0 6.6 shard_map.233
  431.6 10.2 %shard_map.229 = (bf16[1024,512]{1,0:T(8,128)(2,1)}, f32[2,128]{1,0:T(2,128)}) custom-call(s32[8]{0:T(128)} %stack.103.table, f32[256,512]{1,0:T(8,128)} %fusion.100.refs_0_, f32[256,512]{1,0:T(8,128)} %fusion.104.refs_1_, f32[256,512]{1,0:T(8,128)} %fusion.108.refs_2_, f32[256,512]{1,0:T(8,128)} %fusion.112.refs_3_, ...), custom_call_target="tpu_custom_call" | custom-call | flops 1717043200 | bytes 6291456 | tf_op jit(solution)/shard_map/pallas_call | solution.py:279
  442.6 38.2 %all-reduce = (f32[128]{0:T(128)}, f32[128]{0:T(128)}) all-reduce(f32[128]{0:T(128)S(1)} %get-tuple-element.84, f32[128]{0:T(128)S(1)} %get-tuple-element.83), channel_id=1, replica_groups=mesh['dp'=4,'row'=4,'col'=2] {'dp','row','col'}, use_global_device_ids=true, to_apply=%region_6.7 | all-reduce | flops 256 | bytes 2048 | tf_op jit(solution)/shard_map/psum | solution.py:453
  492.6 12.8 %collective-permute-done.69 = bf16[64,1024]{1,0:T(8,128)(2,1)S(1)} collective-permute-done((bf16[64,1024]{1,0:T(8,128)(2,1)S(1)}, bf16[64,1024]{1,0:T(8,128)(2,1)S(1)}, u32[]{:S(2)}, u32[]{:S(2)}) %collective-permute-start.69) | collective-permute-done | bytes 131104 | tf_op jit(solution)/shard_map/ppermute | solution.py:48
  507.3 3.3 collective-permute-done.64
  521.5 3.3 fusion.88
  528.4 5.1 shard_map.231
  535.3 3.3 convolution_convert_fusion.4
  542.4 3.3 collective-permute-done.76.refs_2_
  549.2 25.4 %collective-permute-done.80.refs_5_ = bf16[256,1536]{1,0:T(8,128)(2,1)S(1)} collective-permute-done((bf16[256,1536]{1,0:T(8,128)(2,1)S(1)}, bf16[256,1536]{1,0:T(8,128)(2,1)S(1)}, u32[]{:S(2)}, u32[]{:S(2)}) %collective-permute-start.80) | collective-permute-done | bytes 786464 | tf_op jit(solution)/shard_map/ppermute | solution.py:48
  581.8 13.4 %collective-permute-done.40 = bf16[256,1024]{1,0:T(8,128)(2,1)S(1)} collective-permute-done((bf16[256,1024]{1,0:T(8,128)(2,1)S(1)}, bf16[256,1024]{1,0:T(8,128)(2,1)S(1)}, u32[]{:S(2)}, u32[]{:S(2)}) %collective-permute-start.40) | collective-permute-done | bytes 524320 | tf_op jit(solution)/shard_map/ppermute | solution.py:30
  600.9 3.3 fusion.87
  607.2 9.4 %shard_map.232 = (f32[1024,1536]{1,0:T(8,128)}, f32[1024,1536]{1,0:T(8,128)}) custom-call(s32[10]{0:T(128)} %stack.114.table_ref, bf16[256,1536]{1,0:T(8,128)(2,1)} %add_convert_fusion.5.refs_0_, bf16[256,1536]{1,0:T(8,128)(2,1)} %collective-permute-done.75.refs_1_, bf16[256,1536]{1,0:T(8,128)(2,1)} %collective-permute-done.76.refs_2_, ...), custom_call_target="tpu_custom_call" | custom-call | bytes 18874368 | tf_op jit(solution)/shard_map/pallas_call | solution.py:104
  622.3 4.0 fusion.98
  626.2 41.2 %all-reduce.1 = (f32[1024]{0:T(1024)}, f32[1024]{0:T(1024)}) all-reduce(f32[1024]{0:T(1024)S(1)} %get-tuple-element.45, f32[1024]{0:T(1024)S(1)} %get-tuple-element.43), channel_id=1, replica_groups=mesh['dp'=4,'row'=4,'col'=2] {'dp','row'}, use_global_device_ids=true, to_apply=%region_5.6 | all-reduce | flops 2048 | bytes 16384 | tf_op jit(solution)/shard_map/psum | solution.py:452
  667.6 3.0 fusion.97
  670.7 3.2 collective-permute-done.62.refs_7_
  673.9 5.8 shard_map.230
  (484 shorter events, 187.9 us)
Async XLA Ops:
  7.0 34.9 %collective-permute-start.2 = (bf16[1024,512]{1,0:T(8,128)(2,1)}, bf16[1024,512]{1,0:T(8,128)(2,1)}, u32[]{:S(2)}, u32[]{:S(2)}) collective-permute-start(bf16[1024,512]{1,0:T(8,128)(2,1)} %pad_maximum_fusion.13), channel_id=1, source_target_pairs={{0,1},{1,0},{2,3},{3,2},{4,5},{5,4},{6,7},{7,6},{8,9},{9,8},{10,11... | collective-permute-start | bytes 3145736 | tf_op jit(solution)/shard_map/ppermute | solution.py:26
  8.0 27.8 %collective-permute-start.5 = (bf16[256,1024]{1,0:T(8,128)(2,1)}, bf16[256,1024]{1,0:T(8,128)(2,1)}, u32[]{:S(2)}, u32[]{:S(2)}) collective-permute-start(bf16[256,1024]{1,0:T(8,128)(2,1)} %fusion.93), channel_id=1, source_target_pairs={{0,4},{2,6},{4,0},{6,2},{1,5},{3,7},{5,1},{7,3},{8,12},{10,14},{12... | collective-permute-start | bytes 1572872 | tf_op jit(solution)/shard_map/ppermute | solution.py:30
  12.1 24.4 %collective-permute-start.3 = (bf16[256,1024]{1,0:T(8,128)(2,1)}, bf16[256,1024]{1,0:T(8,128)(2,1)}, u32[]{:S(2)}, u32[]{:S(2)}) collective-permute-start(bf16[256,1024]{1,0:T(8,128)(2,1)} %fusion.93), channel_id=1, source_target_pairs={{0,2},{2,0},{4,6},{6,4},{1,3},{3,1},{5,7},{7,5},{8,10},{10,8},{12,... | collective-permute-start | bytes 1572872 | tf_op jit(solution)/shard_map/ppermute | solution.py:30
  13.7 28.2 %collective-permute-start.1 = (bf16[256,1024]{1,0:T(8,128)(2,1)}, bf16[256,1024]{1,0:T(8,128)(2,1)}, u32[]{:S(2)}, u32[]{:S(2)}) collective-permute-start(bf16[256,1024]{1,0:T(8,128)(2,1)} %fusion.93), channel_id=1, source_target_pairs={{0,1},{1,0},{2,3},{3,2},{4,5},{5,4},{6,7},{7,6},{8,9},{9,8},{10,11... | collective-permute-start | bytes 1572872 | tf_op jit(solution)/shard_map/ppermute | solution.py:26
  68.4 88.0 %collective-permute-start.15 = (bf16[1024,1536]{1,0:T(8,128)(2,1)}, bf16[1024,1536]{1,0:T(8,128)(2,1)}, u32[]{:S(2)}, u32[]{:S(2)}) collective-permute-start(bf16[1024,1536]{1,0:T(8,128)(2,1)} %pad_maximum_fusion.2), channel_id=1, source_target_pairs={{0,1},{1,0},{2,3},{3,2},{4,5},{5,4},{6,7},{7,6},{8,9},{9,8},{10,11... | collective-permute-start | bytes 9437192 | tf_op jit(solution)/shard_map/ppermute | solution.py:26
  72.0 33.3 %collective-permute-start.10 = (bf16[256,1024]{1,0:T(8,128)(2,1)S(1)}, bf16[256,1024]{1,0:T(8,128)(2,1)S(1)}, u32[]{:S(2)}, u32[]{:S(2)}) collective-permute-start(bf16[256,1024]{1,0:T(8,128)(2,1)S(1)} %convolution_convert_fusion.7), channel_id=1, source_target_pairs={{0,2},{2,0},{4,6},{6,4},{1,3},{3,1},{5,7},{7,5},{8,10},{10,8},{12,... | collective-permute-start | bytes 1572872 | tf_op jit(solution)/shard_map/ppermute | solution.py:30
  85.3 38.2 %collective-permute-start.12 = (bf16[256,1024]{1,0:T(8,128)(2,1)S(1)}, bf16[256,1024]{1,0:T(8,128)(2,1)S(1)}, u32[]{:S(2)}, u32[]{:S(2)}) collective-permute-start(bf16[256,1024]{1,0:T(8,128)(2,1)S(1)} %fusion.83), channel_id=1, source_target_pairs={{0,4},{2,6},{4,0},{6,2},{1,5},{3,7},{5,1},{7,3},{8,12},{10,14},{12... | collective-permute-start | bytes 1572872 | tf_op jit(solution)/shard_map/ppermute | solution.py:30
  88.3 44.5 %collective-permute-start.25 = (bf16[256,1024]{1,0:T(8,128)(2,1)S(1)}, bf16[256,1024]{1,0:T(8,128)(2,1)S(1)}, u32[]{:S(2)}, u32[]{:S(2)}) collective-permute-start(bf16[256,1024]{1,0:T(8,128)(2,1)S(1)} %copy-done.9), channel_id=1, source_target_pairs={{0,4},{2,6},{4,0},{6,2},{1,5},{3,7},{5,1},{7,3},{8,12},{10,14},{12... | collective-permute-start | bytes 1572872 | tf_op jit(solution)/shard_map/ppermute | solution.py:30
  126.3 44.6 %collective-permute-start.17 = (bf16[768,1024]{1,0:T(8,128)(2,1)}, bf16[768,1024]{1,0:T(8,128)(2,1)}, u32[]{:S(2)}, u32[]{:S(2)}) collective-permute-start(bf16[768,1024]{1,0:T(8,128)(2,1)} %get-tuple-element.68), channel_id=1, source_target_pairs={{0,1},{1,0},{2,3},{3,2},{4,5},{5,4},{6,7},{7,6},{8,9},{9,8},{10,11... | collective-permute-start | bytes 4718600 | tf_op jit(solution)/shard_map/ppermute | solution.py:26
  144.1 27.4 %collective-permute-start.16 = (bf16[256,1024]{1,0:T(8,128)(2,1)S(1)}, bf16[256,1024]{1,0:T(8,128)(2,1)S(1)}, u32[]{:S(2)}, u32[]{:S(2)}) collective-permute-start(bf16[256,1024]{1,0:T(8,128)(2,1)S(1)} %copy-done.9), channel_id=1, source_target_pairs={{0,1},{1,0},{2,3},{3,2},{4,5},{5,4},{6,7},{7,6},{8,9},{9,8},{10,11... | collective-permute-start | bytes 1572872 | tf_op jit(solution)/shard_map/ppermute | solution.py:26
  155.3 75.6 %collective-permute-start.26 = (bf16[256,1024]{1,0:T(8,128)(2,1)S(1)}, bf16[256,1024]{1,0:T(8,128)(2,1)S(1)}, u32[]{:S(2)}, u32[]{:S(2)}) collective-permute-start(bf16[256,1024]{1,0:T(8,128)(2,1)S(1)} %collective-permute-done.25), channel_id=1, source_target_pairs={{0,1},{1,0},{2,3},{3,2},{4,5},{5,4},{6,7},{7,6},{8,9},{9,8},{10,11... | collective-permute-start | bytes 1572872 | tf_op jit(solution)/shard_map/ppermute | solution.py:26
  156.4 56.7 %collective-permute-start.22 = (bf16[256,1024]{1,0:T(8,128)(2,1)}, bf16[256,1024]{1,0:T(8,128)(2,1)S(1)}, u32[]{:S(2)}, u32[]{:S(2)}) collective-permute-start(bf16[256,1024]{1,0:T(8,128)(2,1)} %collective-permute-done.21), channel_id=1, source_target_pairs={{0,1},{1,0},{2,3},{3,2},{4,5},{5,4},{6,7},{7,6},{8,9},{9,8},{10,11... | collective-permute-start | bytes 1572872 | tf_op jit(solution)/shard_map/ppermute | solution.py:26
  170.9 77.0 %collective-permute-start.31 = (bf16[256,1024]{1,0:T(8,128)(2,1)}, bf16[256,1024]{1,0:T(8,128)(2,1)S(1)}, u32[]{:S(2)}, u32[]{:S(2)}) collective-permute-start(bf16[256,1024]{1,0:T(8,128)(2,1)} %collective-permute-done.30), channel_id=1, source_target_pairs={{0,1},{1,0},{2,3},{3,2},{4,5},{5,4},{6,7},{7,6},{8,9},{9,8},{10,11... | collective-permute-start | bytes 1572872 | tf_op jit(solution)/shard_map/ppermute | solution.py:26
  171.5 27.6 %collective-permute-start.27 = (bf16[256,1024]{1,0:T(8,128)(2,1)}, bf16[256,1024]{1,0:T(8,128)(2,1)S(1)}, u32[]{:S(2)}, u32[]{:S(2)}) collective-permute-start(bf16[256,1024]{1,0:T(8,128)(2,1)} %multiply_convert_fusion), channel_id=1, source_target_pairs={{0,4},{2,6},{4,0},{6,2},{1,5},{3,7},{5,1},{7,3},{8,12},{10,14},{12... | collective-permute-start | bytes 1572872 | tf_op jit(solution)/shard_map/ppermute | solution.py:30
  175.4 23.8 %collective-permute-start.20 = (bf16[256,1024]{1,0:T(8,128)(2,1)S(1)}, bf16[256,1024]{1,0:T(8,128)(2,1)S(1)}, u32[]{:S(2)}, u32[]{:S(2)}) collective-permute-start(bf16[256,1024]{1,0:T(8,128)(2,1)S(1)} %collective-permute-done.19), channel_id=1, source_target_pairs={{0,1},{1,0},{2,3},{3,2},{4,5},{5,4},{6,7},{7,6},{8,9},{9,8},{10,11... | collective-permute-start | bytes 1572872 | tf_op jit(solution)/shard_map/ppermute | solution.py:26
  199.1 62.6 %collective-permute-start.18 = (bf16[256,2304]{1,0:T(8,128)(2,1)S(1)}, bf16[256,2304]{1,0:T(8,128)(2,1)S(1)}, u32[]{:S(2)}, u32[]{:S(2)}) collective-permute-start(bf16[256,2304]{1,0:T(8,128)(2,1)S(1)} %pad_maximum_fusion.9), channel_id=1, source_target_pairs={{0,1},{1,0},{2,3},{3,2},{4,5},{5,4},{6,7},{7,6},{8,9},{9,8},{10,11... | collective-permute-start | bytes 3538952 | tf_op jit(solution)/shard_map/ppermute | solution.py:26
  216.6 47.4 %collective-permute-start.23 = (bf16[256,2304]{1,0:T(8,128)(2,1)S(1)}, bf16[256,2304]{1,0:T(8,128)(2,1)S(1)}, u32[]{:S(2)}, u32[]{:S(2)}) collective-permute-start(bf16[256,2304]{1,0:T(8,128)(2,1)S(1)} %pad_maximum_fusion.10), channel_id=1, source_target_pairs={{0,1},{1,0},{2,3},{3,2},{4,5},{5,4},{6,7},{7,6},{8,9},{9,8},{10,11... | collective-permute-start | bytes 3538952 | tf_op jit(solution)/shard_map/ppermute | solution.py:26
  233.7 47.2 %collective-permute-start.29 = (bf16[256,2304]{1,0:T(8,128)(2,1)S(1)}, bf16[256,2304]{1,0:T(8,128)(2,1)S(1)}, u32[]{:S(2)}, u32[]{:S(2)}) collective-permute-start(bf16[256,2304]{1,0:T(8,128)(2,1)S(1)} %pad_maximum_fusion.11), channel_id=1, source_target_pairs={{0,1},{1,0},{2,3},{3,2},{4,5},{5,4},{6,7},{7,6},{8,9},{9,8},{10,11... | collective-permute-start | bytes 3538952 | tf_op jit(solution)/shard_map/ppermute | solution.py:26
  256.3 30.2 %collective-permute-start.34 = (bf16[256,2304]{1,0:T(8,128)(2,1)}, bf16[256,2304]{1,0:T(8,128)(2,1)S(1)}, u32[]{:S(2)}, u32[]{:S(2)}) collective-permute-start(bf16[256,2304]{1,0:T(8,128)(2,1)} %pad_maximum_fusion.12), channel_id=1, source_target_pairs={{0,1},{1,0},{2,3},{3,2},{4,5},{5,4},{6,7},{7,6},{8,9},{9,8},{10,11... | collective-permute-start | bytes 3538952 | tf_op jit(solution)/shard_map/ppermute | solution.py:26
  261.7 45.8 %collective-permute-start.73 = (bf16[512,1536]{1,0:T(8,128)(2,1)S(1)}, bf16[512,1536]{1,0:T(8,128)(2,1)S(1)}, u32[]{:S(2)}, u32[]{:S(2)}) collective-permute-start(bf16[512,1536]{1,0:T(8,128)(2,1)S(1)} %constant_dynamic-slice_fusion.7), channel_id=1, source_target_pairs={{0,8},{8,0},{16,24},{24,16},{1,9},{9,1},{17,25},{25,17},{2,10},{10... | collective-permute-start | bytes 4718600 | tf_op jit(solution)/shard_map/ppermute | solution.py:48
  278.9 36.7 %collective-permute-start.24 = (bf16[256,1024]{1,0:T(8,128)(2,1)}, bf16[256,1024]{1,0:T(8,128)(2,1)}, u32[]{:S(2)}, u32[]{:S(2)}) collective-permute-start(bf16[256,1024]{1,0:T(8,128)(2,1)} %fusion.80), channel_id=1, source_target_pairs={{0,2},{2,0},{4,6},{6,4},{1,3},{3,1},{5,7},{7,5},{8,10},{10,8},{12,... | collective-permute-start | bytes 1572872 | tf_op jit(solution)/shard_map/ppermute | solution.py:30
  284.9 103.3 %collective-permute-start.85 = (bf16[192,1024]{1,0:T(8,128)(2,1)S(1)}, bf16[192,1024]{1,0:T(8,128)(2,1)S(1)}, u32[]{:S(2)}, u32[]{:S(2)}) collective-permute-start(bf16[192,1024]{1,0:T(8,128)(2,1)S(1)} %add_convert_fusion.9.refs_0_), channel_id=1, source_target_pairs={{0,16},{8,24},{16,0},{24,8},{1,17},{9,25},{17,1},{25,9},{2,18},{10... | collective-permute-start | bytes 1179656 | tf_op jit(solution)/shard_map/ppermute | solution.py:48
  303.0 65.5 %collective-permute-start.78 = (bf16[512,1536]{1,0:T(8,128)(2,1)S(1)}, bf16[512,1536]{1,0:T(8,128)(2,1)S(1)}, u32[]{:S(2)}, u32[]{:S(2)}) collective-permute-start(bf16[512,1536]{1,0:T(8,128)(2,1)S(1)} %constant_dynamic-slice_fusion.5), channel_id=1, source_target_pairs={{0,16},{8,24},{16,0},{24,8},{1,17},{9,25},{17,1},{25,9},{2,18},{10... | collective-permute-start | bytes 4718600 | tf_op jit(solution)/shard_map/ppermute | solution.py:48
  307.5 25.5 %collective-permute-start.36 = (bf16[256,1024]{1,0:T(8,128)(2,1)S(1)}, bf16[256,1024]{1,0:T(8,128)(2,1)S(1)}, u32[]{:S(2)}, u32[]{:S(2)}) collective-permute-start(bf16[256,1024]{1,0:T(8,128)(2,1)S(1)} %fusion.84), channel_id=1, source_target_pairs={{0,4},{2,6},{4,0},{6,2},{1,5},{3,7},{5,1},{7,3},{8,12},{10,14},{12... | collective-permute-start | bytes 1572872 | tf_op jit(solution)/shard_map/ppermute | solution.py:30
  313.3 48.4 %collective-permute-start.74 = (bf16[256,1536]{1,0:T(8,128)(2,1)S(1)}, bf16[256,1536]{1,0:T(8,128)(2,1)S(1)}, u32[]{:S(2)}, u32[]{:S(2)}) collective-permute-start(bf16[256,1536]{1,0:T(8,128)(2,1)S(1)} %constant_dynamic-slice_fusion.6), channel_id=1, source_target_pairs={{0,16},{8,24},{16,0},{24,8},{1,17},{9,25},{17,1},{25,9},{2,18},{10... | collective-permute-start | bytes 2359304 | tf_op jit(solution)/shard_map/ppermute | solution.py:48
  336.2 28.4 %collective-permute-start.89 = (bf16[192,1024]{1,0:T(8,128)(2,1)S(1)}, bf16[192,1024]{1,0:T(8,128)(2,1)S(1)}, u32[]{:S(2)}, u32[]{:S(2)}) collective-permute-start(bf16[192,1024]{1,0:T(8,128)(2,1)S(1)} %constant_dynamic-slice_fusion), channel_id=1, source_target_pairs={{0,8},{8,0},{16,24},{24,16},{1,9},{9,1},{17,25},{25,17},{2,10},{10... | collective-permute-start | bytes 1179656 | tf_op jit(solution)/shard_map/ppermute | solution.py:48
  338.1 30.8 %collective-permute-start.44 = (bf16[256,1024]{1,0:T(8,128)(2,1)S(1)}, bf16[256,1024]{1,0:T(8,128)(2,1)S(1)}, u32[]{:S(2)}, u32[]{:S(2)}) collective-permute-start(bf16[256,1024]{1,0:T(8,128)(2,1)S(1)} %fusion.205), channel_id=1, source_target_pairs={{0,2},{2,0},{4,6},{6,4},{1,3},{3,1},{5,7},{7,5},{8,10},{10,8},{12,... | collective-permute-start | bytes 1572872 | tf_op jit(solution)/shard_map/ppermute | solution.py:30
  361.7 24.0 %collective-permute-start.38 = (bf16[256,1024]{1,0:T(8,128)(2,1)S(1)}, bf16[256,1024]{1,0:T(8,128)(2,1)}, u32[]{:S(2)}, u32[]{:S(2)}) collective-permute-start(bf16[256,1024]{1,0:T(8,128)(2,1)S(1)} %fusion.205), channel_id=1, source_target_pairs={{0,4},{2,6},{4,0},{6,2},{1,5},{3,7},{5,1},{7,3},{8,12},{10,14},{12... | collective-permute-start | bytes 1572872 | tf_op jit(solution)/shard_map/ppermute | solution.py:30
  366.0 23.8 %collective-permute-start.90 = (bf16[192,1024]{1,0:T(8,128)(2,1)S(1)}, bf16[192,1024]{1,0:T(8,128)(2,1)S(1)}, u32[]{:S(2)}, u32[]{:S(2)}) collective-permute-start(bf16[192,1024]{1,0:T(8,128)(2,1)S(1)} %add_convert_fusion.8.refs_4_), channel_id=1, source_target_pairs={{0,8},{8,0},{16,24},{24,16},{1,9},{9,1},{17,25},{25,17},{2,10},{10... | collective-permute-start | bytes 1179656 | tf_op jit(solution)/shard_map/ppermute | solution.py:48
  387.2 30.5 %collective-permute-start.39 = (bf16[256,1024]{1,0:T(8,128)(2,1)}, bf16[256,1024]{1,0:T(8,128)(2,1)}, u32[]{:S(2)}, u32[]{:S(2)}) collective-permute-start(bf16[256,1024]{1,0:T(8,128)(2,1)} %collective-permute-done.38), channel_id=1, source_target_pairs={{0,2},{2,0},{4,6},{6,4},{1,3},{3,1},{5,7},{7,5},{8,10},{10,8},{12,... | collective-permute-start | bytes 1572872 | tf_op jit(solution)/shard_map/ppermute | solution.py:30
  400.3 112.0 %collective-permute-start.75 = (bf16[256,1536]{1,0:T(8,128)(2,1)}, bf16[256,1536]{1,0:T(8,128)(2,1)}, u32[]{:S(2)}, u32[]{:S(2)}) collective-permute-start(bf16[256,1536]{1,0:T(8,128)(2,1)} %add_convert_fusion.5.refs_0_), channel_id=1, source_target_pairs={{0,16},{8,24},{16,0},{24,8},{1,17},{9,25},{17,1},{25,9},{2,18},{10... | collective-permute-start | bytes 2359304 | tf_op jit(solution)/shard_map/ppermute | solution.py:48
  408.2 78.1 %collective-permute-start.79 = (bf16[256,1536]{1,0:T(8,128)(2,1)}, bf16[256,1536]{1,0:T(8,128)(2,1)}, u32[]{:S(2)}, u32[]{:S(2)}) collective-permute-start(bf16[256,1536]{1,0:T(8,128)(2,1)} %constant_dynamic-slice_fusion.4), channel_id=1, source_target_pairs={{0,8},{8,0},{16,24},{24,16},{1,9},{9,1},{17,25},{25,17},{2,10},{10... | collective-permute-start | bytes 2359304 | tf_op jit(solution)/shard_map/ppermute | solution.py:48
  422.4 65.2 %collective-permute-start.68 = (bf16[128,1024]{1,0:T(8,128)(2,1)}, bf16[128,1024]{1,0:T(8,128)(2,1)}, u32[]{:S(2)}, u32[]{:S(2)}) collective-permute-start(bf16[128,1024]{1,0:T(8,128)(2,1)} %constant_dynamic-slice_fusion.9), channel_id=1, source_target_pairs={{0,16},{8,24},{16,0},{24,8},{1,17},{9,25},{17,1},{25,9},{2,18},{10... | collective-permute-start | bytes 786440 | tf_op jit(solution)/shard_map/ppermute | solution.py:48
  426.1 65.0 %collective-permute-start.63 = (bf16[128,1024]{1,0:T(8,128)(2,1)}, bf16[128,1024]{1,0:T(8,128)(2,1)}, u32[]{:S(2)}, u32[]{:S(2)}) collective-permute-start(bf16[128,1024]{1,0:T(8,128)(2,1)} %constant_dynamic-slice_fusion.11), channel_id=1, source_target_pairs={{0,8},{8,0},{16,24},{24,16},{1,9},{9,1},{17,25},{25,17},{2,10},{10... | collective-permute-start | bytes 786440 | tf_op jit(solution)/shard_map/ppermute | solution.py:48
  427.6 92.6 %collective-permute-start.41 = (bf16[256,1024]{1,0:T(8,128)(2,1)}, bf16[256,1024]{1,0:T(8,128)(2,1)}, u32[]{:S(2)}, u32[]{:S(2)}) collective-permute-start(bf16[256,1024]{1,0:T(8,128)(2,1)} %fusion.158), channel_id=1, source_target_pairs={{0,2},{2,0},{4,6},{6,4},{1,3},{3,1},{5,7},{7,5},{8,10},{10,8},{12,... | collective-permute-start | bytes 1572872 | tf_op jit(solution)/shard_map/ppermute | solution.py:30
  486.2 49.1 %collective-permute-start.48 = (bf16[1024,512]{1,0:T(8,128)(2,1)}, bf16[1024,512]{1,0:T(8,128)(2,1)}, u32[]{:S(2)}, u32[]{:S(2)}) collective-permute-start(bf16[1024,512]{1,0:T(8,128)(2,1)} %get-tuple-element.36), channel_id=1, source_target_pairs={{0,1},{1,0},{2,3},{3,2},{4,5},{5,4},{6,7},{7,6},{8,9},{9,8},{10,11... | collective-permute-start | bytes 3145736 | tf_op jit(solution)/shard_map/ppermute | solution.py:26
  487.7 25.7 %collective-permute-start.53 = (bf16[512,512]{1,0:T(8,128)(2,1)S(1)}, bf16[512,512]{1,0:T(8,128)(2,1)S(1)}, u32[]{:S(2)}, u32[]{:S(2)}) collective-permute-start(bf16[512,512]{1,0:T(8,128)(2,1)S(1)} %constant_dynamic-slice_fusion.15), channel_id=1, source_target_pairs={{0,8},{8,0},{16,24},{24,16},{1,9},{9,1},{17,25},{25,17},{2,10},{10... | collective-permute-start | bytes 1572872 | tf_op jit(solution)/shard_map/ppermute | solution.py:48
  526.2 71.3 %collective-permute-start.77 = (bf16[256,1536]{1,0:T(8,128)(2,1)}, bf16[256,1536]{1,0:T(8,128)(2,1)}, u32[]{:S(2)}, u32[]{:S(2)}) collective-permute-start(bf16[256,1536]{1,0:T(8,128)(2,1)} %collective-permute-done.75.refs_1_), channel_id=1, source_target_pairs={{0,8},{8,0},{16,24},{24,16},{1,9},{9,1},{17,25},{25,17},{2,10},{10... | collective-permute-start | bytes 2359304 | tf_op jit(solution)/shard_map/ppermute | solution.py:48
  527.7 69.9 %collective-permute-start.81 = (bf16[256,1536]{1,0:T(8,128)(2,1)S(1)}, bf16[256,1536]{1,0:T(8,128)(2,1)}, u32[]{:S(2)}, u32[]{:S(2)}) collective-permute-start(bf16[256,1536]{1,0:T(8,128)(2,1)S(1)} %add_convert_fusion.4.refs_4_), channel_id=1, source_target_pairs={{0,16},{8,24},{16,0},{24,8},{1,17},{9,25},{17,1},{25,9},{2,18},{10... | collective-permute-start | bytes 2359304 | tf_op jit(solution)/shard_map/ppermute | solution.py:48
  533.5 41.2 %collective-permute-start.80 = (bf16[256,1536]{1,0:T(8,128)(2,1)S(1)}, bf16[256,1536]{1,0:T(8,128)(2,1)S(1)}, u32[]{:S(2)}, u32[]{:S(2)}) collective-permute-start(bf16[256,1536]{1,0:T(8,128)(2,1)S(1)} %add_convert_fusion.4.refs_4_), channel_id=1, source_target_pairs={{0,8},{8,0},{16,24},{24,16},{1,9},{9,1},{17,25},{25,17},{2,10},{10... | collective-permute-start | bytes 2359304 | tf_op jit(solution)/shard_map/ppermute | solution.py:48
  538.6 38.0 %collective-permute-start.58 = (bf16[512,512]{1,0:T(8,128)(2,1)S(1)}, bf16[512,512]{1,0:T(8,128)(2,1)S(1)}, u32[]{:S(2)}, u32[]{:S(2)}) collective-permute-start(bf16[512,512]{1,0:T(8,128)(2,1)S(1)} %constant_dynamic-slice_fusion.13), channel_id=1, source_target_pairs={{0,16},{8,24},{16,0},{24,8},{1,17},{9,25},{17,1},{25,9},{2,18},{10... | collective-permute-start | bytes 1572872 | tf_op jit(solution)/shard_map/ppermute | solution.py:48
  545.7 32.0 %collective-permute-start.50 = (bf16[256,1024]{1,0:T(8,128)(2,1)S(1)}, bf16[256,1024]{1,0:T(8,128)(2,1)S(1)}, u32[]{:S(2)}, u32[]{:S(2)}) collective-permute-start(bf16[256,1024]{1,0:T(8,128)(2,1)S(1)} %convolution_convert_fusion.10), channel_id=1, source_target_pairs={{0,2},{2,0},{4,6},{6,4},{1,3},{3,1},{5,7},{7,5},{8,10},{10,8},{12,... | collective-permute-start | bytes 1572872 | tf_op jit(solution)/shard_map/ppermute | solution.py:30
  577.7 27.3 %collective-permute-start.82 = (bf16[256,1536]{1,0:T(8,128)(2,1)S(1)}, bf16[256,1536]{1,0:T(8,128)(2,1)S(1)}, u32[]{:S(2)}, u32[]{:S(2)}) collective-permute-start(bf16[256,1536]{1,0:T(8,128)(2,1)S(1)} %collective-permute-done.80.refs_5_), channel_id=1, source_target_pairs={{0,16},{8,24},{16,0},{24,8},{1,17},{9,25},{17,1},{25,9},{2,18},{10... | collective-permute-start | bytes 2359304 | tf_op jit(solution)/shard_map/ppermute | solution.py:48
  604.2 66.4 %collective-permute-start.56 = (bf16[256,512]{1,0:T(8,128)(2,1)}, bf16[256,512]{1,0:T(8,128)(2,1)S(1)}, u32[]{:S(2)}, u32[]{:S(2)}) collective-permute-start(bf16[256,512]{1,0:T(8,128)(2,1)} %add_convert_fusion.13.refs_0_), channel_id=1, source_target_pairs={{0,8},{8,0},{16,24},{24,16},{1,9},{9,1},{17,25},{25,17},{2,10},{10... | collective-permute-start | bytes 786440 | tf_op jit(solution)/shard_map/ppermute | solution.py:48
  606.0 64.7 %collective-permute-start.57 = (bf16[256,512]{1,0:T(8,128)(2,1)}, bf16[256,512]{1,0:T(8,128)(2,1)S(1)}, u32[]{:S(2)}, u32[]{:S(2)}) collective-permute-start(bf16[256,512]{1,0:T(8,128)(2,1)} %collective-permute-done.55.refs_1_), channel_id=1, source_target_pairs={{0,8},{8,0},{16,24},{24,16},{1,9},{9,1},{17,25},{25,17},{2,10},{10... | collective-permute-start | bytes 786440 | tf_op jit(solution)/shard_map/ppermute | solution.py:48
  617.6 53.0 %collective-permute-start.61 = (bf16[256,512]{1,0:T(8,128)(2,1)S(1)}, bf16[256,512]{1,0:T(8,128)(2,1)S(1)}, u32[]{:S(2)}, u32[]{:S(2)}) collective-permute-start(bf16[256,512]{1,0:T(8,128)(2,1)S(1)} %add_convert_fusion.12.refs_4_), channel_id=1, source_target_pairs={{0,16},{8,24},{16,0},{24,8},{1,17},{9,25},{17,1},{25,9},{2,18},{10... | collective-permute-start | bytes 786440 | tf_op jit(solution)/shard_map/ppermute | solution.py:48
  618.7 48.7 %collective-permute-start.60 = (bf16[256,512]{1,0:T(8,128)(2,1)S(1)}, bf16[256,512]{1,0:T(8,128)(2,1)S(1)}, u32[]{:S(2)}, u32[]{:S(2)}) collective-permute-start(bf16[256,512]{1,0:T(8,128)(2,1)S(1)} %add_convert_fusion.12.refs_4_), channel_id=1, source_target_pairs={{0,8},{8,0},{16,24},{24,16},{1,9},{9,1},{17,25},{25,17},{2,10},{10... | collective-permute-start | bytes 786440 | tf_op jit(solution)/shard_map/ppermute | solution.py:48
  626.2 41.4 %collective-permute-start.52 = (f32[256]{0:T(256)S(1)}, f32[256]{0:T(256)S(1)}, u32[]{:S(2)}, u32[]{:S(2)}) collective-permute-start(f32[256]{0:T(256)S(1)} %get-tuple-element.46), channel_id=1, source_target_pairs={{0,1},{1,0},{2,3},{3,2},{4,5},{5,4},{6,7},{7,6},{8,9},{9,8},{10,11... | collective-permute-start | bytes 3080 | tf_op jit(solution)/shard_map/ppermute | solution.py:26
  (152 other events, 2399.4 us)

commit v2 on v1

--- a/solution.py
+++ b/solution.py
@@ -20,6 +20,9 @@
 
 F32 = jnp.float32
 BF16 = jnp.bfloat16
+SMEM = pl.BlockSpec(memory_space=pltpu.SMEM)
+VMEM = pl.BlockSpec(memory_space=pltpu.VMEM)
+NO_COST = pl.CostEstimate(flops=1, transcendentals=0, bytes_accessed=1)
 
 
 def swap(x):
@@ -30,22 +33,19 @@
     return lax.ppermute(x, "row", [(i, i ^ mask) for i in range(ROWS)])
 
 
-def gather_slots(x):
-    two = row_swap(x, 2)
-    one = row_swap(x, 1)
-    three = row_swap(two, 1)
-    return [x, one, two, three]
-
-
-def scatter_slots(own, one, two, three):
-    got_three = row_swap(three.astype(BF16), 1)
-    got_one = row_swap(one.astype(BF16), 1)
-    got_two = row_swap((two + got_three.astype(F32)).astype(BF16), 2)
-    return own + got_one.astype(F32) + got_two.astype(F32)
+def after(x, *others):
+    return lax.optimization_barrier((x, *others))[0]
 
 
 def dp_swap(x, mask, dp):
     return lax.ppermute(x, "dp", [(i, i ^ mask) for i in range(dp)])
+
+
+def small_sum(x, axis, size):
+    swapped = lambda mask: lax.ppermute(x, axis, [(i, i ^ mask) for i in range(size)])
+    if size == 4:
+        return (x + swapped(1)) + (swapped(2) + swapped(3))
+    return lax.psum(x, axis)
 
 
 def halving(part, bits, me, dp):
@@ -113,10 +113,42 @@
                 for width in widths
             ],
         ),
-        cost_estimate=pl.CostEstimate(
-            flops=0, transcendentals=0, bytes_accessed=8 * rows * columns * 6
+        compiler_params=pltpu.CompilerParams(vmem_limit_bytes=16 << 20),
+        cost_estimate=NO_COST,
+    )(table, *pieces_a, *pieces_b)
+
+
+def place_kernel(widths, table_ref, a_ref, b_ref, *outs):
+    for half, ref in enumerate((a_ref, b_ref)):
+
+        @pl.when(pl.program_id(0) == half)
+        def _(ref=ref):
+            at = 0
+            for width, out in zip(widths, outs):
+                out[...] = ref[:, at : at + width].astype(F32)
+                at += width
+
+
+def place(total_a, total_b, core, widths):
+    rows, columns = total_a.shape
+    block = min(256, rows)
+    last = rows // block - 1
+    table = jnp.stack([core, 1 - core]).astype(jnp.int32)
+    return pl.pallas_call(
+        functools.partial(place_kernel, widths),
+        out_shape=[jax.ShapeDtypeStruct((rows, 2 * width), F32) for width in widths],
+        grid_spec=pltpu.PrefetchScalarGridSpec(
+            num_scalar_prefetch=1,
+            grid=(2, rows // block),
+            in_specs=[
+                pl.BlockSpec((block, columns), lambda h, r, t: (jnp.where(h == 0, r, last), 0)),
+                pl.BlockSpec((block, columns), lambda h, r, t: (jnp.where(h == 1, r, 0), 0)),
+            ],
+            out_specs=[pl.BlockSpec((block, width), lambda h, r, t: (r, t[h])) for width in widths],
         ),
-    )(table, *pieces_a, *pieces_b)
+        compiler_params=pltpu.CompilerParams(vmem_limit_bytes=16 << 20),
+        cost_estimate=NO_COST,
+    )(table, total_a, total_b)
 
 
 def reduce_grads(part_a, part_b, me, core, dp, widths, split):
@@ -200,13 +232,13 @@
 
 def attend_back_kernel(groups, table, *refs):
     raws = refs[:ROWS]
-    grads = refs[ROWS : 2 * ROWS]
-    cosine, sine, q_gain, k_gain, query, key, value, lse = refs[2 * ROWS : 2 * ROWS + 8]
-    out, gains, d_query, d_key, d_value, grad = refs[2 * ROWS + 8 :]
+    grads, others = refs[ROWS : 2 * ROWS], refs[2 * ROWS : 3 * ROWS]
+    cosine, sine, q_gain, k_gain, query, key, value, lse = refs[3 * ROWS : 3 * ROWS + 8]
+    out, gains, d_query, d_key, d_value, grad = refs[3 * ROWS + 8 :]
     width = HEAD_SIZE
     for s in range(ROWS):
         rows = pl.ds(pl.multiple_of(table[s] * BLOCK, BLOCK), BLOCK)
-        grad[rows, :] = grads[s][...]
+        grad[rows, :] = (grads[s][...] + others[s][...].astype(F32)).astype(BF16)
     d_key[...] = jnp.zeros_like(d_key)
     d_value[...] = jnp.zeros_like(d_value)
     for i in range(ROWS):
@@ -243,19 +275,6 @@
     gains[1:2, :] = gain_sums[1]
 
 
-SMEM = pl.BlockSpec(memory_space=pltpu.SMEM)
-VMEM = pl.BlockSpec(memory_space=pltpu.VMEM)
-
-
-def attention_cost(groups, products):
-    area = groups * SEQUENCE_LENGTH * SEQUENCE_LENGTH * 5 // 8
-    return pl.CostEstimate(
-        flops=2 * products * area * HEAD_SIZE + 30 * area,
-        transcendentals=area,
-        bytes_accessed=SEQUENCE_LENGTH * HEAD_SIZE * 4 * (groups + 2) * 3,
-    )
-
-
 def attend(table, raws, cosine, sine, q_gain, k_gain, groups):
     wide = (SEQUENCE_LENGTH, groups * HEAD_SIZE)
     one = (SEQUENCE_LENGTH, HEAD_SIZE)
@@ -270,11 +289,12 @@
         ],
         in_specs=[SMEM] + [VMEM] * (ROWS + 4),
         out_specs=[VMEM] * 5,
-        cost_estimate=attention_cost(groups, 2),
+        compiler_params=pltpu.CompilerParams(vmem_limit_bytes=16 << 20),
+        cost_estimate=NO_COST,
     )(table, *raws, cosine, sine, q_gain[None], k_gain[None])
 
 
-def attend_back(table, raws, grads, cosine, sine, q_gain, k_gain, saved, groups):
+def attend_back(table, raws, grads, others, cosine, sine, q_gain, k_gain, saved, groups):
     query, key, value, lse = saved
     return pl.pallas_call(
         functools.partial(attend_back_kernel, groups),
@@ -282,7 +302,7 @@
             jax.ShapeDtypeStruct((SEQUENCE_LENGTH, (groups + 2) * HEAD_SIZE), BF16),
             jax.ShapeDtypeStruct((2, HEAD_SIZE), F32),
         ],
-        in_specs=[SMEM] + [VMEM] * (2 * ROWS + 8),
+        in_specs=[SMEM] + [VMEM] * (3 * ROWS + 8),
         out_specs=[VMEM] * 2,
         scratch_shapes=[
             pltpu.VMEM((SEQUENCE_LENGTH, groups * HEAD_SIZE), F32),
@@ -290,16 +310,230 @@
             pltpu.VMEM((SEQUENCE_LENGTH, HEAD_SIZE), F32),
             pltpu.VMEM((SEQUENCE_LENGTH, groups * HEAD_SIZE), BF16),
         ],
-        cost_estimate=attention_cost(groups, 5),
-    )(table, *raws, *grads, cosine, sine, q_gain[None], k_gain[None], query, key, value, lse)
-
-
-def own_other(weight, core, axis):
-    half = weight.shape[axis] // 2
-    return (
-        lax.dynamic_slice_in_dim(weight, core * half, half, axis),
-        lax.dynamic_slice_in_dim(weight, (1 - core) * half, half, axis),
-    )
+        compiler_params=pltpu.CompilerParams(vmem_limit_bytes=20 << 20),
+        cost_estimate=NO_COST,
+    )(table, *raws, *grads, *others, cosine, sine, q_gain[None], k_gain[None], query, key, value, lse)
+
+
+def product(kernel, t, ins, outs):
+    return pl.pallas_call(
+        kernel,
+        out_shape=[jax.ShapeDtypeStruct(shape, kind) for shape, kind in outs],
+        in_specs=[SMEM] + [VMEM] * len(ins),
+        out_specs=[VMEM] * len(outs),
+        compiler_params=pltpu.CompilerParams(vmem_limit_bytes=16 << 20),
+        cost_estimate=NO_COST,
+    )(t, *ins)
+
+
+def part(t, other, size, start=0, width=None):
+    return pl.ds(pl.multiple_of(t[2 * ROWS + other] * size + start, 128), width or size)
+
+
+def block_rows(t, s):
+    return pl.ds(pl.multiple_of(t[s] * BLOCK, BLOCK), BLOCK)
+
+
+def head_rows_kernel(t, own, other, q, k, v, x, out):
+    at = 0
+    for weight in (q, k, v):
+        width = weight.shape[1] // 2
+        cols = slice(at, at + width)
+        out[:, cols] = dot(own[...], weight[:, part(t, 0, width)], NN) + dot(
+            other[...], x[:, cols], NN
+        )
+        at += width
+
+
+def head_rows(own, other, weights, x, t):
+    return product(
+        head_rows_kernel, t, (own, other, *weights, x), [((own.shape[0], x.shape[1]), F32)]
+    )[0]
+
+
+def out_rows_kernel(s, t, own, other, weight, out):
+    rows = slice(s * BLOCK, (s + 1) * BLOCK)
+    half = weight.shape[0] // 2
+    total = dot(own[rows, :], weight[part(t, 0, half), :], NN)
+    total += dot(other[rows, :], weight[part(t, 1, half), :], NN)
+    out[...] = total.astype(out.dtype)
+
+
+def out_rows(own, other, weight, s, kind, t):
+    return product(
+        functools.partial(out_rows_kernel, s), t, (own, other, weight),
+        [((BLOCK, weight.shape[1]), kind)],
+    )[0]
+
+
+def g_mixed_kernel(t, own, other, weight, x, out):
+    half = x.shape[0]
+    for s in range(ROWS):
+        rows = block_rows(t, s)
+        total = dot(own[rows, :], weight[part(t, 0, half), :], NT)
+        out[s] = total + dot(other[rows, :], x[...], NT)
+
+
+def g_mixed_rows(own, other, weight, x, t):
+    return product(
+        g_mixed_kernel, t, (own, other, weight, x), [((ROWS, BLOCK, x.shape[0]), F32)]
+    )[0]
+
+
+FF_BLOCK = 256
+
+
+def mlp_kernel(s, t, own, other, gate_weight, up_weight, gate_x, up_x, g_mixed, out):
+    ff = gate_x.shape[1]
+    for start in range(0, ff, FF_BLOCK):
+        cols = slice(start, start + FF_BLOCK)
+        mine = part(t, 0, ff, start, FF_BLOCK)
+        gate = dot(own[...], gate_weight[:, mine], NN) + dot(other[...], gate_x[:, cols], NN)
+        upper = dot(own[...], up_weight[:, mine], NN) + dot(other[...], up_x[:, cols], NN)
+        sigma = 1.0 / (1.0 + jnp.exp(-gate))
+        activ = gate * sigma
+        grad = g_mixed[s, :, cols]
+        out[0, :, cols] = (activ * upper).astype(BF16)
+        out[1, :, cols] = (grad * upper * sigma * (1.0 + gate * (1.0 - sigma))).astype(BF16)
+        out[2, :, cols] = (grad * activ).astype(BF16)
+
+
+def mlp(own, other, gate_weight, up_weight, gate_x, up_x, g_mixed, s, t):
+    return product(
+        functools.partial(mlp_kernel, s), t,
+        (own, other, gate_weight, up_weight, gate_x, up_x, g_mixed),
+        [((3, own.shape[0], gate_x.shape[1]), BF16)],
+    )[0]
+
+
+def mlp_back_kernel(t, own, other, gate_weight, up_weight, out):
+    ff = own.shape[2]
+    mine, theirs = part(t, 0, ff), part(t, 1, ff)
+    for start in range(0, out.shape[1], 256):
+        rows = slice(start, start + 256)
+        total = dot(own[1], gate_weight[rows, mine], NT) + dot(own[2], up_weight[rows, mine], NT)
+        total += dot(other[1], gate_weight[rows, theirs], NT)
+        total += dot(other[2], up_weight[rows, theirs], NT)
+        out[:, rows] = total.astype(out.dtype)
+
+
+def mlp_back(own, other, gate_weight, up_weight, kind, t):
+    return product(
+        mlp_back_kernel, t, (own, other, gate_weight, up_weight),
+        [((own.shape[1], gate_weight.shape[0]), kind)],
+    )[0]
+
+
+def down_rows_kernel(t, weight, *refs):
+    out = refs[-1]
+    half = weight.shape[0] // 2
+    for s in range(ROWS):
+        total = dot(refs[2 * s][0], weight[part(t, 0, half), :], NN)
+        total += dot(refs[2 * s + 1][0], weight[part(t, 1, half), :], NN)
+        out[block_rows(t, s), :] = total.astype(BF16)
+
+
+def down_rows(packs, weight, t):
+    return product(
+        down_rows_kernel, t, (weight, *[p for pair in packs for p in pair]),
+        [((ROWS * BLOCK, weight.shape[1]), BF16)],
+    )[0]
+
+
+def g_heads_kernel(t, x, weight, own, sent):
+    half = weight.shape[0] // 2
+    own[...] = dot(x[...], weight[part(t, 0, half), :], NT)
+    sent[...] = dot(x[...], weight[part(t, 1, half), :], NT).astype(BF16)
+
+
+def g_heads(x, weight, t):
+    shape = (x.shape[0], weight.shape[0] // 2)
+    return product(g_heads_kernel, t, (x, weight), [(shape, F32), (shape, BF16)])
+
+
+def head_back_kernel(s, t, own, other, q, k, v, out):
+    rows = slice(s * BLOCK, (s + 1) * BLOCK)
+    total = 0.0
+    for which, grad in enumerate((own, other)):
+        at = 0
+        for weight in (q, k, v):
+            width = weight.shape[1] // 2
+            total += dot(grad[rows, at : at + width], weight[:, part(t, which, width)], NT)
+            at += width
+    out[...] = total.astype(out.dtype)
+
+
+def head_back(own, other, weights, s, kind, t):
+    return product(
+        functools.partial(head_back_kernel, s), t, (own, other, *weights),
+        [((BLOCK, weights[0].shape[0]), kind)],
+    )[0]
+
+
+def down_grads_kernel(t, *refs):
+    packs, cot, outs = refs[: 2 * ROWS], refs[2 * ROWS], refs[2 * ROWS + 1 :]
+    for which, out in enumerate(outs):
+        for start in range(0, out.shape[0], FF_BLOCK):
+            cols = slice(start, start + FF_BLOCK)
+            total = 0.0
+            for s in range(ROWS):
+                total += dot(packs[2 * s + which][0, :, cols], cot[block_rows(t, s), :], TN)
+            out[cols, :] = total.astype(BF16)
+
+
+def down_grads(packs, cot, t):
+    shape = (packs[0][0].shape[2], cot.shape[1])
+    return product(
+        down_grads_kernel, t, (*[p for pair in packs for p in pair], cot), [(shape, BF16)] * 2
+    )
+
+
+def gu_grads_kernel(t, *refs):
+    packs, rows, outs = refs[: 2 * ROWS], refs[2 * ROWS : 3 * ROWS], refs[3 * ROWS :]
+    ff = packs[0].shape[2]
+    for start in range(0, rows[0].shape[1], 256):
+        cols = slice(start, start + 256)
+        for which, out in enumerate(outs):
+            for part_of in range(2):
+                total = 0.0
+                for s in range(ROWS):
+                    total += dot(rows[s][:, cols], packs[2 * s + which][part_of + 1], TN)
+                out[cols, part_of * ff : (part_of + 1) * ff] = total.astype(BF16)
+
+
+def gu_grads(packs, n2, t):
+    shape = (n2[0].shape[1], 2 * packs[0][0].shape[2])
+    return product(
+        gu_grads_kernel, t, (*[p for pair in packs for p in pair], *n2), [(shape, BF16)] * 2
+    )
+
+
+def out_grads_kernel(t, own, other, *refs):
+    for att, out in ((own, refs[-2]), (other, refs[-1])):
+        total = 0.0
+        for s in range(ROWS):
+            total += dot(att[s * BLOCK : (s + 1) * BLOCK, :], refs[s][...], TN)
+        out[...] = total.astype(BF16)
+
+
+def out_grads(own, other, dmid, t):
+    shape = (own.shape[1], dmid[0].shape[1])
+    return product(out_grads_kernel, t, (own, other, *dmid), [(shape, BF16)] * 2)
+
+
+def head_grads_kernel(t, own, other, *refs):
+    for grad, out in ((own, refs[-2]), (other, refs[-1])):
+        for start in range(0, out.shape[0], 256):
+            cols = slice(start, start + 256)
+            total = 0.0
+            for s in range(ROWS):
+                total += dot(refs[s][:, cols], grad[s * BLOCK : (s + 1) * BLOCK, :], TN)
+            out[cols, :] = total.astype(BF16)
+
+
+def head_grads(own, other, n1, t):
+    shape = (n1[0].shape[1], own.shape[1])
+    return product(head_grads_kernel, t, (own, other, *n1), [(shape, BF16)] * 2)
 
 
 def norm_stats(x):
@@ -317,10 +551,6 @@
 
 def cat(items, axis):
     return jnp.concatenate(items, axis)
-
-
-def after(x, *others):
-    return lax.optimization_barrier((x, *others))[0]
 
 
 def on_device(
@@ -340,117 +570,159 @@
 ):
     dp = lax.axis_size("dp")
     k, core, me = lax.axis_index("row"), lax.axis_index("col"), lax.axis_index("dp")
-    table = jnp.stack([k ^ i for i in range(ROWS)] * 2).astype(jnp.int32)
+    t = jnp.stack([k ^ i for i in range(ROWS)] * 2 + [core, 1 - core]).astype(jnp.int32)
     groups = query_weight.shape[1] // (2 * HEAD_SIZE)
-    cosine, sine = rope_tables()
-
-    q_own, q_oth = own_other(query_weight, core, 1)
-    k_own, k_oth = own_other(key_matrix, core, 1)
-    v_own, v_oth = own_other(value_matrix, core, 1)
-    g_own, g_oth = own_other(gate_weight, core, 1)
-    u_own, u_oth = own_other(up_weight, core, 1)
-    down_own, down_oth = own_other(down_weight, core, 0)
-    out_own, out_oth = own_other(output_weight, core, 0)
-    qkv_own, qkv_oth = cat([q_own, k_own, v_own], 1), cat([q_oth, k_oth, v_oth], 1)
-    gu_own, gu_oth = cat([g_own, u_own], 1), cat([g_oth, u_oth], 1)
+    token = [hidden]
+
+    def step(function, *args):
+        flat, tree = jax.tree.flatten(args)
+        flat = lax.optimization_barrier((*flat, token[0]))[:-1]
+        out = function(*jax.tree.unflatten(tree, flat))
+        token[0] = jax.tree.leaves(out)[0]
+        return out
+
+    def now(x):
+        return after(x, token[0])
+
+    def gather(x, work, between=lambda: None):
+        two, one = row_swap(x, 2), row_swap(x, 1)
+        first = swap(x)
+        token[0] = x
+        done = [work(0, x, first)]
+        between()
+        two = now(two)
+        three = row_swap(two, 1)
+        second = swap(two)
+        token[0] = two
+        one = now(one)
+        done.append(work(1, one, swap(one)))
+        done.append(work(2, two, second))
+        three = now(three)
+        done.append(work(3, three, swap(three)))
+        return [x, one, two, three], done
+
+    def scatter(term, between=lambda: None):
+        part_three = term(3, BF16)
+        got_three = row_swap(part_three, 1)
+        part_one = term(1, BF16)
+        part_two = term(2, F32)
+        got_three = now(got_three)
+        sent = (part_two + got_three.astype(F32)).astype(BF16)
+        token[0] = sent
+        got_two = row_swap(sent, 2)
+        got_one = row_swap(after(part_one, got_three), 1)
+        own = term(0, F32)
+        between()
+        got_one, got_two = now(got_one), now(got_two)
+        return own + got_one.astype(F32) + got_two.astype(F32)
 
     resid = hidden.astype(F32)
     unit_one, factor_one = norm_stats(resid)
-    n1 = gather_slots((unit_one * norm_before).astype(BF16))
-    qkv_full = cat([qkv_own, swap(qkv_oth)], 0)
-    raws = [dot(cat([x, swap(x)], 1), qkv_full, NN) for x in n1]
-    att, lse, query, key, value = attend(table, raws, cosine, sine, query_gain, key_gain, groups)
-
-    cot = gather_slots(after(cotangent, n1[3]))
-    gu_full = cat([gu_own, swap(gu_oth)], 0)
-    down_full = cat([down_own, swap(down_oth)], 1)
-
+    sent_one = (unit_one * norm_before).astype(BF16)
+
+    def for_other(weight, axis):
+        half = weight.shape[axis] // 2
+        return lax.dynamic_slice_in_dim(after(weight, sent_one), (1 - core) * half, half, axis)
+
+    heads = (query_weight, key_matrix, value_matrix)
+    qkv_x = swap(cat([for_other(w, 1) for w in heads], 1))
+    gate_x, up_x = swap(for_other(gate_weight, 1)), swap(for_other(up_weight, 1))
+    down_x = swap(for_other(down_weight, 0))
+    cosine, sine = rope_tables()
+
+    n1, raws = gather(
+        sent_one, lambda s, own, other: step(head_rows, own, other, heads, qkv_x, t)
+    )
+    cot = lax.all_gather(now(cotangent), "row", axis=0, tiled=True)
+    att, lse, query, key, value = step(
+        lambda *a: attend(*a, groups), t, raws, cosine, sine, query_gain, key_gain
+    )
     att_oth = swap(att)
-    att_both = cat([att, att_oth], 1)
-    out_both = cat([out_own, out_oth], 0)
-    parts = [dot(att_both[s * BLOCK : (s + 1) * BLOCK], out_both, NN) for s in range(ROWS)]
-    middle = resid + scatter_slots(*parts)
-
+    middle = resid + scatter(
+        lambda s, kind: step(
+            lambda *a: out_rows(*a[:3], s, kind, a[3]), att, att_oth, output_weight, t
+        )
+    )
+
+    cot = after(cot, middle)
+    cot_x = swap(cot)
     unit_two, factor_two = norm_stats(middle)
-    n2 = gather_slots((unit_two * norm_after).astype(BF16))
-    ff = g_own.shape[1]
-    g_mixed = [dot(cat([x, swap(x)], 1), down_full, NT) for x in cot]
-    mixed, dgu, mixed_oth, dgu_oth = [], [], [], []
-    for s in range(ROWS):
-        both = dot(cat([n2[s], swap(n2[s])], 1), gu_full, NN)
-        gate, upper = both[:, :ff], both[:, ff:]
-        sigma = jax.nn.sigmoid(gate)
-        activ = gate * sigma
-        gm = g_mixed[s]
-        packed = cat(
-            [
-                (activ * upper).astype(BF16),
-                (gm * upper * sigma * (1.0 + gate * (1.0 - sigma))).astype(BF16),
-                (gm * activ).astype(BF16),
-            ],
-            1,
+    sent_two = (unit_two * norm_after).astype(BF16)
+    g_mixed = []
+
+    def hidden_units(s, own, other):
+        if s == 0:
+            g_mixed.append(step(g_mixed_rows, cot, cot_x, down_weight, down_x, t))
+        packed = step(
+            lambda *a: mlp(*a[:7], s, a[7]),
+            own, other, gate_weight, up_weight, gate_x, up_x, g_mixed[0], t,
         )
-        other = swap(packed)
-        mixed.append(packed[:, :ff])
-        dgu.append(packed[:, ff:])
-        mixed_oth.append(other[:, :ff])
-        dgu_oth.append(other[:, ff:])
-    gu_both = cat([gu_own, gu_oth], 1)
-    parts = [dot(cat([dgu[s], dgu_oth[s]], 1), gu_both, NT) for s in range(ROWS)]
-    dsecond = scatter_slots(*parts)
-
-    cot_all = cat(cot, 0)
-    mixed_all, mixed_oth_all = cat(mixed, 0), cat(mixed_oth, 0)
-    (down_grad,) = reduce_grads(
-        dot(mixed_all, cot_all, TN).astype(BF16),
-        dot(mixed_oth_all, cot_all, TN).astype(BF16),
-        me, core, dp, (down_weight.shape[1],), 0,
-    )
-    n2_all = cat(n2, 0)
-    gate_grad, up_grad = reduce_grads(
-        dot(n2_all, cat(dgu, 0), TN).astype(BF16),
-        dot(n2_all, cat(dgu_oth, 0), TN).astype(BF16),
-        me, core, dp, (ff, ff), 1,
-    )
+        return packed, swap(packed)
+
+    n2, packs = gather(sent_two, hidden_units)
+    grads = {}
+
+    def ff_grads():
+        grads["down"] = step(down_grads, packs, cot, t)
+        grads["gu"] = step(gu_grads, packs, n2, t)
+
+    dsecond = scatter(
+        lambda s, kind: step(
+            lambda *a: mlp_back(*a[:4], kind, a[4]), *packs[s], gate_weight, up_weight, t
+        ),
+        ff_grads,
+    )
+    (down_grad,) = reduce_grads(*grads["down"], me, core, dp, (down_weight.shape[1],), 0)
+    ff = gate_x.shape[1]
+    gate_grad, up_grad = place(*lax.psum(tuple(grads["gu"]), "dp"), core, (ff, ff))
 
     dmid_norm, after_part = norm_backward(dsecond, unit_two, factor_two, norm_after)
     dmiddle = cotangent.astype(F32) + dmid_norm
-    dmid = gather_slots(dmiddle.astype(BF16))
-
-    down_both = cat([down_own, down_oth], 0)
-    parts = [dot(cat([mixed[s], mixed_oth[s]], 1), down_both, NN) for s in range(ROWS)]
-    parts[1], parts[3] = after(parts[1], dmid[3]), after(parts[3], dmid[3])
-    layer_out = (middle + scatter_slots(*parts)).astype(BF16)
-
-    datt = [
-        (dot(x, out_own, NT) + swap(dot(x, out_oth, NT).astype(BF16)).astype(F32)).astype(BF16)
-        for x in dmid
-    ]
-    dmid_all = cat(dmid, 0)
-    (output_grad,) = reduce_grads(
-        dot(att, dmid_all, TN).astype(BF16),
-        dot(att_oth, dmid_all, TN).astype(BF16),
-        me, core, dp, (output_weight.shape[1],), 0,
-    )
-    dqkv, gain_parts = attend_back(
-        table, raws, datt, cosine, sine, query_gain, key_gain, (query, key, value, lse), groups
+
+    def g_attended(s, own, other):
+        mine, sent = step(g_heads, own, output_weight, t)
+        return mine, swap(sent)
+
+    width = down_weight.shape[1]
+    last = []
+    dmid, datt = gather(
+        dmiddle.astype(BF16), g_attended,
+        lambda: last.append(step(down_rows, packs, down_weight, t)),
+    )
+    last_sum = lax.psum_scatter(now(last[0]), "row", scatter_dimension=0, tiled=True)
+
+    dqkv, gain_parts = step(
+        lambda *a: attend_back(*a, groups),
+        t, raws, [d for d, _ in datt], [d for _, d in datt],
+        cosine, sine, query_gain, key_gain, (query, key, value, lse),
     )
     dqkv_oth = swap(dqkv)
-    dqkv_both = cat([dqkv, dqkv_oth], 1)
-    qkv_both = cat([qkv_own, qkv_oth], 1)
-    parts = [dot(dqkv_both[s * BLOCK : (s + 1) * BLOCK], qkv_both, NT) for s in range(ROWS)]
-    dfirst = scatter_slots(*parts)
-    n1_all = cat(n1, 0)
+
+    def head_grad():
+        grads["qkv"] = step(head_grads, dqkv, dqkv_oth, n1, t)
+        grads["out"] = step(out_grads, att, att_oth, dmid, t)
+
+    dfirst = scatter(
+        lambda s, kind: step(
+            lambda *a: head_back(*a[:2], a[2:5], s, kind, a[5]), dqkv, dqkv_oth, *heads, t
+        ),
+        head_grad,
+    )
+    layer_out = (middle + last_sum.astype(F32)).astype(BF16)
     query_grad, key_grad, value_grad = reduce_grads(
-        dot(n1_all, dqkv, TN).astype(BF16),
-        dot(n1_all, dqkv_oth, TN).astype(BF16),
-        me, core, dp, (q_own.shape[1], k_own.shape[1], v_own.shape[1]), 1,
-    )
+        *grads["qkv"], me, core, dp, tuple(w.shape[1] // 2 for w in heads), 1
+    )
+    (output_grad,) = reduce_grads(*grads["out"], me, core, dp, (width,), 0)
     dres_norm, before_part = norm_backward(dfirst, unit_one, factor_one, norm_before)
     hidden_grad = dmiddle + dres_norm
 
-    before_grad, after_grad = lax.psum((before_part, after_part), ("dp", "row"))
-    gain_query, gain_key = lax.psum((gain_parts[0], gain_parts[1]), ("dp", "row", "col"))
+    def everywhere(x):
+        return small_sum(small_sum(x, "row", ROWS), "dp", dp)
+
+    early = everywhere(cat([after_part, gain_parts.reshape(-1)], 0))
+    before_grad = everywhere(before_part)
+    after_grad = early[:width]
+    gains = early[width:] + swap(early[width:])
     return (
         layer_out,
         hidden_grad,
@@ -458,8 +730,8 @@
         query_grad,
         key_grad,
         value_grad,
-        gain_query,
-        gain_key,
+        gains[:HEAD_SIZE],
+        gains[HEAD_SIZE:],
         output_grad,
         after_grad,
         gate_grad,

time: 690 us -> 569 us (0.82)
  matrix products: 147 us -> 0 us
  blocking collectives: 79.4 us -> 0 us
  Pallas kernels: 45.1 us -> 108 us
  waiting for transfers between devices: 266 us -> 300 us
  starting transfers between devices: 87.1 us -> 73.9 us
  between operations: 3.01 us -> 15.5 us
  local copies, waits for them, and re-layouts: 29 us -> 38.9 us
    dot_general x44 -> x0, matrix products: 147 us -> none  [dot(): return lax.dot_general(a, b, (dims, ((), ())), preferred_element_type=F32)]
    pallas_call x0 -> x31, Pallas kernels: none -> 81.6 us  [the longest x30 75.5 us: product(): pl.pallas_call(kernel, out_shape=[jax.ShapeDtypeStruct(shape, kind) for s...]
    psum x2 -> x0, blocking collectives: 79.4 us -> none  [the longest x1 41.2 us: on_device(): before_grad, after_grad = lax.psum((before_part, after_part), ('dp', 'row'))]
    ppermute x0 -> x12, waiting for transfers between devices: none -> 20.6 us  [small_sum(): lax.ppermute(x, axis, [(i, i ^ mask) for i in range(size)])]
    ppermute x24 -> x18, waiting for transfers between devices: 164 us -> 146 us  [row_swap(): return lax.ppermute(x, 'row', [(i, i ^ mask) for i in range(ROWS)])]
    unnamed x224 -> x160, local copies, waits for them, and re-layouts: 10.2 us -> 27.3 us
    ppermute x29 -> x28, waiting for transfers between devices: 1.27 us -> 17.6 us  [swap(): return lax.ppermute(x, 'col', [(0, 1), (1, 0)])]
    ppermute x40 -> x30, starting transfers between devices: 47.3 us -> 32.5 us  [dp_swap(): return lax.ppermute(x, 'dp', [(i, i ^ mask) for i in range(dp)])]
  transfers between devices with their start and end apart: 93 -> 91, of which waited for: 31 -> 40; matrix products, arithmetic and copies ran while one was open for 28% -> 5% of each run, Pallas kernels for 5% -> 17%
where the time goes in v2:
time: 569 us; the launch traced here: 563 us
  waiting for transfers between devices  300 us (53%)
  Pallas kernels  108 us (19%)
  starting transfers between devices  73.9 us (13%)
  local copies, waits for them, and re-layouts  38.9 us (7%)
  other arithmetic  26 us (5%)
  between operations  15.5 us (3%)
    ppermute x18, waiting for transfers between devices, row_swap(): return lax.ppermute(x, 'row', [(i, i ^ mask) for i in range(ROWS)])  146 us
    ppermute x30, waiting for transfers between devices, dp_swap(): return lax.ppermute(x, 'dp', [(i, i ^ mask) for i in range(dp)])  116 us
    pallas_call x30, Pallas kernels, product(): pl.pallas_call(kernel, out_shape=[jax.ShapeDtypeStruct(shape, kind) for s...  75.5 us
    ppermute x30, starting transfers between devices, dp_swap(): return lax.ppermute(x, 'dp', [(i, i ^ mask) for i in range(dp)])  32.5 us
    unnamed x160, local copies, waits for them, and re-layouts  27.3 us
    ppermute x18, starting transfers between devices, row_swap(): return lax.ppermute(x, 'row', [(i, i ^ mask) for i in range(ROWS)])  24.1 us
    ppermute x12, waiting for transfers between devices, small_sum(): lax.ppermute(x, axis, [(i, i ^ mask) for i in range(size)])  20.6 us
    ppermute x28, waiting for transfers between devices, swap(): return lax.ppermute(x, 'col', [(0, 1), (1, 0)])  17.6 us
  transfers between devices with their start and end apart: 91, of which 40 were waited for; matrix products, arithmetic and copies ran while one was open for 5% of the time, Pallas kernels for 17%

profile of v2, /device:TPU:0, one launch (start us, length us, event | category | flops | bytes accessed | tf_op | source)
XLA Modules:
  0.0 563.0 jit_solution(16417653487637264934)
XLA Ops:
  13.7 3.9 collective-permute-start.4
  22.3 19.2 %collective-permute-done.4.own.refs_2_ = bf16[256,1024]{1,0:T(8,128)(2,1)} collective-permute-done((bf16[256,1024]{1,0:T(8,128)(2,1)}, bf16[256,1024]{1,0:T(8,128)(2,1)}, u32[]{:S(2)}, u32[]{:S(2)}) %collective-permute-start.4) | collective-permute-done | bytes 524320 | tf_op jit(solution)/shard_map/ppermute | solution.py:33
  49.6 6.7 %collective-permute-done.7.own.refs_3_ = bf16[256,1024]{1,0:T(8,128)(2,1)S(1)} collective-permute-done((bf16[256,1024]{1,0:T(8,128)(2,1)}, bf16[256,1024]{1,0:T(8,128)(2,1)S(1)}, u32[]{:S(2)}, u32[]{:S(2)}) %collective-permute-start.7) | collective-permute-done | bytes 524320 | tf_op jit(solution)/shard_map/ppermute | solution.py:33
  65.5 5.6 %shard_map.232 = (bf16[1024,256]{1,0:T(8,128)(2,1)S(1)}, f32[1024,256]{1,0:T(8,128)S(1)}, bf16[1024,256]{1,0:T(8,128)(2,1)S(1)}, bf16[1024,128]{1,0:T(8,128)(2,1)S(1)}, bf16[1024,128]{1,0:T(8,128)(2,1)S(1)}) custom-call(s32[10]{0:T(128)S(1)} %stack.101.t.table, f32[256,512]{1,0:T(8,128)S(1)} %copy-done.15, f32[256,512]{1,0:T(8,128)S(1)} %copy-done.18, ...), custom_call_target="tpu_custom_call" | custom-call | flops 1 | bytes 1 | tf_op jit(solution)/shard_map/pallas_call | solution.py:281
  77.7 37.4 %collective-permute-done.10 = bf16[256,1024]{1,0:T(8,128)(2,1)S(1)} collective-permute-done((bf16[256,1024]{1,0:T(8,128)(2,1)S(1)}, bf16[256,1024]{1,0:T(8,128)(2,1)S(1)}, u32[]{:S(2)}, u32[]{:S(2)}) %collective-permute-start.10) | collective-permute-done | bytes 524320 | tf_op jit(solution)/shard_map/ppermute | solution.py:33
  115.7 2.5 collective-permute-start.11
  119.1 22.3 %collective-permute-done.12 = bf16[256,1024]{1,0:T(8,128)(2,1)S(1)} collective-permute-done((bf16[256,1024]{1,0:T(8,128)(2,1)S(1)}, bf16[256,1024]{1,0:T(8,128)(2,1)S(1)}, u32[]{:S(2)}, u32[]{:S(2)}) %collective-permute-start.12) | collective-permute-done | bytes 524320 | tf_op jit(solution)/shard_map/ppermute | solution.py:33
  147.2 6.6 %collective-permute-done.13 = f32[256]{0:T(256)S(1)} collective-permute-done((f32[256]{0:T(256)S(1)}, f32[256]{0:T(256)S(1)}, u32[]{:S(2)}, u32[]{:S(2)}) %collective-permute-start.13) | collective-permute-done | bytes 1056 | tf_op jit(solution)/shard_map/ppermute | solution.py:29
  157.8 5.5 shard_map.237.g_mixed
  163.4 2.6 shard_map.238.own.refs_0_
  166.0 13.5 %collective-permute-done.21.own.refs_10_ = bf16[256,1024]{1,0:T(8,128)(2,1)S(1)} collective-permute-done((bf16[256,1024]{1,0:T(8,128)(2,1)S(1)}, bf16[256,1024]{1,0:T(8,128)(2,1)S(1)}, u32[]{:S(2)}, u32[]{:S(2)}) %collective-permute-start.21) | collective-permute-done | bytes 524320 | tf_op jit(solution)/shard_map/ppermute | solution.py:33
  182.5 2.6 shard_map.239.own.refs_2_
  185.2 2.6 shard_map.240.own.refs_4_
  187.8 7.1 %collective-permute-done.26.own.refs_11_ = bf16[256,1024]{1,0:T(8,128)(2,1)S(1)} collective-permute-done((bf16[256,1024]{1,0:T(8,128)(2,1)S(1)}, bf16[256,1024]{1,0:T(8,128)(2,1)S(1)}, u32[]{:S(2)}, u32[]{:S(2)}) %collective-permute-start.26) | collective-permute-done | bytes 524320 | tf_op jit(solution)/shard_map/ppermute | solution.py:33
  196.9 2.6 shard_map.241.own.refs_6_
  209.9 8.9 %collective-permute-done.29 = bf16[256,1024]{1,0:T(8,128)(2,1)S(1)} collective-permute-done((bf16[256,1024]{1,0:T(8,128)(2,1)S(1)}, bf16[256,1024]{1,0:T(8,128)(2,1)S(1)}, u32[]{:S(2)}, u32[]{:S(2)}) %collective-permute-start.29) | collective-permute-done | bytes 524320 | tf_op jit(solution)/shard_map/ppermute | solution.py:33
  221.1 2.5 shard_map.245
  223.6 4.0 shard_map.246
  229.9 7.4 %shard_map.247 = (bf16[1024,1536]{1,0:T(8,128)(2,1)S(1)}, bf16[1024,1536]{1,0:T(8,128)(2,1)S(1)}) custom-call(s32[10]{0:T(128)S(1)} %stack.101.t.table, bf16[3,256,768]{2,1,0:T(8,128)(2,1)S(1)} %shard_map.238.own.refs_0_, bf16[3,256,768]{2,1,0:T(8,128)(2,1)S(1)} %collective-permute-done.19.other.refs_1_, bf16[3,256,768]{2,1,0:T(8,128)(2,1)S(1)} %shard_map.239.own.refs_2_, ...), custom_call_target="tpu_custom_call" | custom-call | flops 1 | bytes 1 | tf_op jit(solution)/shard_map/pallas_call | solution.py:319
  239.0 5.1 collective-permute-done.31
  252.4 4.2 shard_map.249
  258.0 15.6 %collective-permute-done.33.x.refs_2_ = bf16[256,1024]{1,0:T(8,128)(2,1)} collective-permute-done((bf16[256,1024]{1,0:T(8,128)(2,1)}, bf16[256,1024]{1,0:T(8,128)(2,1)}, u32[]{:S(2)}, u32[]{:S(2)}) %collective-permute-start.33) | collective-permute-done | bytes 524320 | tf_op jit(solution)/shard_map/ppermute | solution.py:33
  278.9 8.7 %collective-permute-done.34.x.refs_3_ = bf16[256,1024]{1,0:T(8,128)(2,1)S(1)} collective-permute-done((bf16[256,1024]{1,0:T(8,128)(2,1)}, bf16[256,1024]{1,0:T(8,128)(2,1)S(1)}, u32[]{:S(2)}, u32[]{:S(2)}) %collective-permute-start.34) | collective-permute-done | bytes 524320 | tf_op jit(solution)/shard_map/ppermute | solution.py:33
  298.1 12.9 %collective-permute-done.78 = bf16[384,1024]{1,0:T(8,128)(2,1)} collective-permute-done((bf16[384,1024]{1,0:T(8,128)(2,1)}, bf16[384,1024]{1,0:T(8,128)(2,1)}, u32[]{:S(2)}, u32[]{:S(2)}) %collective-permute-start.78) | collective-permute-done | bytes 786464 | tf_op jit(solution)/shard_map/ppermute | solution.py:41
  322.6 7.3 %shard_map.253 = (bf16[1024,512]{1,0:T(8,128)(2,1)S(1)}, f32[2,128]{1,0:T(2,128)S(1)}) custom-call(s32[10]{0:T(128)S(1)} %stack.101.t.table, f32[256,512]{1,0:T(8,128)S(1)} %copy-done.16, f32[256,512]{1,0:T(8,128)S(1)} %copy-done.19, f32[256,512]{1,0:T(8,128)S(1)} %copy-done.22, f32[256,512]{1,0:T(8,128)S(1)} %copy-done.25, f32[256,256]{1,0:T(8,128)S(1)} %copy-done.48, ...), custom_call_target="tpu_custom_call" | custom-call | flops 1 | bytes 1 | tf_op jit(solution)/shard_map/pallas_call | solution.py:299
  337.6 5.0 collective-permute-done.84
  350.8 3.2 shard_map.254
  355.4 10.3 %collective-permute-done.66 = f32[1280]{0:T(1024)} collective-permute-done((f32[1280]{0:T(1024)}, f32[1280]{0:T(1024)}, u32[]{:S(2)}, u32[]{:S(2)}) %collective-permute-start.66) | collective-permute-done | bytes 5152 | tf_op jit(solution)/shard_map/ppermute | solution.py:45
  375.3 13.8 %collective-permute-done.81.refs_2_ = bf16[192,1024]{1,0:T(8,128)(2,1)S(1)} collective-permute-done((bf16[192,1024]{1,0:T(8,128)(2,1)S(1)}, bf16[192,1024]{1,0:T(8,128)(2,1)S(1)}, u32[]{:S(2)}, u32[]{:S(2)}) %collective-permute-start.81) | collective-permute-done | bytes 393248 | tf_op jit(solution)/shard_map/ppermute | solution.py:41
  389.2 14.5 %collective-permute-done.82.refs_3_ = bf16[192,1024]{1,0:T(8,128)(2,1)S(1)} collective-permute-done((bf16[192,1024]{1,0:T(8,128)(2,1)}, bf16[192,1024]{1,0:T(8,128)(2,1)S(1)}, u32[]{:S(2)}, u32[]{:S(2)}) %collective-permute-start.82) | collective-permute-done | bytes 393248 | tf_op jit(solution)/shard_map/ppermute | solution.py:41
  403.7 6.1 %shard_map.263 = f32[1536,1024]{1,0:T(8,128)} custom-call(s32[10]{0:T(128)S(1)} %stack.119.table_ref, bf16[192,1024]{1,0:T(8,128)(2,1)S(1)} %add_convert_fusion.9.refs_0_, bf16[192,1024]{1,0:T(8,128)(2,1)} %collective-permute-done.80.refs_1_, bf16[192,1024]{1,0:T(8,128)(2,1)S(1)} %collective-permute-done.81.refs_2_, ...), custom_call_target="tpu_custom_call" | custom-call | flops 1 | bytes 1 | tf_op jit(solution)/shard_map/pallas_call | solution.py:104
  409.8 2.5 shard_map.255
  415.8 2.5 collective-permute-start.43
  420.5 4.2 shard_map.258
  426.3 2.7 shard_map.259
  432.8 5.4 collective-permute-done.68
  439.9 22.1 %collective-permute-done.73 = bf16[128,1024]{1,0:T(8,128)(2,1)S(1)} collective-permute-done((bf16[128,1024]{1,0:T(8,128)(2,1)S(1)}, bf16[128,1024]{1,0:T(8,128)(2,1)S(1)}, u32[]{:S(2)}, u32[]{:S(2)}) %collective-permute-start.73) | collective-permute-done | bytes 262176 | tf_op jit(solution)/shard_map/ppermute | solution.py:41
  461.9 2.5 collective-permute-start.69
  464.5 4.7 collective-permute-done.69
  469.3 6.3 %collective-permute-done.74 = bf16[64,1024]{1,0:T(8,128)(2,1)S(1)} collective-permute-done((bf16[64,1024]{1,0:T(8,128)(2,1)S(1)}, bf16[64,1024]{1,0:T(8,128)(2,1)S(1)}, u32[]{:S(2)}, u32[]{:S(2)}) %collective-permute-start.74) | collective-permute-done | bytes 131104 | tf_op jit(solution)/shard_map/ppermute | solution.py:41
  481.0 12.4 %collective-permute-done.52 = bf16[256,512]{1,0:T(8,128)(2,1)S(1)} collective-permute-done((bf16[256,512]{1,0:T(8,128)(2,1)S(1)}, bf16[256,512]{1,0:T(8,128)(2,1)S(1)}, u32[]{:S(2)}, u32[]{:S(2)}) %collective-permute-start.52) | collective-permute-done | bytes 262176 | tf_op jit(solution)/shard_map/ppermute | solution.py:41
  495.9 2.8 collective-permute-done.47
  500.2 4.1 collective-permute-done.75.refs_5_
  507.8 7.1 %collective-permute-done.49 = f32[1024]{0:T(1024)S(1)} collective-permute-done((f32[1024]{0:T(1024)S(1)}, f32[1024]{0:T(1024)S(1)}, u32[]{:S(2)}, u32[]{:S(2)}) %collective-permute-start.49) | collective-permute-done | bytes 4128 | tf_op jit(solution)/shard_map/ppermute | solution.py:45
  525.0 11.3 %collective-permute-done.77.refs_7_ = bf16[64,1024]{1,0:T(8,128)(2,1)S(1)} collective-permute-done((bf16[64,1024]{1,0:T(8,128)(2,1)S(1)}, bf16[64,1024]{1,0:T(8,128)(2,1)S(1)}, u32[]{:S(2)}, u32[]{:S(2)}) %collective-permute-start.77) | collective-permute-done | bytes 131104 | tf_op jit(solution)/shard_map/ppermute | solution.py:41
  536.4 3.7 shard_map.261
  540.0 4.2 shard_map.260
  550.0 6.0 %shard_map.262 = (f32[1024,1536]{1,0:T(8,128)}, f32[1024,1536]{1,0:T(8,128)}) custom-call(s32[2]{0:T(128)S(1)} %pad_add_fusion.table_ref, bf16[1024,1536]{1,0:T(8,128)(2,1)S(1)} %copy-done.32, bf16[1024,1536]{1,0:T(8,128)(2,1)S(1)} %copy-done.33), custom_call_target="tpu_custom_call" | custom-call | flops 1 | bytes 1 | tf_op jit(solution)/shard_map/pallas_call | solution.py:137
  (396 shorter events, 172.7 us)
Async XLA Ops:
  7.2 135.4 %all-gather.2.cloned.1.call-start = ((), (), s32[]{:S(2)}) async-start(), calls=%async_computation.1 | async-start | bytes 2621440 | tf_op jit(solution)/shard_map/all_gather | solution.py:636
  13.7 27.8 %collective-permute-start.4 = (bf16[256,1024]{1,0:T(8,128)(2,1)}, bf16[256,1024]{1,0:T(8,128)(2,1)}, u32[]{:S(2)}, u32[]{:S(2)}) collective-permute-start(bf16[256,1024]{1,0:T(8,128)(2,1)} %fusion.4.own.refs_0_), channel_id=1, source_target_pairs={{0,4},{2,6},{4,0},{6,2},{1,5},{3,7},{5,1},{7,3},{8,12},{10,14},{12... | collective-permute-start | bytes 1572872 | tf_op jit(solution)/shard_map/ppermute | solution.py:33
  17.6 24.1 %collective-permute-start.3 = (bf16[256,1024]{1,0:T(8,128)(2,1)}, bf16[256,1024]{1,0:T(8,128)(2,1)}, u32[]{:S(2)}, u32[]{:S(2)}) collective-permute-start(bf16[256,1024]{1,0:T(8,128)(2,1)} %fusion.4.own.refs_0_), channel_id=1, source_target_pairs={{0,2},{2,0},{4,6},{6,4},{1,3},{3,1},{5,7},{7,5},{8,10},{10,8},{12,... | collective-permute-start | bytes 1572872 | tf_op jit(solution)/shard_map/ppermute | solution.py:33
  61.4 482.9 %reduce-scatter.2.cloned.1.call-start = ((), (), s32[]{:S(2)}) async-start(), calls=%async_computation.2 | async-start | bytes 2621440 | tf_op jit(solution)/shard_map/reduce_scatter | solution.py:692
  74.2 40.9 %collective-permute-start.10 = (bf16[256,1024]{1,0:T(8,128)(2,1)S(1)}, bf16[256,1024]{1,0:T(8,128)(2,1)S(1)}, u32[]{:S(2)}, u32[]{:S(2)}) collective-permute-start(bf16[256,1024]{1,0:T(8,128)(2,1)S(1)} %shard_map.233), channel_id=1, source_target_pairs={{0,2},{2,0},{4,6},{6,4},{1,3},{3,1},{5,7},{7,5},{8,10},{10,8},{12,... | collective-permute-start | bytes 1572872 | tf_op jit(solution)/shard_map/ppermute | solution.py:33
  115.3 26.1 %collective-permute-start.12 = (bf16[256,1024]{1,0:T(8,128)(2,1)S(1)}, bf16[256,1024]{1,0:T(8,128)(2,1)S(1)}, u32[]{:S(2)}, u32[]{:S(2)}) collective-permute-start(bf16[256,1024]{1,0:T(8,128)(2,1)S(1)} %add_convert_fusion.7), channel_id=1, source_target_pairs={{0,4},{2,6},{4,0},{6,2},{1,5},{3,7},{5,1},{7,3},{8,12},{10,14},{12... | collective-permute-start | bytes 1572872 | tf_op jit(solution)/shard_map/ppermute | solution.py:33
  115.7 25.7 %collective-permute-start.11 = (bf16[256,1024]{1,0:T(8,128)(2,1)S(1)}, bf16[256,1024]{1,0:T(8,128)(2,1)S(1)}, u32[]{:S(2)}, u32[]{:S(2)}) collective-permute-start(bf16[256,1024]{1,0:T(8,128)(2,1)S(1)} %shard_map.234), channel_id=1, source_target_pairs={{0,2},{2,0},{4,6},{6,4},{1,3},{3,1},{5,7},{7,5},{8,10},{10,8},{12,... | collective-permute-start | bytes 1572872 | tf_op jit(solution)/shard_map/ppermute | solution.py:33
  145.1 18.2 %collective-permute-start.15 = (bf16[1024,768]{1,0:T(8,128)(2,1)S(1)}, bf16[1024,768]{1,0:T(8,128)(2,1)S(1)}, u32[]{:S(2)}, u32[]{:S(2)}) collective-permute-start(bf16[1024,768]{1,0:T(8,128)(2,1)S(1)} %constant_dynamic-slice_fusion.14), channel_id=1, source_target_pairs={{0,1},{1,0},{2,3},{3,2},{4,5},{5,4},{6,7},{7,6},{8,9},{9,8},{10,11... | collective-permute-start | bytes 4718600 | tf_op jit(solution)/shard_map/ppermute | solution.py:29
  146.5 16.8 %collective-permute-start.16 = (bf16[1024,768]{1,0:T(8,128)(2,1)S(1)}, bf16[1024,768]{1,0:T(8,128)(2,1)S(1)}, u32[]{:S(2)}, u32[]{:S(2)}) collective-permute-start(bf16[1024,768]{1,0:T(8,128)(2,1)S(1)} %constant_dynamic-slice_fusion.13), channel_id=1, source_target_pairs={{0,1},{1,0},{2,3},{3,2},{4,5},{5,4},{6,7},{7,6},{8,9},{9,8},{10,11... | collective-permute-start | bytes 4718600 | tf_op jit(solution)/shard_map/ppermute | solution.py:29
  154.1 25.4 %collective-permute-start.21 = (bf16[256,1024]{1,0:T(8,128)(2,1)S(1)}, bf16[256,1024]{1,0:T(8,128)(2,1)S(1)}, u32[]{:S(2)}, u32[]{:S(2)}) collective-permute-start(bf16[256,1024]{1,0:T(8,128)(2,1)S(1)} %multiply_convert_fusion.own.refs_8_), channel_id=1, source_target_pairs={{0,4},{2,6},{4,0},{6,2},{1,5},{3,7},{5,1},{7,3},{8,12},{10,14},{12... | collective-permute-start | bytes 1572872 | tf_op jit(solution)/shard_map/ppermute | solution.py:33
  155.4 25.2 %collective-permute-start.20 = (bf16[256,1024]{1,0:T(8,128)(2,1)S(1)}, bf16[256,1024]{1,0:T(8,128)(2,1)S(1)}, u32[]{:S(2)}, u32[]{:S(2)}) collective-permute-start(bf16[256,1024]{1,0:T(8,128)(2,1)S(1)} %multiply_convert_fusion.own.refs_8_), channel_id=1, source_target_pairs={{0,2},{2,0},{4,6},{6,4},{1,3},{3,1},{5,7},{7,5},{8,10},{10,8},{12,... | collective-permute-start | bytes 1572872 | tf_op jit(solution)/shard_map/ppermute | solution.py:33
  204.8 14.0 %collective-permute-start.29 = (bf16[256,1024]{1,0:T(8,128)(2,1)S(1)}, bf16[256,1024]{1,0:T(8,128)(2,1)S(1)}, u32[]{:S(2)}, u32[]{:S(2)}) collective-permute-start(bf16[256,1024]{1,0:T(8,128)(2,1)S(1)} %shard_map.242), channel_id=1, source_target_pairs={{0,2},{2,0},{4,6},{6,4},{1,3},{3,1},{5,7},{7,5},{8,10},{10,8},{12,... | collective-permute-start | bytes 1572872 | tf_op jit(solution)/shard_map/ppermute | solution.py:33
  205.2 15.9 %collective-permute-start.19 = (bf16[3,256,768]{2,1,0:T(8,128)(2,1)S(1)}, bf16[3,256,768]{2,1,0:T(8,128)(2,1)S(1)}, u32[]{:S(2)}, u32[]{:S(2)}) collective-permute-start(bf16[3,256,768]{2,1,0:T(8,128)(2,1)S(1)} %shard_map.238.own.refs_0_), channel_id=1, source_target_pairs={{0,1},{1,0},{2,3},{3,2},{4,5},{5,4},{6,7},{7,6},{8,9},{9,8},{10,11... | collective-permute-start | bytes 3538952 | tf_op jit(solution)/shard_map/ppermute | solution.py:29
  219.0 25.1 %collective-permute-start.31 = (bf16[256,1024]{1,0:T(8,128)(2,1)S(1)}, bf16[256,1024]{1,0:T(8,128)(2,1)S(1)}, u32[]{:S(2)}, u32[]{:S(2)}) collective-permute-start(bf16[256,1024]{1,0:T(8,128)(2,1)S(1)} %add_convert_fusion.6), channel_id=1, source_target_pairs={{0,4},{2,6},{4,0},{6,2},{1,5},{3,7},{5,1},{7,3},{8,12},{10,14},{12... | collective-permute-start | bytes 1572872 | tf_op jit(solution)/shard_map/ppermute | solution.py:33
  219.3 24.8 %collective-permute-start.30 = (bf16[256,1024]{1,0:T(8,128)(2,1)S(1)}, bf16[256,1024]{1,0:T(8,128)(2,1)S(1)}, u32[]{:S(2)}, u32[]{:S(2)}) collective-permute-start(bf16[256,1024]{1,0:T(8,128)(2,1)S(1)} %shard_map.243), channel_id=1, source_target_pairs={{0,2},{2,0},{4,6},{6,4},{1,3},{3,1},{5,7},{7,5},{8,10},{10,8},{12,... | collective-permute-start | bytes 1572872 | tf_op jit(solution)/shard_map/ppermute | solution.py:33
  247.9 25.7 %collective-permute-start.33 = (bf16[256,1024]{1,0:T(8,128)(2,1)}, bf16[256,1024]{1,0:T(8,128)(2,1)}, u32[]{:S(2)}, u32[]{:S(2)}) collective-permute-start(bf16[256,1024]{1,0:T(8,128)(2,1)} %get-tuple-element.540.x.refs_0_), channel_id=1, source_target_pairs={{0,4},{2,6},{4,0},{6,2},{1,5},{3,7},{5,1},{7,3},{8,12},{10,14},{12... | collective-permute-start | bytes 1572872 | tf_op jit(solution)/shard_map/ppermute | solution.py:33
  248.5 25.3 %collective-permute-start.35 = (bf16[256,1024]{1,0:T(8,128)(2,1)}, bf16[256,1024]{1,0:T(8,128)(2,1)}, u32[]{:S(2)}, u32[]{:S(2)}) collective-permute-start(bf16[256,1024]{1,0:T(8,128)(2,1)} %get-tuple-element.540.x.refs_0_), channel_id=1, source_target_pairs={{0,2},{2,0},{4,6},{6,4},{1,3},{3,1},{5,7},{7,5},{8,10},{10,8},{12,... | collective-permute-start | bytes 1572872 | tf_op jit(solution)/shard_map/ppermute | solution.py:33
  290.0 256.3 %all-reduce.3.cloned.1.call-start = ((), (), s32[]{:S(2)}) async-start(), calls=%async_computation.3 | async-start | bytes 12582912 | tf_op jit(solution)/shard_map/psum | solution.py:677
  292.1 18.9 %collective-permute-start.78 = (bf16[384,1024]{1,0:T(8,128)(2,1)}, bf16[384,1024]{1,0:T(8,128)(2,1)}, u32[]{:S(2)}, u32[]{:S(2)}) collective-permute-start(bf16[384,1024]{1,0:T(8,128)(2,1)} %constant_dynamic-slice_fusion.3), channel_id=1, source_target_pairs={{0,8},{8,0},{16,24},{24,16},{1,9},{9,1},{17,25},{25,17},{2,10},{10... | collective-permute-start | bytes 2359304 | tf_op jit(solution)/shard_map/ppermute | solution.py:41
  295.8 20.0 %collective-permute-start.83 = (bf16[384,1024]{1,0:T(8,128)(2,1)}, bf16[384,1024]{1,0:T(8,128)(2,1)}, u32[]{:S(2)}, u32[]{:S(2)}) collective-permute-start(bf16[384,1024]{1,0:T(8,128)(2,1)} %constant_dynamic-slice_fusion.1), channel_id=1, source_target_pairs={{0,16},{8,24},{16,0},{24,8},{1,17},{9,25},{17,1},{25,9},{2,18},{10... | collective-permute-start | bytes 2359304 | tf_op jit(solution)/shard_map/ppermute | solution.py:41
  298.1 19.2 %collective-permute-start.36 = (bf16[256,256]{1,0:T(8,128)(2,1)S(1)}, bf16[256,256]{1,0:T(8,128)(2,1)S(1)}, u32[]{:S(2)}, u32[]{:S(2)}) collective-permute-start(bf16[256,256]{1,0:T(8,128)(2,1)S(1)} %copy-done.58), channel_id=1, source_target_pairs={{0,1},{1,0},{2,3},{3,2},{4,5},{5,4},{6,7},{7,6},{8,9},{9,8},{10,11... | collective-permute-start | bytes 393224 | tf_op jit(solution)/shard_map/ppermute | solution.py:29
  313.7 19.1 %collective-permute-start.79 = (bf16[192,1024]{1,0:T(8,128)(2,1)}, bf16[192,1024]{1,0:T(8,128)(2,1)}, u32[]{:S(2)}, u32[]{:S(2)}) collective-permute-start(bf16[192,1024]{1,0:T(8,128)(2,1)} %constant_dynamic-slice_fusion.2), channel_id=1, source_target_pairs={{0,16},{8,24},{16,0},{24,8},{1,17},{9,25},{17,1},{25,9},{2,18},{10... | collective-permute-start | bytes 1179656 | tf_op jit(solution)/shard_map/ppermute | solution.py:41
  329.9 19.9 %collective-permute-start.40 = (bf16[1024,512]{1,0:T(8,128)(2,1)S(1)}, bf16[1024,512]{1,0:T(8,128)(2,1)}, u32[]{:S(2)}, u32[]{:S(2)}) collective-permute-start(bf16[1024,512]{1,0:T(8,128)(2,1)S(1)} %get-tuple-element.530.own), channel_id=1, source_target_pairs={{0,1},{1,0},{2,3},{3,2},{4,5},{5,4},{6,7},{7,6},{8,9},{9,8},{10,11... | collective-permute-start | bytes 3145736 | tf_op jit(solution)/shard_map/ppermute | solution.py:29
  334.0 37.5 %collective-permute-start.80 = (bf16[192,1024]{1,0:T(8,128)(2,1)S(1)}, bf16[192,1024]{1,0:T(8,128)(2,1)}, u32[]{:S(2)}, u32[]{:S(2)}) collective-permute-start(bf16[192,1024]{1,0:T(8,128)(2,1)S(1)} %add_convert_fusion.9.refs_0_), channel_id=1, source_target_pairs={{0,16},{8,24},{16,0},{24,8},{1,17},{9,25},{17,1},{25,9},{2,18},{10... | collective-permute-start | bytes 1179656 | tf_op jit(solution)/shard_map/ppermute | solution.py:41
  345.2 27.5 %collective-permute-start.85 = (bf16[192,1024]{1,0:T(8,128)(2,1)}, bf16[192,1024]{1,0:T(8,128)(2,1)}, u32[]{:S(2)}, u32[]{:S(2)}) collective-permute-start(bf16[192,1024]{1,0:T(8,128)(2,1)} %add_convert_fusion.8.refs_4_), channel_id=1, source_target_pairs={{0,8},{8,0},{16,24},{24,16},{1,9},{9,1},{17,25},{25,17},{2,10},{10... | collective-permute-start | bytes 1179656 | tf_op jit(solution)/shard_map/ppermute | solution.py:41
  348.1 17.6 %collective-permute-start.66 = (f32[1280]{0:T(1024)}, f32[1280]{0:T(1024)}, u32[]{:S(2)}, u32[]{:S(2)}) collective-permute-start(f32[1280]{0:T(1024)} %add_add_fusion.1), channel_id=1, source_target_pairs={{0,24},{8,16},{16,8},{24,0},{1,25},{9,17},{17,9},{25,1},{2,26},{10... | collective-permute-start | bytes 15368 | tf_op jit(solution)/shard_map/ppermute | solution.py:45
  349.8 16.3 %collective-permute-start.64 = (f32[1280]{0:T(1024)}, f32[1280]{0:T(1024)}, u32[]{:S(2)}, u32[]{:S(2)}) collective-permute-start(f32[1280]{0:T(1024)} %add_add_fusion.1), channel_id=1, source_target_pairs={{0,8},{8,0},{16,24},{24,16},{1,9},{9,1},{17,25},{25,17},{2,10},{10... | collective-permute-start | bytes 15368 | tf_op jit(solution)/shard_map/ppermute | solution.py:45
  354.0 60.6 %collective-permute-start.41 = (bf16[256,1024]{1,0:T(8,128)(2,1)}, bf16[256,1024]{1,0:T(8,128)(2,1)}, u32[]{:S(2)}, u32[]{:S(2)}) collective-permute-start(bf16[256,1024]{1,0:T(8,128)(2,1)} %shard_map.254), channel_id=1, source_target_pairs={{0,2},{2,0},{4,6},{6,4},{1,3},{3,1},{5,7},{7,5},{8,10},{10,8},{12,... | collective-permute-start | bytes 1572872 | tf_op jit(solution)/shard_map/ppermute | solution.py:33
  368.8 20.4 %collective-permute-start.81 = (bf16[192,1024]{1,0:T(8,128)(2,1)S(1)}, bf16[192,1024]{1,0:T(8,128)(2,1)S(1)}, u32[]{:S(2)}, u32[]{:S(2)}) collective-permute-start(bf16[192,1024]{1,0:T(8,128)(2,1)S(1)} %add_convert_fusion.9.refs_0_), channel_id=1, source_target_pairs={{0,8},{8,0},{16,24},{24,16},{1,9},{9,1},{17,25},{25,17},{2,10},{10... | collective-permute-start | bytes 1179656 | tf_op jit(solution)/shard_map/ppermute | solution.py:41
  371.5 17.7 %collective-permute-start.86 = (bf16[192,1024]{1,0:T(8,128)(2,1)}, bf16[192,1024]{1,0:T(8,128)(2,1)S(1)}, u32[]{:S(2)}, u32[]{:S(2)}) collective-permute-start(bf16[192,1024]{1,0:T(8,128)(2,1)} %add_convert_fusion.8.refs_4_), channel_id=1, source_target_pairs={{0,16},{8,24},{16,0},{24,8},{1,17},{9,25},{17,1},{25,9},{2,18},{10... | collective-permute-start | bytes 1179656 | tf_op jit(solution)/shard_map/ppermute | solution.py:41
  372.7 31.0 %collective-permute-start.82 = (bf16[192,1024]{1,0:T(8,128)(2,1)}, bf16[192,1024]{1,0:T(8,128)(2,1)S(1)}, u32[]{:S(2)}, u32[]{:S(2)}) collective-permute-start(bf16[192,1024]{1,0:T(8,128)(2,1)} %collective-permute-done.80.refs_1_), channel_id=1, source_target_pairs={{0,8},{8,0},{16,24},{24,16},{1,9},{9,1},{17,25},{25,17},{2,10},{10... | collective-permute-start | bytes 1179656 | tf_op jit(solution)/shard_map/ppermute | solution.py:41
  373.3 30.4 %collective-permute-start.87 = (bf16[192,1024]{1,0:T(8,128)(2,1)}, bf16[192,1024]{1,0:T(8,128)(2,1)S(1)}, u32[]{:S(2)}, u32[]{:S(2)}) collective-permute-start(bf16[192,1024]{1,0:T(8,128)(2,1)} %collective-permute-done.85.refs_5_), channel_id=1, source_target_pairs={{0,16},{8,24},{16,0},{24,8},{1,17},{9,25},{17,1},{25,9},{2,18},{10... | collective-permute-start | bytes 1179656 | tf_op jit(solution)/shard_map/ppermute | solution.py:41
  415.8 62.5 %collective-permute-start.43 = (bf16[256,1024]{1,0:T(8,128)(2,1)S(1)}, bf16[256,1024]{1,0:T(8,128)(2,1)S(1)}, u32[]{:S(2)}, u32[]{:S(2)}) collective-permute-start(bf16[256,1024]{1,0:T(8,128)(2,1)S(1)} %add_convert_fusion.4), channel_id=1, source_target_pairs={{0,4},{2,6},{4,0},{6,2},{1,5},{3,7},{5,1},{7,3},{8,12},{10,14},{12... | collective-permute-start | bytes 1572872 | tf_op jit(solution)/shard_map/ppermute | solution.py:33
  424.7 53.6 %collective-permute-start.42 = (bf16[256,1024]{1,0:T(8,128)(2,1)S(1)}, bf16[256,1024]{1,0:T(8,128)(2,1)S(1)}, u32[]{:S(2)}, u32[]{:S(2)}) collective-permute-start(bf16[256,1024]{1,0:T(8,128)(2,1)S(1)} %shard_map.255), channel_id=1, source_target_pairs={{0,2},{2,0},{4,6},{6,4},{1,3},{3,1},{5,7},{7,5},{8,10},{10,8},{12,... | collective-permute-start | bytes 1572872 | tf_op jit(solution)/shard_map/ppermute | solution.py:33
  429.3 47.8 %collective-permute-start.51 = (bf16[512,512]{1,0:T(8,128)(2,1)S(1)}, bf16[512,512]{1,0:T(8,128)(2,1)S(1)}, u32[]{:S(2)}, u32[]{:S(2)}) collective-permute-start(bf16[512,512]{1,0:T(8,128)(2,1)S(1)} %constant_dynamic-slice_fusion.11), channel_id=1, source_target_pairs={{0,8},{8,0},{16,24},{24,16},{1,9},{9,1},{17,25},{25,17},{2,10},{10... | collective-permute-start | bytes 1572872 | tf_op jit(solution)/shard_map/ppermute | solution.py:41
  431.3 46.2 %collective-permute-start.56 = (bf16[512,512]{1,0:T(8,128)(2,1)S(1)}, bf16[512,512]{1,0:T(8,128)(2,1)S(1)}, u32[]{:S(2)}, u32[]{:S(2)}) collective-permute-start(bf16[512,512]{1,0:T(8,128)(2,1)S(1)} %constant_dynamic-slice_fusion.9), channel_id=1, source_target_pairs={{0,16},{8,24},{16,0},{24,8},{1,17},{9,25},{17,1},{25,9},{2,18},{10... | collective-permute-start | bytes 1572872 | tf_op jit(solution)/shard_map/ppermute | solution.py:41
  438.3 23.6 %collective-permute-start.73 = (bf16[128,1024]{1,0:T(8,128)(2,1)S(1)}, bf16[128,1024]{1,0:T(8,128)(2,1)S(1)}, u32[]{:S(2)}, u32[]{:S(2)}) collective-permute-start(bf16[128,1024]{1,0:T(8,128)(2,1)S(1)} %constant_dynamic-slice_fusion.5), channel_id=1, source_target_pairs={{0,16},{8,24},{16,0},{24,8},{1,17},{9,25},{17,1},{25,9},{2,18},{10... | collective-permute-start | bytes 786440 | tf_op jit(solution)/shard_map/ppermute | solution.py:41
  475.6 19.8 %collective-permute-start.70 = (bf16[64,1024]{1,0:T(8,128)(2,1)S(1)}, bf16[64,1024]{1,0:T(8,128)(2,1)S(1)}, u32[]{:S(2)}, u32[]{:S(2)}) collective-permute-start(bf16[64,1024]{1,0:T(8,128)(2,1)S(1)} %add_convert_fusion.15.refs_0_), channel_id=1, source_target_pairs={{0,16},{8,24},{16,0},{24,8},{1,17},{9,25},{17,1},{25,9},{2,18},{10... | collective-permute-start | bytes 393224 | tf_op jit(solution)/shard_map/ppermute | solution.py:41
  477.1 18.3 %collective-permute-start.71 = (bf16[64,1024]{1,0:T(8,128)(2,1)S(1)}, bf16[64,1024]{1,0:T(8,128)(2,1)S(1)}, u32[]{:S(2)}, u32[]{:S(2)}) collective-permute-start(bf16[64,1024]{1,0:T(8,128)(2,1)S(1)} %add_convert_fusion.15.refs_0_), channel_id=1, source_target_pairs={{0,8},{8,0},{16,24},{24,16},{1,9},{9,1},{17,25},{25,17},{2,10},{10... | collective-permute-start | bytes 393224 | tf_op jit(solution)/shard_map/ppermute | solution.py:41
  477.4 15.9 %collective-permute-start.52 = (bf16[256,512]{1,0:T(8,128)(2,1)S(1)}, bf16[256,512]{1,0:T(8,128)(2,1)S(1)}, u32[]{:S(2)}, u32[]{:S(2)}) collective-permute-start(bf16[256,512]{1,0:T(8,128)(2,1)S(1)} %constant_dynamic-slice_fusion.10), channel_id=1, source_target_pairs={{0,16},{8,24},{16,0},{24,8},{1,17},{9,25},{17,1},{25,9},{2,18},{10... | collective-permute-start | bytes 786440 | tf_op jit(solution)/shard_map/ppermute | solution.py:41
  478.3 16.7 %collective-permute-start.57 = (bf16[256,512]{1,0:T(8,128)(2,1)S(1)}, bf16[256,512]{1,0:T(8,128)(2,1)S(1)}, u32[]{:S(2)}, u32[]{:S(2)}) collective-permute-start(bf16[256,512]{1,0:T(8,128)(2,1)S(1)} %constant_dynamic-slice_fusion.8), channel_id=1, source_target_pairs={{0,8},{8,0},{16,24},{24,16},{1,9},{9,1},{17,25},{25,17},{2,10},{10... | collective-permute-start | bytes 786440 | tf_op jit(solution)/shard_map/ppermute | solution.py:41
  480.9 15.0 %collective-permute-start.46 = (f32[1024]{0:T(1024)S(1)}, f32[1024]{0:T(1024)S(1)}, u32[]{:S(2)}, u32[]{:S(2)}) collective-permute-start(f32[1024]{0:T(1024)S(1)} %get-tuple-element.559), channel_id=1, source_target_pairs={{0,4},{2,6},{4,0},{6,2},{1,5},{3,7},{5,1},{7,3},{8,12},{10,14},{12... | collective-permute-start | bytes 12296 | tf_op jit(solution)/shard_map/ppermute | solution.py:45
  498.8 18.6 %collective-permute-start.53 = (bf16[256,512]{1,0:T(8,128)(2,1)S(1)}, bf16[256,512]{1,0:T(8,128)(2,1)S(1)}, u32[]{:S(2)}, u32[]{:S(2)}) collective-permute-start(bf16[256,512]{1,0:T(8,128)(2,1)S(1)} %add_convert_fusion.13.refs_0_), channel_id=1, source_target_pairs={{0,16},{8,24},{16,0},{24,8},{1,17},{9,25},{17,1},{25,9},{2,18},{10... | collective-permute-start | bytes 786440 | tf_op jit(solution)/shard_map/ppermute | solution.py:41
  500.2 19.1 %collective-permute-start.58 = (bf16[256,512]{1,0:T(8,128)(2,1)S(1)}, bf16[256,512]{1,0:T(8,128)(2,1)S(1)}, u32[]{:S(2)}, u32[]{:S(2)}) collective-permute-start(bf16[256,512]{1,0:T(8,128)(2,1)S(1)} %add_convert_fusion.12.refs_4_), channel_id=1, source_target_pairs={{0,8},{8,0},{16,24},{24,16},{1,9},{9,1},{17,25},{25,17},{2,10},{10... | collective-permute-start | bytes 786440 | tf_op jit(solution)/shard_map/ppermute | solution.py:41
  516.8 23.2 %collective-permute-start.54 = (bf16[256,512]{1,0:T(8,128)(2,1)S(1)}, bf16[256,512]{1,0:T(8,128)(2,1)S(1)}, u32[]{:S(2)}, u32[]{:S(2)}) collective-permute-start(bf16[256,512]{1,0:T(8,128)(2,1)S(1)} %add_convert_fusion.13.refs_0_), channel_id=1, source_target_pairs={{0,8},{8,0},{16,24},{24,16},{1,9},{9,1},{17,25},{25,17},{2,10},{10... | collective-permute-start | bytes 786440 | tf_op jit(solution)/shard_map/ppermute | solution.py:41
  516.9 23.1 %collective-permute-start.59 = (bf16[256,512]{1,0:T(8,128)(2,1)S(1)}, bf16[256,512]{1,0:T(8,128)(2,1)S(1)}, u32[]{:S(2)}, u32[]{:S(2)}) collective-permute-start(bf16[256,512]{1,0:T(8,128)(2,1)S(1)} %add_convert_fusion.12.refs_4_), channel_id=1, source_target_pairs={{0,16},{8,24},{16,0},{24,8},{1,17},{9,25},{17,1},{25,9},{2,18},{10... | collective-permute-start | bytes 786440 | tf_op jit(solution)/shard_map/ppermute | solution.py:41
  517.3 22.7 %collective-permute-start.55 = (bf16[256,512]{1,0:T(8,128)(2,1)S(1)}, bf16[256,512]{1,0:T(8,128)(2,1)S(1)}, u32[]{:S(2)}, u32[]{:S(2)}) collective-permute-start(bf16[256,512]{1,0:T(8,128)(2,1)S(1)} %collective-permute-done.53.refs_1_), channel_id=1, source_target_pairs={{0,8},{8,0},{16,24},{24,16},{1,9},{9,1},{17,25},{25,17},{2,10},{10... | collective-permute-start | bytes 786440 | tf_op jit(solution)/shard_map/ppermute | solution.py:41
  519.3 20.8 %collective-permute-start.60 = (bf16[256,512]{1,0:T(8,128)(2,1)S(1)}, bf16[256,512]{1,0:T(8,128)(2,1)S(1)}, u32[]{:S(2)}, u32[]{:S(2)}) collective-permute-start(bf16[256,512]{1,0:T(8,128)(2,1)S(1)} %collective-permute-done.58.refs_5_), channel_id=1, source_target_pairs={{0,16},{8,24},{16,0},{24,8},{1,17},{9,25},{17,1},{25,9},{2,18},{10... | collective-permute-start | bytes 786440 | tf_op jit(solution)/shard_map/ppermute | solution.py:41
  (123 other events, 795.7 us)
Sparse Core Ops, SparseCore 0:
  61.5 56.6 all-gather.1
  290.1 43.5 reduce-scatter.1
  337.8 194.8 all-reduce.2

commit v3 on v2

--- a/solution.py
+++ b/solution.py
@@ -46,23 +46,6 @@
     if size == 4:
         return (x + swapped(1)) + (swapped(2) + swapped(3))
     return lax.psum(x, axis)
-
-
-def halving(part, bits, me, dp):
-    first, second = bits
-    v1, v2 = (me // first) % 2, (me // second) % 2
-    half = part.shape[0] // 2
-    kept = lax.dynamic_slice_in_dim(part, v1 * half, half, 0)
-    sent = lax.dynamic_slice_in_dim(part, (1 - v1) * half, half, 0)
-    total = (kept.astype(F32) + dp_swap(sent, first, dp).astype(F32)).astype(BF16)
-    quarter = half // 2
-    kept = lax.dynamic_slice_in_dim(total, v2 * quarter, quarter, 0)
-    sent = lax.dynamic_slice_in_dim(total, (1 - v2) * quarter, quarter, 0)
-    mine = (kept.astype(F32) + dp_swap(sent, second, dp).astype(F32)).astype(BF16)
-    near = dp_swap(mine, second, dp)
-    far = dp_swap(mine, first, dp)
-    cross = dp_swap(near, first, dp)
-    return [mine, near, far, cross]
 
 
 def piece_rows(bits, me):
@@ -151,20 +134,19 @@
     )(table, total_a, total_b)
 
 
-def reduce_grads(part_a, part_b, me, core, dp, widths, split):
-    if dp == 4:
-        pieces_a = halving(part_a, (1, 2), me, dp)
-        pieces_b = halving(part_b, (2, 1), me, dp)
-        return assemble(pieces_a, pieces_b, me, core, widths, split)
-    total_a, total_b = lax.psum(part_a, "dp"), lax.psum(part_b, "dp")
+def whole_sums(parts, core, widths, split):
+    total_a, total_b = lax.psum(tuple(cat(list(p), 0) for p in parts), "dp")
     outs, at = [], 0
     for width in widths:
         a, b = total_a[:, at : at + width], total_b[:, at : at + width]
-        axis = split
-        nat = jnp.where(core == 0, jnp.concatenate([a, b], axis), jnp.concatenate([b, a], axis))
+        nat = jnp.where(core == 0, cat([a, b], split), cat([b, a], split))
         outs.append(nat.astype(F32))
         at += width
     return outs
+
+
+def cat(items, axis):
+    return jnp.concatenate(items, axis)
 
 
 def rope_tables():
@@ -425,19 +407,20 @@
 
 
 def down_rows_kernel(t, weight, *refs):
-    out = refs[-1]
     half = weight.shape[0] // 2
     for s in range(ROWS):
+        out = refs[2 * ROWS + s]
         total = dot(refs[2 * s][0], weight[part(t, 0, half), :], NN)
         total += dot(refs[2 * s + 1][0], weight[part(t, 1, half), :], NN)
-        out[block_rows(t, s), :] = total.astype(BF16)
+        out[...] = total.astype(out.dtype)
 
 
 def down_rows(packs, weight, t):
+    shape = (BLOCK, weight.shape[1])
     return product(
         down_rows_kernel, t, (weight, *[p for pair in packs for p in pair]),
-        [((ROWS * BLOCK, weight.shape[1]), BF16)],
-    )[0]
+        [(shape, kind) for kind in (F32, BF16, F32, BF16)],
+    )
 
 
 def g_heads_kernel(t, x, weight, own, sent):
@@ -470,21 +453,27 @@
     )[0]
 
 
+def halves(t, which, size):
+    kept = t[2 * ROWS + 2 + which]
+    return kept * size, (1 - kept) * size
+
+
 def down_grads_kernel(t, *refs):
     packs, cot, outs = refs[: 2 * ROWS], refs[2 * ROWS], refs[2 * ROWS + 1 :]
-    for which, out in enumerate(outs):
-        for start in range(0, out.shape[0], FF_BLOCK):
-            cols = slice(start, start + FF_BLOCK)
+    half = outs[0].shape[0]
+    for which in range(2):
+        for out, begin in zip(outs[2 * which : 2 * which + 2], halves(t, which, half)):
+            cols = pl.ds(pl.multiple_of(begin, 128), half)
             total = 0.0
             for s in range(ROWS):
                 total += dot(packs[2 * s + which][0, :, cols], cot[block_rows(t, s), :], TN)
-            out[cols, :] = total.astype(BF16)
+            out[...] = total.astype(BF16)
 
 
 def down_grads(packs, cot, t):
-    shape = (packs[0][0].shape[2], cot.shape[1])
+    shape = (packs[0][0].shape[2] // 2, cot.shape[1])
     return product(
-        down_grads_kernel, t, (*[p for pair in packs for p in pair], cot), [(shape, BF16)] * 2
+        down_grads_kernel, t, (*[p for pair in packs for p in pair], cot), [(shape, BF16)] * 4
     )
 
 
@@ -509,31 +498,38 @@
 
 
 def out_grads_kernel(t, own, other, *refs):
-    for att, out in ((own, refs[-2]), (other, refs[-1])):
-        total = 0.0
-        for s in range(ROWS):
-            total += dot(att[s * BLOCK : (s + 1) * BLOCK, :], refs[s][...], TN)
-        out[...] = total.astype(BF16)
-
-
-def out_grads(own, other, dmid, t):
-    shape = (own.shape[1], dmid[0].shape[1])
-    return product(out_grads_kernel, t, (own, other, *dmid), [(shape, BF16)] * 2)
-
-
-def head_grads_kernel(t, own, other, *refs):
-    for grad, out in ((own, refs[-2]), (other, refs[-1])):
-        for start in range(0, out.shape[0], 256):
-            cols = slice(start, start + 256)
+    outs = refs[ROWS:]
+    half = outs[0].shape[0]
+    for which, att in enumerate((own, other)):
+        for out, begin in zip(outs[2 * which : 2 * which + 2], halves(t, which, half)):
+            cols = pl.ds(pl.multiple_of(begin, 128), half)
             total = 0.0
             for s in range(ROWS):
-                total += dot(refs[s][:, cols], grad[s * BLOCK : (s + 1) * BLOCK, :], TN)
-            out[cols, :] = total.astype(BF16)
+                total += dot(att[s * BLOCK : (s + 1) * BLOCK, cols], refs[s][...], TN)
+            out[...] = total.astype(BF16)
+
+
+def out_grads(own, other, dmid, t):
+    shape = (own.shape[1] // 2, dmid[0].shape[1])
+    return product(out_grads_kernel, t, (own, other, *dmid), [(shape, BF16)] * 4)
+
+
+def head_grads_kernel(t, own, other, *refs):
+    outs = refs[ROWS:]
+    half = outs[0].shape[0]
+    for which, grad in enumerate((own, other)):
+        for out, begin in zip(outs[2 * which : 2 * which + 2], halves(t, which, half)):
+            for start in range(0, half, 256):
+                cols = pl.ds(pl.multiple_of(begin + start, 128), 256)
+                total = 0.0
+                for s in range(ROWS):
+                    total += dot(refs[s][:, cols], grad[s * BLOCK : (s + 1) * BLOCK, :], TN)
+                out[start : start + 256, :] = total.astype(BF16)
 
 
 def head_grads(own, other, n1, t):
-    shape = (n1[0].shape[1], own.shape[1])
-    return product(head_grads_kernel, t, (own, other, *n1), [(shape, BF16)] * 2)
+    shape = (n1[0].shape[1] // 2, own.shape[1])
+    return product(head_grads_kernel, t, (own, other, *n1), [(shape, BF16)] * 4)
 
 
 def norm_stats(x):
@@ -547,10 +543,6 @@
     part = jnp.sum(scaled * unit, axis=1)
     inner = (part + swap(part)) / MODEL_WIDTH
     return (factor[:, None] * (scaled - unit * inner[:, None]), jnp.sum(grad * unit, axis=0))
-
-
-def cat(items, axis):
-    return jnp.concatenate(items, axis)
 
 
 def on_device(
@@ -570,7 +562,8 @@
 ):
     dp = lax.axis_size("dp")
     k, core, me = lax.axis_index("row"), lax.axis_index("col"), lax.axis_index("dp")
-    t = jnp.stack([k ^ i for i in range(ROWS)] * 2 + [core, 1 - core]).astype(jnp.int32)
+    keeps = [me % 2, (me // 2) % 2] if dp == 4 else [0 * me, 0 * me]
+    t = jnp.stack([k ^ i for i in range(ROWS)] * 2 + [core, 1 - core] + keeps).astype(jnp.int32)
     groups = query_weight.shape[1] // (2 * HEAD_SIZE)
     token = [hidden]
 
@@ -601,6 +594,68 @@
         done.append(work(3, three, swap(three)))
         return [x, one, two, three], done
 
+    def halving(kept, sent, bits):
+        first, second = bits
+        keep = (me // second) % 2
+        got = dp_swap(sent, first, dp)
+        yield
+        kept, got = now(kept), now(got)
+        size = kept.shape[0] // 2
+
+        def add(v):
+            a = lax.dynamic_slice_in_dim(kept, v * size, size, 0)
+            b = lax.dynamic_slice_in_dim(got, v * size, size, 0)
+            return (a.astype(F32) + b.astype(F32)).astype(BF16)
+
+        sent, mine = add(1 - keep), add(keep)
+        token[0] = sent
+        got = dp_swap(sent, second, dp)
+        yield
+        mine = (mine.astype(F32) + now(got).astype(F32)).astype(BF16)
+        token[0] = mine
+        near = dp_swap(mine, second, dp)
+        far = dp_swap(mine, first, dp)
+        yield
+        near = now(near)
+        token[0] = near
+        return [mine, near, far, dp_swap(near, first, dp)]
+
+    class Sum:
+        def __init__(self, parts, widths, split):
+            self.args = (core, widths, split)
+            self.halves = (parts[:2], parts[2:])
+            if dp == 4:
+                self.runs = [halving(*parts[:2], (1, 2)), halving(*parts[2:], (2, 1))]
+                self.done = [None, None]
+                self.step()
+            else:
+                self.outs = whole_sums(self.halves, *self.args)
+
+        def step(self):
+            if dp != 4:
+                return
+            for i, run in enumerate(self.runs):
+                try:
+                    next(run)
+                except StopIteration as stop:
+                    self.done[i] = stop.value
+
+        def result(self):
+            if dp != 4:
+                return self.outs
+            return assemble(*self.done, me, *self.args)
+
+    def spread(parts):
+        got_three = row_swap(parts[3], 1)
+        yield
+        got_three = now(got_three)
+        sent = (parts[2] + got_three.astype(F32)).astype(BF16)
+        token[0] = sent
+        got_two = row_swap(sent, 2)
+        got_one = row_swap(after(parts[1], got_three), 1)
+        yield
+        return parts[0] + now(got_one).astype(F32) + now(got_two).astype(F32)
+
     def scatter(term, between=lambda: None):
         part_three = term(3, BF16)
         got_three = row_swap(part_three, 1)
@@ -633,7 +688,7 @@
     n1, raws = gather(
         sent_one, lambda s, own, other: step(head_rows, own, other, heads, qkv_x, t)
     )
-    cot = lax.all_gather(now(cotangent), "row", axis=0, tiled=True)
+    cot = lax.all_gather(cotangent, "row", axis=0, tiled=True)
     att, lse, query, key, value = step(
         lambda *a: attend(*a, groups), t, raws, cosine, sine, query_gain, key_gain
     )
@@ -660,22 +715,15 @@
         return packed, swap(packed)
 
     n2, packs = gather(sent_two, hidden_units)
-    grads = {}
-
-    def ff_grads():
-        grads["down"] = step(down_grads, packs, cot, t)
-        grads["gu"] = step(gu_grads, packs, n2, t)
-
+    width = down_weight.shape[1]
+    down_sum = Sum(step(down_grads, packs, cot, t), (width,), 0)
+    gu_sums = lax.psum(tuple(step(gu_grads, packs, n2, t)), "dp")
     dsecond = scatter(
         lambda s, kind: step(
             lambda *a: mlp_back(*a[:4], kind, a[4]), *packs[s], gate_weight, up_weight, t
         ),
-        ff_grads,
-    )
-    (down_grad,) = reduce_grads(*grads["down"], me, core, dp, (down_weight.shape[1],), 0)
-    ff = gate_x.shape[1]
-    gate_grad, up_grad = place(*lax.psum(tuple(grads["gu"]), "dp"), core, (ff, ff))
-
+        down_sum.step,
+    )
     dmid_norm, after_part = norm_backward(dsecond, unit_two, factor_two, norm_after)
     dmiddle = cotangent.astype(F32) + dmid_norm
 
@@ -683,24 +731,36 @@
         mine, sent = step(g_heads, own, output_weight, t)
         return mine, swap(sent)
 
-    width = down_weight.shape[1]
     last = []
-    dmid, datt = gather(
-        dmiddle.astype(BF16), g_attended,
-        lambda: last.append(step(down_rows, packs, down_weight, t)),
-    )
-    last_sum = lax.psum_scatter(now(last[0]), "row", scatter_dimension=0, tiled=True)
-
+
+    def feed_forward_rows():
+        last.extend(step(down_rows, packs, down_weight, t))
+        down_sum.step()
+
+    dmid, datt = gather(dmiddle.astype(BF16), g_attended, feed_forward_rows)
+    last_run = spread(last)
+    next(last_run)
+    down_sum.step()
+
+    out_sum = Sum(step(out_grads, att, att_oth, dmid, t), (width,), 0)
     dqkv, gain_parts = step(
         lambda *a: attend_back(*a, groups),
         t, raws, [d for d, _ in datt], [d for _, d in datt],
         cosine, sine, query_gain, key_gain, (query, key, value, lse),
     )
+    next(last_run)
     dqkv_oth = swap(dqkv)
+    out_sum.step()
+    sums = []
 
     def head_grad():
-        grads["qkv"] = step(head_grads, dqkv, dqkv_oth, n1, t)
-        grads["out"] = step(out_grads, att, att_oth, dmid, t)
+        sums.append(
+            Sum(
+                step(head_grads, dqkv, dqkv_oth, n1, t),
+                tuple(w.shape[1] // 2 for w in heads), 1,
+            )
+        )
+        out_sum.step()
 
     dfirst = scatter(
         lambda s, kind: step(
@@ -708,11 +768,20 @@
         ),
         head_grad,
     )
-    layer_out = (middle + last_sum.astype(F32)).astype(BF16)
-    query_grad, key_grad, value_grad = reduce_grads(
-        *grads["qkv"], me, core, dp, tuple(w.shape[1] // 2 for w in heads), 1
-    )
-    (output_grad,) = reduce_grads(*grads["out"], me, core, dp, (width,), 0)
+    (qkv_sum,) = sums
+    qkv_sum.step()
+    out_sum.step()
+    try:
+        next(last_run)
+    except StopIteration as stop:
+        layer_out = (middle + stop.value).astype(BF16)
+    qkv_sum.step()
+    (down_grad,) = down_sum.result()
+    qkv_sum.step()
+    (output_grad,) = out_sum.result()
+    ff = gate_x.shape[1]
+    gate_grad, up_grad = place(*gu_sums, core, (ff, ff))
+    query_grad, key_grad, value_grad = qkv_sum.result()
     dres_norm, before_part = norm_backward(dfirst, unit_one, factor_one, norm_before)
     hidden_grad = dmiddle + dres_norm
 

time: 569 us -> 494 us (0.87)
  waiting for transfers between devices: 300 us -> 208 us
  starting transfers between devices: 73.9 us -> 88.8 us
  other arithmetic: 26 us -> 35.9 us
  local copies, waits for them, and re-layouts: 38.9 us -> 32.2 us
    ppermute x30, waiting for transfers between devices: 116 us -> 44.4 us  [dp_swap(): return lax.ppermute(x, 'dp', [(i, i ^ mask) for i in range(dp)])]
    ppermute x12, waiting for transfers between devices: 20.6 us -> 0.03 us  [small_sum(): lax.ppermute(x, axis, [(i, i ^ mask) for i in range(size)])]
    ppermute x18 -> x21, starting transfers between devices: 24.1 us -> 34.5 us  [row_swap(): return lax.ppermute(x, 'row', [(i, i ^ mask) for i in range(ROWS)])]
    convert_element_type x14 -> x15, other arithmetic: 10.7 us -> 17.1 us  [the longest x6 6.64 us: add(): return (a.astype(F32) + b.astype(F32)).astype(BF16)]
    dynamic_slice x12 -> x0, local copies, waits for them, and re-layouts: 5.91 us -> none  [the longest x6 4.24 us: halving(): sent = lax.dynamic_slice_in_dim(part, (1 - v1) * half, half, 0)]
    ppermute x18 -> x21, waiting for transfers between devices: 146 us -> 149 us  [row_swap(): return lax.ppermute(x, 'row', [(i, i ^ mask) for i in range(ROWS)])]
    unnamed x160 -> x216, local copies, waits for them, and re-layouts: 27.3 us -> 26 us
  transfers between devices with their start and end apart: 91 -> 93, of which waited for: 40 -> 32; matrix products, arithmetic and copies ran while one was open for 5% -> 7% of each run, Pallas kernels for 17% -> 18%
where the time goes in v3:
time: 494 us; the launch traced here: 491 us
  waiting for transfers between devices  208 us (42%)
  Pallas kernels  110 us (22%)
  starting transfers between devices  88.8 us (18%)
  other arithmetic  35.9 us (7%)
  local copies, waits for them, and re-layouts  32.2 us (7%)
  between operations  15.7 us (3%)
    ppermute x21, waiting for transfers between devices, row_swap(): return lax.ppermute(x, 'row', [(i, i ^ mask) for i in range(ROWS)])  149 us
    pallas_call x30, Pallas kernels, product(): pl.pallas_call(kernel, out_shape=[jax.ShapeDtypeStruct(shape, kind) for s...  77.9 us
    ppermute x30, waiting for transfers between devices, dp_swap(): return lax.ppermute(x, 'dp', [(i, i ^ mask) for i in range(dp)])  44.4 us
    ppermute x21, starting transfers between devices, row_swap(): return lax.ppermute(x, 'row', [(i, i ^ mask) for i in range(ROWS)])  34.5 us
    ppermute x30, starting transfers between devices, dp_swap(): return lax.ppermute(x, 'dp', [(i, i ^ mask) for i in range(dp)])  33 us
    unnamed x216, local copies, waits for them, and re-layouts  26 us
    ppermute x12, starting transfers between devices, small_sum(): lax.ppermute(x, axis, [(i, i ^ mask) for i in range(size)])  15 us
    ppermute x28, waiting for transfers between devices, swap(): return lax.ppermute(x, 'col', [(0, 1), (1, 0)])  14.8 us
  transfers between devices with their start and end apart: 93, of which 32 were waited for; matrix products, arithmetic and copies ran while one was open for 7% of the time, Pallas kernels for 18%

profile of v3, /device:TPU:0, one launch (start us, length us, event | category | flops | bytes accessed | tf_op | source)
XLA Modules:
  0.0 490.5 jit_solution(8548962293646576916)
XLA Ops:
  14.8 3.9 collective-permute-start.4
  23.4 19.2 %collective-permute-done.4.own.refs_2_ = bf16[256,1024]{1,0:T(8,128)(2,1)} collective-permute-done((bf16[256,1024]{1,0:T(8,128)(2,1)}, bf16[256,1024]{1,0:T(8,128)(2,1)}, u32[]{:S(2)}, u32[]{:S(2)}) %collective-permute-start.4) | collective-permute-done | bytes 524320 | tf_op jit(solution)/shard_map/ppermute | solution.py:33
  47.4 2.4 shard_map.230.refs_2_
  49.8 15.9 %collective-permute-done.7.own.refs_3_ = bf16[256,1024]{1,0:T(8,128)(2,1)} collective-permute-done((bf16[256,1024]{1,0:T(8,128)(2,1)}, bf16[256,1024]{1,0:T(8,128)(2,1)}, u32[]{:S(2)}, u32[]{:S(2)}) %collective-permute-start.7) | collective-permute-done | bytes 524320 | tf_op jit(solution)/shard_map/ppermute | solution.py:33
  68.0 2.4 shard_map.231.refs_3_
  70.6 5.6 %shard_map.232 = (bf16[1024,256]{1,0:T(8,128)(2,1)S(1)}, f32[1024,256]{1,0:T(8,128)S(1)}, bf16[1024,256]{1,0:T(8,128)(2,1)S(1)}, bf16[1024,128]{1,0:T(8,128)(2,1)S(1)}, bf16[1024,128]{1,0:T(8,128)(2,1)S(1)}) custom-call(s32[12]{0:T(128)S(1)} %stack.109.t.table, f32[256,512]{1,0:T(8,128)S(1)} %copy-done.40, f32[256,512]{1,0:T(8,128)S(1)} %shard_map.229.refs_1_, ...), custom_call_target="tpu_custom_call" | custom-call | flops 1 | bytes 1 | tf_op jit(solution)/shard_map/pallas_call | solution.py:263
  81.5 20.8 %collective-permute-done.10 = bf16[256,1024]{1,0:T(8,128)(2,1)S(1)} collective-permute-done((bf16[256,1024]{1,0:T(8,128)(2,1)S(1)}, bf16[256,1024]{1,0:T(8,128)(2,1)S(1)}, u32[]{:S(2)}, u32[]{:S(2)}) %collective-permute-start.10) | collective-permute-done | bytes 524320 | tf_op jit(solution)/shard_map/ppermute | solution.py:33
  102.5 2.6 collective-permute-start.12
  107.4 21.1 %collective-permute-done.12 = bf16[256,1024]{1,0:T(8,128)(2,1)S(1)} collective-permute-done((bf16[256,1024]{1,0:T(8,128)(2,1)S(1)}, bf16[256,1024]{1,0:T(8,128)(2,1)S(1)}, u32[]{:S(2)}, u32[]{:S(2)}) %collective-permute-start.12) | collective-permute-done | bytes 524320 | tf_op jit(solution)/shard_map/ppermute | solution.py:33
  134.7 6.2 %collective-permute-done.13 = f32[256]{0:T(256)S(1)} collective-permute-done((f32[256]{0:T(256)S(1)}, f32[256]{0:T(256)S(1)}, u32[]{:S(2)}, u32[]{:S(2)}) %collective-permute-start.13) | collective-permute-done | bytes 1056 | tf_op jit(solution)/shard_map/ppermute | solution.py:29
  146.7 5.1 %shard_map.237.g_mixed = f32[4,256,768]{2,1,0:T(8,128)S(1)} custom-call(s32[12]{0:T(128)S(1)} %stack.109.t.table, bf16[1024,1024]{1,0:T(8,128)(2,1)S(1)} %copy-done.37, bf16[1024,1024]{1,0:T(8,128)(2,1)} %collective-permute-done.17.other, bf16[1536,1024]{1,0:T(8,128)(2,1)S(1)} %copy-done.20, bf16[768,1024]{1,0:T(8,128)(2,1)S(1)} %collective-permute-done.18.x), custom_call_target="tpu_custom_call" | custom-call | flops 1 | bytes 1 | tf_op jit(solution)/shard_map/pallas_call | solution.py:301
  151.8 2.6 shard_map.238.refs_0_.own
  154.4 13.1 %collective-permute-done.21.own.refs_10_ = bf16[256,1024]{1,0:T(8,128)(2,1)S(1)} collective-permute-done((bf16[256,1024]{1,0:T(8,128)(2,1)S(1)}, bf16[256,1024]{1,0:T(8,128)(2,1)S(1)}, u32[]{:S(2)}, u32[]{:S(2)}) %collective-permute-start.21) | collective-permute-done | bytes 524320 | tf_op jit(solution)/shard_map/ppermute | solution.py:33
  169.5 2.6 shard_map.239.refs_2_.own
  172.1 2.6 shard_map.240.refs_4_.own
  174.8 7.1 %collective-permute-done.26.own.refs_11_ = bf16[256,1024]{1,0:T(8,128)(2,1)S(1)} collective-permute-done((bf16[256,1024]{1,0:T(8,128)(2,1)S(1)}, bf16[256,1024]{1,0:T(8,128)(2,1)S(1)}, u32[]{:S(2)}, u32[]{:S(2)}) %collective-permute-start.26) | collective-permute-done | bytes 524320 | tf_op jit(solution)/shard_map/ppermute | solution.py:33
  183.8 2.6 shard_map.241.refs_6_.own
  190.6 5.1 %shard_map.242 = (bf16[384,1024]{1,0:T(8,128)(2,1)S(1)}, bf16[384,1024]{1,0:T(8,128)(2,1)}, bf16[384,1024]{1,0:T(8,128)(2,1)S(1)}, bf16[384,1024]{1,0:T(8,128)(2,1)}) custom-call(s32[12]{0:T(128)S(1)} %stack.109.t.table, bf16[3,256,768]{2,1,0:T(8,128)(2,1)S(1)} %shard_map.238.refs_0_.own, bf16[3,256,768]{2,1,0:T(8,128)(2,1)S(1)} %collective-permute-done.19.refs_1_.other, ...), custom_call_target="tpu_custom_call" | custom-call | flops 1 | bytes 1 | tf_op jit(solution)/shard_map/pallas_call | solution.py:301
  196.6 7.3 %shard_map.243 = (bf16[1024,1536]{1,0:T(8,128)(2,1)S(1)}, bf16[1024,1536]{1,0:T(8,128)(2,1)S(1)}) custom-call(s32[12]{0:T(128)S(1)} %stack.109.t.table, bf16[3,256,768]{2,1,0:T(8,128)(2,1)S(1)} %shard_map.238.refs_0_.own, bf16[3,256,768]{2,1,0:T(8,128)(2,1)S(1)} %collective-permute-done.19.refs_1_.other, bf16[3,256,768]{2,1,0:T(8,128)(2,1)S(1)} %shard_map.239.refs_2_.own, ...), custom_call_target="tpu_custom_call" | custom-call | flops 1 | bytes 1 | tf_op jit(solution)/shard_map/pallas_call | solution.py:301
  203.9 2.4 shard_map.244
  210.7 3.2 shard_map.245
  213.9 2.4 shard_map.246
  216.2 4.3 collective-permute-done.29
  229.4 2.4 shard_map.247
  236.0 11.1 %collective-permute-done.33 = bf16[256,1024]{1,0:T(8,128)(2,1)} collective-permute-done((bf16[256,1024]{1,0:T(8,128)(2,1)}, bf16[256,1024]{1,0:T(8,128)(2,1)}, u32[]{:S(2)}, u32[]{:S(2)}) %collective-permute-start.33) | collective-permute-done | bytes 524320 | tf_op jit(solution)/shard_map/ppermute | solution.py:33
  247.2 2.5 multiply_reduce_fusion
  252.9 3.4 fusion.14
  270.7 4.8 shard_map.249
  278.7 3.8 collective-permute-done.37.x.refs_2_
  287.4 8.9 %collective-permute-done.40.x.refs_3_ = bf16[256,1024]{1,0:T(8,128)(2,1)S(1)} collective-permute-done((bf16[256,1024]{1,0:T(8,128)(2,1)}, bf16[256,1024]{1,0:T(8,128)(2,1)S(1)}, u32[]{:S(2)}, u32[]{:S(2)}) %collective-permute-start.40) | collective-permute-done | bytes 524320 | tf_op jit(solution)/shard_map/ppermute | solution.py:33
  297.4 5.2 %collective-permute-done.46.refs_1_ = bf16[192,1024]{1,0:T(8,128)(2,1)S(1)} collective-permute-done((bf16[192,1024]{1,0:T(8,128)(2,1)S(1)}, bf16[192,1024]{1,0:T(8,128)(2,1)S(1)}, u32[]{:S(2)}, u32[]{:S(2)}) %collective-permute-start.46) | collective-permute-done | bytes 393248 | tf_op jit(solution)/shard_map/ppermute | solution.py:41
  303.0 2.6 shard_map.253
  308.6 7.7 %shard_map.254 = (bf16[1024,512]{1,0:T(8,128)(2,1)S(1)}, f32[2,128]{1,0:T(2,128)S(1)}) custom-call(s32[12]{0:T(128)S(1)} %stack.109.t.table, f32[256,512]{1,0:T(8,128)S(1)} %copy-done.41, f32[256,512]{1,0:T(8,128)S(1)} %copy-done.43, f32[256,512]{1,0:T(8,128)S(1)} %copy-done.45, f32[256,512]{1,0:T(8,128)S(1)} %copy-done.51, ...), custom_call_target="tpu_custom_call" | custom-call | flops 1 | bytes 1 | tf_op jit(solution)/shard_map/pallas_call | solution.py:281
  322.5 8.7 %collective-permute-done.35 = bf16[256,1024]{1,0:T(8,128)(2,1)} collective-permute-done((bf16[256,1024]{1,0:T(8,128)(2,1)}, bf16[256,1024]{1,0:T(8,128)(2,1)}, u32[]{:S(2)}, u32[]{:S(2)}) %collective-permute-start.35) | collective-permute-done | bytes 524320 | tf_op jit(solution)/shard_map/ppermute | solution.py:33
  338.8 3.0 shard_map.255
  362.8 4.3 shard_map.259
  372.8 8.9 %collective-permute-done.88.refs_3_ = bf16[192,1024]{1,0:T(8,128)(2,1)S(1)} collective-permute-done((bf16[192,1024]{1,0:T(8,128)(2,1)}, bf16[192,1024]{1,0:T(8,128)(2,1)S(1)}, u32[]{:S(2)}, u32[]{:S(2)}) %collective-permute-start.88) | collective-permute-done | bytes 393248 | tf_op jit(solution)/shard_map/ppermute | solution.py:41
  382.1 4.8 shard_map.263
  387.0 2.5 collective-permute-start.60
  391.0 12.0 %collective-permute-done.50 = bf16[64,1024]{1,0:T(8,128)(2,1)S(1)} collective-permute-done((bf16[64,1024]{1,0:T(8,128)(2,1)S(1)}, bf16[64,1024]{1,0:T(8,128)(2,1)S(1)}, u32[]{:S(2)}, u32[]{:S(2)}) %collective-permute-start.50) | collective-permute-done | bytes 131104 | tf_op jit(solution)/shard_map/ppermute | solution.py:41
  408.2 6.9 %collective-permute-done.60 = bf16[256,1024]{1,0:T(8,128)(2,1)S(1)} collective-permute-done((bf16[256,1024]{1,0:T(8,128)(2,1)S(1)}, bf16[256,1024]{1,0:T(8,128)(2,1)S(1)}, u32[]{:S(2)}, u32[]{:S(2)}) %collective-permute-start.60) | collective-permute-done | bytes 524320 | tf_op jit(solution)/shard_map/ppermute | solution.py:33
  419.3 6.6 %collective-permute-done.54.refs_5_ = bf16[64,1024]{1,0:T(8,128)(2,1)S(1)} collective-permute-done((bf16[64,1024]{1,0:T(8,128)(2,1)S(1)}, bf16[64,1024]{1,0:T(8,128)(2,1)S(1)}, u32[]{:S(2)}, u32[]{:S(2)}) %collective-permute-start.54) | collective-permute-done | bytes 131104 | tf_op jit(solution)/shard_map/ppermute | solution.py:41
  425.9 7.5 %collective-permute-done.58 = bf16[256,1024]{1,0:T(8,128)(2,1)S(1)} collective-permute-done((bf16[256,1024]{1,0:T(8,128)(2,1)S(1)}, bf16[256,1024]{1,0:T(8,128)(2,1)S(1)}, u32[]{:S(2)}, u32[]{:S(2)}) %collective-permute-start.58) | collective-permute-done | bytes 524320 | tf_op jit(solution)/shard_map/ppermute | solution.py:33
  433.5 3.4 collective-permute-start.64
  457.2 8.6 %collective-permute-done.86.refs_7_ = bf16[64,1024]{1,0:T(8,128)(2,1)S(1)} collective-permute-done((bf16[64,1024]{1,0:T(8,128)(2,1)S(1)}, bf16[64,1024]{1,0:T(8,128)(2,1)S(1)}, u32[]{:S(2)}, u32[]{:S(2)}) %collective-permute-start.86) | collective-permute-done | bytes 131104 | tf_op jit(solution)/shard_map/ppermute | solution.py:41
  465.8 3.7 shard_map.261
  469.5 4.2 shard_map.260
  477.5 6.0 %shard_map.262 = (f32[1024,1536]{1,0:T(8,128)}, f32[1024,1536]{1,0:T(8,128)}) custom-call(s32[2]{0:T(128)S(1)} %pad_add_fusion.table_ref, bf16[1024,1536]{1,0:T(8,128)(2,1)S(1)} %copy-done.54, bf16[1024,1536]{1,0:T(8,128)(2,1)S(1)} %copy-done.55), custom_call_target="tpu_custom_call" | custom-call | flops 1 | bytes 1 | tf_op jit(solution)/shard_map/pallas_call | solution.py:120
  (444 shorter events, 170.7 us)
Async XLA Ops:
  7.2 122.5 %all-gather.2.cloned.1.call-start = ((), (), s32[]{:S(2)}) async-start(), calls=%async_computation | async-start | bytes 2621440 | tf_op jit(solution)/shard_map/all_gather | solution.py:691
  14.8 27.8 %collective-permute-start.4 = (bf16[256,1024]{1,0:T(8,128)(2,1)}, bf16[256,1024]{1,0:T(8,128)(2,1)}, u32[]{:S(2)}, u32[]{:S(2)}) collective-permute-start(bf16[256,1024]{1,0:T(8,128)(2,1)} %fusion.4.own.refs_0_), channel_id=1, source_target_pairs={{0,4},{2,6},{4,0},{6,2},{1,5},{3,7},{5,1},{7,3},{8,12},{10,14},{12... | collective-permute-start | bytes 1572872 | tf_op jit(solution)/shard_map/ppermute | solution.py:33
  18.7 24.1 %collective-permute-start.3 = (bf16[256,1024]{1,0:T(8,128)(2,1)}, bf16[256,1024]{1,0:T(8,128)(2,1)}, u32[]{:S(2)}, u32[]{:S(2)}) collective-permute-start(bf16[256,1024]{1,0:T(8,128)(2,1)} %fusion.4.own.refs_0_), channel_id=1, source_target_pairs={{0,2},{2,0},{4,6},{6,4},{1,3},{3,1},{5,7},{7,5},{8,10},{10,8},{12,... | collective-permute-start | bytes 1572872 | tf_op jit(solution)/shard_map/ppermute | solution.py:33
  43.3 22.3 %collective-permute-start.7 = (bf16[256,1024]{1,0:T(8,128)(2,1)}, bf16[256,1024]{1,0:T(8,128)(2,1)}, u32[]{:S(2)}, u32[]{:S(2)}) collective-permute-start(bf16[256,1024]{1,0:T(8,128)(2,1)} %collective-permute-done.4.own.refs_2_), channel_id=1, source_target_pairs={{0,2},{2,0},{4,6},{6,4},{1,3},{3,1},{5,7},{7,5},{8,10},{10,8},{12,... | collective-permute-start | bytes 1572872 | tf_op jit(solution)/shard_map/ppermute | solution.py:33
  44.8 428.9 %all-reduce.3.cloned.1.call-start = ((), (), s32[]{:S(2)}) async-start(), calls=%async_computation.1 | async-start | bytes 12582912 | tf_op jit(solution)/shard_map/psum | solution.py:720
  79.4 22.9 %collective-permute-start.10 = (bf16[256,1024]{1,0:T(8,128)(2,1)S(1)}, bf16[256,1024]{1,0:T(8,128)(2,1)S(1)}, u32[]{:S(2)}, u32[]{:S(2)}) collective-permute-start(bf16[256,1024]{1,0:T(8,128)(2,1)S(1)} %shard_map.233), channel_id=1, source_target_pairs={{0,2},{2,0},{4,6},{6,4},{1,3},{3,1},{5,7},{7,5},{8,10},{10,8},{12,... | collective-permute-start | bytes 1572872 | tf_op jit(solution)/shard_map/ppermute | solution.py:33
  102.5 26.0 %collective-permute-start.12 = (bf16[256,1024]{1,0:T(8,128)(2,1)S(1)}, bf16[256,1024]{1,0:T(8,128)(2,1)S(1)}, u32[]{:S(2)}, u32[]{:S(2)}) collective-permute-start(bf16[256,1024]{1,0:T(8,128)(2,1)S(1)} %add_convert_fusion.4), channel_id=1, source_target_pairs={{0,4},{2,6},{4,0},{6,2},{1,5},{3,7},{5,1},{7,3},{8,12},{10,14},{12... | collective-permute-start | bytes 1572872 | tf_op jit(solution)/shard_map/ppermute | solution.py:33
  105.0 23.4 %collective-permute-start.11 = (bf16[256,1024]{1,0:T(8,128)(2,1)S(1)}, bf16[256,1024]{1,0:T(8,128)(2,1)S(1)}, u32[]{:S(2)}, u32[]{:S(2)}) collective-permute-start(bf16[256,1024]{1,0:T(8,128)(2,1)S(1)} %shard_map.234), channel_id=1, source_target_pairs={{0,2},{2,0},{4,6},{6,4},{1,3},{3,1},{5,7},{7,5},{8,10},{10,8},{12,... | collective-permute-start | bytes 1572872 | tf_op jit(solution)/shard_map/ppermute | solution.py:33
  132.2 19.6 %collective-permute-start.15 = (bf16[1024,768]{1,0:T(8,128)(2,1)S(1)}, bf16[1024,768]{1,0:T(8,128)(2,1)S(1)}, u32[]{:S(2)}, u32[]{:S(2)}) collective-permute-start(bf16[1024,768]{1,0:T(8,128)(2,1)S(1)} %constant_dynamic-slice_fusion.2), channel_id=1, source_target_pairs={{0,1},{1,0},{2,3},{3,2},{4,5},{5,4},{6,7},{7,6},{8,9},{9,8},{10,11... | collective-permute-start | bytes 4718600 | tf_op jit(solution)/shard_map/ppermute | solution.py:29
  134.1 17.7 %collective-permute-start.16 = (bf16[1024,768]{1,0:T(8,128)(2,1)S(1)}, bf16[1024,768]{1,0:T(8,128)(2,1)S(1)}, u32[]{:S(2)}, u32[]{:S(2)}) collective-permute-start(bf16[1024,768]{1,0:T(8,128)(2,1)S(1)} %constant_dynamic-slice_fusion.1), channel_id=1, source_target_pairs={{0,1},{1,0},{2,3},{3,2},{4,5},{5,4},{6,7},{7,6},{8,9},{9,8},{10,11... | collective-permute-start | bytes 4718600 | tf_op jit(solution)/shard_map/ppermute | solution.py:29
  141.2 26.3 %collective-permute-start.21 = (bf16[256,1024]{1,0:T(8,128)(2,1)S(1)}, bf16[256,1024]{1,0:T(8,128)(2,1)S(1)}, u32[]{:S(2)}, u32[]{:S(2)}) collective-permute-start(bf16[256,1024]{1,0:T(8,128)(2,1)S(1)} %multiply_convert_fusion.own.refs_8_), channel_id=1, source_target_pairs={{0,4},{2,6},{4,0},{6,2},{1,5},{3,7},{5,1},{7,3},{8,12},{10,14},{12... | collective-permute-start | bytes 1572872 | tf_op jit(solution)/shard_map/ppermute | solution.py:33
  143.1 24.4 %collective-permute-start.20 = (bf16[256,1024]{1,0:T(8,128)(2,1)S(1)}, bf16[256,1024]{1,0:T(8,128)(2,1)S(1)}, u32[]{:S(2)}, u32[]{:S(2)}) collective-permute-start(bf16[256,1024]{1,0:T(8,128)(2,1)S(1)} %multiply_convert_fusion.own.refs_8_), channel_id=1, source_target_pairs={{0,2},{2,0},{4,6},{6,4},{1,3},{3,1},{5,7},{7,5},{8,10},{10,8},{12,... | collective-permute-start | bytes 1572872 | tf_op jit(solution)/shard_map/ppermute | solution.py:33
  207.7 24.2 %collective-permute-start.31 = (bf16[384,1024]{1,0:T(8,128)(2,1)}, bf16[384,1024]{1,0:T(8,128)(2,1)}, u32[]{:S(2)}, u32[]{:S(2)}) collective-permute-start(bf16[384,1024]{1,0:T(8,128)(2,1)} %get-tuple-element.478), channel_id=1, source_target_pairs={{0,8},{8,0},{16,24},{24,16},{1,9},{9,1},{17,25},{25,17},{2,10},{10... | collective-permute-start | bytes 2359304 | tf_op jit(solution)/shard_map/ppermute | solution.py:41
  209.2 25.0 %collective-permute-start.32 = (bf16[384,1024]{1,0:T(8,128)(2,1)}, bf16[384,1024]{1,0:T(8,128)(2,1)}, u32[]{:S(2)}, u32[]{:S(2)}) collective-permute-start(bf16[384,1024]{1,0:T(8,128)(2,1)} %get-tuple-element.481), channel_id=1, source_target_pairs={{0,16},{8,24},{16,0},{24,8},{1,17},{9,25},{17,1},{25,9},{2,18},{10... | collective-permute-start | bytes 2359304 | tf_op jit(solution)/shard_map/ppermute | solution.py:41
  221.5 25.7 %collective-permute-start.33 = (bf16[256,1024]{1,0:T(8,128)(2,1)}, bf16[256,1024]{1,0:T(8,128)(2,1)}, u32[]{:S(2)}, u32[]{:S(2)}) collective-permute-start(bf16[256,1024]{1,0:T(8,128)(2,1)} %add_convert_fusion.3), channel_id=1, source_target_pairs={{0,4},{2,6},{4,0},{6,2},{1,5},{3,7},{5,1},{7,3},{8,12},{10,14},{12... | collective-permute-start | bytes 1572872 | tf_op jit(solution)/shard_map/ppermute | solution.py:33
  223.3 23.9 %collective-permute-start.30 = (bf16[256,1024]{1,0:T(8,128)(2,1)}, bf16[256,1024]{1,0:T(8,128)(2,1)}, u32[]{:S(2)}, u32[]{:S(2)}) collective-permute-start(bf16[256,1024]{1,0:T(8,128)(2,1)} %shard_map.245), channel_id=1, source_target_pairs={{0,2},{2,0},{4,6},{6,4},{1,3},{3,1},{5,7},{7,5},{8,10},{10,8},{12,... | collective-permute-start | bytes 1572872 | tf_op jit(solution)/shard_map/ppermute | solution.py:33
  249.7 27.6 %collective-permute-start.38 = (bf16[192,1024]{1,0:T(8,128)(2,1)}, bf16[192,1024]{1,0:T(8,128)(2,1)}, u32[]{:S(2)}, u32[]{:S(2)}) collective-permute-start(bf16[192,1024]{1,0:T(8,128)(2,1)} %add_convert_fusion.9), channel_id=1, source_target_pairs={{0,8},{8,0},{16,24},{24,16},{1,9},{9,1},{17,25},{25,17},{2,10},{10... | collective-permute-start | bytes 1179656 | tf_op jit(solution)/shard_map/ppermute | solution.py:41
  251.3 24.1 %collective-permute-start.39 = (bf16[192,1024]{1,0:T(8,128)(2,1)}, bf16[192,1024]{1,0:T(8,128)(2,1)}, u32[]{:S(2)}, u32[]{:S(2)}) collective-permute-start(bf16[192,1024]{1,0:T(8,128)(2,1)} %add_convert_fusion.10), channel_id=1, source_target_pairs={{0,16},{8,24},{16,0},{24,8},{1,17},{9,25},{17,1},{25,9},{2,18},{10... | collective-permute-start | bytes 1179656 | tf_op jit(solution)/shard_map/ppermute | solution.py:41
  256.3 26.2 %collective-permute-start.37 = (bf16[256,1024]{1,0:T(8,128)(2,1)}, bf16[256,1024]{1,0:T(8,128)(2,1)}, u32[]{:S(2)}, u32[]{:S(2)}) collective-permute-start(bf16[256,1024]{1,0:T(8,128)(2,1)} %get-tuple-element.532.x.refs_0_), channel_id=1, source_target_pairs={{0,4},{2,6},{4,0},{6,2},{1,5},{3,7},{5,1},{7,3},{8,12},{10,14},{12... | collective-permute-start | bytes 1572872 | tf_op jit(solution)/shard_map/ppermute | solution.py:33
  257.3 26.9 %collective-permute-start.36 = (bf16[256,1024]{1,0:T(8,128)(2,1)}, bf16[256,1024]{1,0:T(8,128)(2,1)S(1)}, u32[]{:S(2)}, u32[]{:S(2)}) collective-permute-start(bf16[256,1024]{1,0:T(8,128)(2,1)} %get-tuple-element.532.x.refs_0_), channel_id=1, source_target_pairs={{0,2},{2,0},{4,6},{6,4},{1,3},{3,1},{5,7},{7,5},{8,10},{10,8},{12,... | collective-permute-start | bytes 1572872 | tf_op jit(solution)/shard_map/ppermute | solution.py:33
  282.5 20.0 %collective-permute-start.46 = (bf16[192,1024]{1,0:T(8,128)(2,1)S(1)}, bf16[192,1024]{1,0:T(8,128)(2,1)S(1)}, u32[]{:S(2)}, u32[]{:S(2)}) collective-permute-start(bf16[192,1024]{1,0:T(8,128)(2,1)S(1)} %add_convert_fusion.6.refs_0_), channel_id=1, source_target_pairs={{0,16},{8,24},{16,0},{24,8},{1,17},{9,25},{17,1},{25,9},{2,18},{10... | collective-permute-start | bytes 1179656 | tf_op jit(solution)/shard_map/ppermute | solution.py:41
  283.0 20.0 %collective-permute-start.45 = (bf16[192,1024]{1,0:T(8,128)(2,1)S(1)}, bf16[192,1024]{1,0:T(8,128)(2,1)S(1)}, u32[]{:S(2)}, u32[]{:S(2)}) collective-permute-start(bf16[192,1024]{1,0:T(8,128)(2,1)S(1)} %add_convert_fusion.5.refs_4_), channel_id=1, source_target_pairs={{0,8},{8,0},{16,24},{24,16},{1,9},{9,1},{17,25},{25,17},{2,10},{10... | collective-permute-start | bytes 1179656 | tf_op jit(solution)/shard_map/ppermute | solution.py:41
  284.2 24.3 %collective-permute-start.41 = (bf16[256,256]{1,0:T(8,128)(2,1)S(1)}, bf16[256,256]{1,0:T(8,128)(2,1)S(1)}, u32[]{:S(2)}, u32[]{:S(2)}) collective-permute-start(bf16[256,256]{1,0:T(8,128)(2,1)S(1)} %get-tuple-element.519), channel_id=1, source_target_pairs={{0,1},{1,0},{2,3},{3,2},{4,5},{5,4},{6,7},{7,6},{8,9},{9,8},{10,11... | collective-permute-start | bytes 393224 | tf_op jit(solution)/shard_map/ppermute | solution.py:29
  285.2 23.3 %collective-permute-start.42 = (bf16[256,256]{1,0:T(8,128)(2,1)S(1)}, bf16[256,256]{1,0:T(8,128)(2,1)S(1)}, u32[]{:S(2)}, u32[]{:S(2)}) collective-permute-start(bf16[256,256]{1,0:T(8,128)(2,1)S(1)} %get-tuple-element.520), channel_id=1, source_target_pairs={{0,1},{1,0},{2,3},{3,2},{4,5},{5,4},{6,7},{7,6},{8,9},{9,8},{10,11... | collective-permute-start | bytes 393224 | tf_op jit(solution)/shard_map/ppermute | solution.py:29
  316.4 22.4 %collective-permute-start.52 = (bf16[1024,512]{1,0:T(8,128)(2,1)S(1)}, bf16[1024,512]{1,0:T(8,128)(2,1)}, u32[]{:S(2)}, u32[]{:S(2)}) collective-permute-start(bf16[1024,512]{1,0:T(8,128)(2,1)S(1)} %get-tuple-element.595.own), channel_id=1, source_target_pairs={{0,1},{1,0},{2,3},{3,2},{4,5},{5,4},{6,7},{7,6},{8,9},{9,8},{10,11... | collective-permute-start | bytes 3145736 | tf_op jit(solution)/shard_map/ppermute | solution.py:29
  318.5 19.6 %collective-permute-start.49 = (bf16[128,1024]{1,0:T(8,128)(2,1)}, bf16[128,1024]{1,0:T(8,128)(2,1)S(1)}, u32[]{:S(2)}, u32[]{:S(2)}) collective-permute-start(bf16[128,1024]{1,0:T(8,128)(2,1)} %copy-done.88), channel_id=1, source_target_pairs={{0,16},{8,24},{16,0},{24,8},{1,17},{9,25},{17,1},{25,9},{2,18},{10... | collective-permute-start | bytes 786440 | tf_op jit(solution)/shard_map/ppermute | solution.py:41
  319.6 16.1 %collective-permute-start.48 = (bf16[128,1024]{1,0:T(8,128)(2,1)}, bf16[128,1024]{1,0:T(8,128)(2,1)S(1)}, u32[]{:S(2)}, u32[]{:S(2)}) collective-permute-start(bf16[128,1024]{1,0:T(8,128)(2,1)} %copy-done.89), channel_id=1, source_target_pairs={{0,8},{8,0},{16,24},{24,16},{1,9},{9,1},{17,25},{25,17},{2,10},{10... | collective-permute-start | bytes 786440 | tf_op jit(solution)/shard_map/ppermute | solution.py:41
  321.8 21.4 %collective-permute-start.77 = (f32[1280]{0:T(1024)}, f32[1280]{0:T(1024)}, u32[]{:S(2)}, u32[]{:S(2)}) collective-permute-start(f32[1280]{0:T(1024)} %pad_maximum_fusion.3), channel_id=1, source_target_pairs={{0,4},{2,6},{4,0},{6,2},{1,5},{3,7},{5,1},{7,3},{8,12},{10,14},{12... | collective-permute-start | bytes 15368 | tf_op jit(solution)/shard_map/ppermute | solution.py:45
  341.8 17.4 %collective-permute-start.53 = (bf16[256,1024]{1,0:T(8,128)(2,1)}, bf16[256,1024]{1,0:T(8,128)(2,1)}, u32[]{:S(2)}, u32[]{:S(2)}) collective-permute-start(bf16[256,1024]{1,0:T(8,128)(2,1)} %shard_map.255), channel_id=1, source_target_pairs={{0,2},{2,0},{4,6},{6,4},{1,3},{3,1},{5,7},{7,5},{8,10},{10,8},{12,... | collective-permute-start | bytes 1572872 | tf_op jit(solution)/shard_map/ppermute | solution.py:33
  349.4 20.4 %collective-permute-start.87 = (bf16[192,1024]{1,0:T(8,128)(2,1)S(1)}, bf16[192,1024]{1,0:T(8,128)(2,1)S(1)}, u32[]{:S(2)}, u32[]{:S(2)}) collective-permute-start(bf16[192,1024]{1,0:T(8,128)(2,1)S(1)} %add_convert_fusion.6.refs_0_), channel_id=1, source_target_pairs={{0,8},{8,0},{16,24},{24,16},{1,9},{9,1},{17,25},{25,17},{2,10},{10... | collective-permute-start | bytes 1179656 | tf_op jit(solution)/shard_map/ppermute | solution.py:41
  350.5 20.8 %collective-permute-start.89 = (bf16[192,1024]{1,0:T(8,128)(2,1)}, bf16[192,1024]{1,0:T(8,128)(2,1)S(1)}, u32[]{:S(2)}, u32[]{:S(2)}) collective-permute-start(bf16[192,1024]{1,0:T(8,128)(2,1)} %copy-done.56), channel_id=1, source_target_pairs={{0,16},{8,24},{16,0},{24,8},{1,17},{9,25},{17,1},{25,9},{2,18},{10... | collective-permute-start | bytes 1179656 | tf_op jit(solution)/shard_map/ppermute | solution.py:41
  351.6 30.1 %collective-permute-start.88 = (bf16[192,1024]{1,0:T(8,128)(2,1)}, bf16[192,1024]{1,0:T(8,128)(2,1)S(1)}, u32[]{:S(2)}, u32[]{:S(2)}) collective-permute-start(bf16[192,1024]{1,0:T(8,128)(2,1)} %copy-done.71), channel_id=1, source_target_pairs={{0,8},{8,0},{16,24},{24,16},{1,9},{9,1},{17,25},{25,17},{2,10},{10... | collective-permute-start | bytes 1179656 | tf_op jit(solution)/shard_map/ppermute | solution.py:41
  352.9 29.2 %collective-permute-start.90 = (bf16[192,1024]{1,0:T(8,128)(2,1)}, bf16[192,1024]{1,0:T(8,128)(2,1)S(1)}, u32[]{:S(2)}, u32[]{:S(2)}) collective-permute-start(bf16[192,1024]{1,0:T(8,128)(2,1)} %copy-done.73), channel_id=1, source_target_pairs={{0,16},{8,24},{16,0},{24,8},{1,17},{9,25},{17,1},{25,9},{2,18},{10... | collective-permute-start | bytes 1179656 | tf_op jit(solution)/shard_map/ppermute | solution.py:41
  367.1 38.2 %collective-permute-start.56 = (bf16[512,512]{1,0:T(8,128)(2,1)S(1)}, bf16[512,512]{1,0:T(8,128)(2,1)S(1)}, u32[]{:S(2)}, u32[]{:S(2)}) collective-permute-start(bf16[512,512]{1,0:T(8,128)(2,1)S(1)} %get-tuple-element.606), channel_id=1, source_target_pairs={{0,8},{8,0},{16,24},{24,16},{1,9},{9,1},{17,25},{25,17},{2,10},{10... | collective-permute-start | bytes 1572872 | tf_op jit(solution)/shard_map/ppermute | solution.py:41
  369.8 19.7 %collective-permute-start.51 = (bf16[64,1024]{1,0:T(8,128)(2,1)S(1)}, bf16[64,1024]{1,0:T(8,128)(2,1)S(1)}, u32[]{:S(2)}, u32[]{:S(2)}) collective-permute-start(bf16[64,1024]{1,0:T(8,128)(2,1)S(1)} %copy-done.102), channel_id=1, source_target_pairs={{0,16},{8,24},{16,0},{24,8},{1,17},{9,25},{17,1},{25,9},{2,18},{10... | collective-permute-start | bytes 393224 | tf_op jit(solution)/shard_map/ppermute | solution.py:41
  371.3 35.5 %collective-permute-start.57 = (bf16[512,512]{1,0:T(8,128)(2,1)S(1)}, bf16[512,512]{1,0:T(8,128)(2,1)S(1)}, u32[]{:S(2)}, u32[]{:S(2)}) collective-permute-start(bf16[512,512]{1,0:T(8,128)(2,1)S(1)} %get-tuple-element.609), channel_id=1, source_target_pairs={{0,16},{8,24},{16,0},{24,8},{1,17},{9,25},{17,1},{25,9},{2,18},{10... | collective-permute-start | bytes 1572872 | tf_op jit(solution)/shard_map/ppermute | solution.py:41
  381.7 21.2 %collective-permute-start.50 = (bf16[64,1024]{1,0:T(8,128)(2,1)S(1)}, bf16[64,1024]{1,0:T(8,128)(2,1)S(1)}, u32[]{:S(2)}, u32[]{:S(2)}) collective-permute-start(bf16[64,1024]{1,0:T(8,128)(2,1)S(1)} %copy-done.101), channel_id=1, source_target_pairs={{0,8},{8,0},{16,24},{24,16},{1,9},{9,1},{17,25},{25,17},{2,10},{10... | collective-permute-start | bytes 393224 | tf_op jit(solution)/shard_map/ppermute | solution.py:41
  387.0 28.2 %collective-permute-start.60 = (bf16[256,1024]{1,0:T(8,128)(2,1)S(1)}, bf16[256,1024]{1,0:T(8,128)(2,1)S(1)}, u32[]{:S(2)}, u32[]{:S(2)}) collective-permute-start(bf16[256,1024]{1,0:T(8,128)(2,1)S(1)} %add_convert_fusion.1), channel_id=1, source_target_pairs={{0,4},{2,6},{4,0},{6,2},{1,5},{3,7},{5,1},{7,3},{8,12},{10,14},{12... | collective-permute-start | bytes 1572872 | tf_op jit(solution)/shard_map/ppermute | solution.py:33
  389.5 27.2 %collective-permute-start.59 = (bf16[256,1024]{1,0:T(8,128)(2,1)S(1)}, bf16[256,1024]{1,0:T(8,128)(2,1)S(1)}, u32[]{:S(2)}, u32[]{:S(2)}) collective-permute-start(bf16[256,1024]{1,0:T(8,128)(2,1)S(1)} %shard_map.256), channel_id=1, source_target_pairs={{0,2},{2,0},{4,6},{6,4},{1,3},{3,1},{5,7},{7,5},{8,10},{10,8},{12,... | collective-permute-start | bytes 1572872 | tf_op jit(solution)/shard_map/ppermute | solution.py:33
  403.0 30.5 %collective-permute-start.58 = (bf16[256,1024]{1,0:T(8,128)(2,1)S(1)}, bf16[256,1024]{1,0:T(8,128)(2,1)S(1)}, u32[]{:S(2)}, u32[]{:S(2)}) collective-permute-start(bf16[256,1024]{1,0:T(8,128)(2,1)S(1)} %copy-done.96), channel_id=1, source_target_pairs={{0,4},{2,6},{4,0},{6,2},{1,5},{3,7},{5,1},{7,3},{8,12},{10,14},{12... | collective-permute-start | bytes 1572872 | tf_op jit(solution)/shard_map/ppermute | solution.py:33
  405.3 31.5 %collective-permute-start.47 = (bf16[256,1024]{1,0:T(8,128)(2,1)S(1)}, bf16[256,1024]{1,0:T(8,128)(2,1)S(1)}, u32[]{:S(2)}, u32[]{:S(2)}) collective-permute-start(bf16[256,1024]{1,0:T(8,128)(2,1)S(1)} %copy-done.87), channel_id=1, source_target_pairs={{0,2},{2,0},{4,6},{6,4},{1,3},{3,1},{5,7},{7,5},{8,10},{10,8},{12,... | collective-permute-start | bytes 1572872 | tf_op jit(solution)/shard_map/ppermute | solution.py:33
  415.1 21.7 %collective-permute-start.68 = (bf16[256,512]{1,0:T(8,128)(2,1)S(1)}, bf16[256,512]{1,0:T(8,128)(2,1)S(1)}, u32[]{:S(2)}, u32[]{:S(2)}) collective-permute-start(bf16[256,512]{1,0:T(8,128)(2,1)S(1)} %add_convert_fusion.16), channel_id=1, source_target_pairs={{0,16},{8,24},{16,0},{24,8},{1,17},{9,25},{17,1},{25,9},{2,18},{10... | collective-permute-start | bytes 786440 | tf_op jit(solution)/shard_map/ppermute | solution.py:41
  418.1 20.5 %collective-permute-start.70 = (bf16[256,512]{1,0:T(8,128)(2,1)S(1)}, bf16[256,512]{1,0:T(8,128)(2,1)S(1)}, u32[]{:S(2)}, u32[]{:S(2)}) collective-permute-start(bf16[256,512]{1,0:T(8,128)(2,1)S(1)} %add_convert_fusion.15), channel_id=1, source_target_pairs={{0,8},{8,0},{16,24},{24,16},{1,9},{9,1},{17,25},{25,17},{2,10},{10... | collective-permute-start | bytes 786440 | tf_op jit(solution)/shard_map/ppermute | solution.py:41
  425.9 15.3 %collective-permute-start.63 = (f32[1024]{0:T(1024)S(1)}, f32[1024]{0:T(1024)S(1)}, u32[]{:S(2)}, u32[]{:S(2)}) collective-permute-start(f32[1024]{0:T(1024)S(1)} %get-tuple-element.631), channel_id=1, source_target_pairs={{0,4},{2,6},{4,0},{6,2},{1,5},{3,7},{5,1},{7,3},{8,12},{10,14},{12... | collective-permute-start | bytes 12296 | tf_op jit(solution)/shard_map/ppermute | solution.py:45
  450.6 18.9 %collective-permute-start.71 = (bf16[256,512]{1,0:T(8,128)(2,1)S(1)}, bf16[256,512]{1,0:T(8,128)(2,1)S(1)}, u32[]{:S(2)}, u32[]{:S(2)}) collective-permute-start(bf16[256,512]{1,0:T(8,128)(2,1)S(1)} %add_convert_fusion.13.refs_0_), channel_id=1, source_target_pairs={{0,8},{8,0},{16,24},{24,16},{1,9},{9,1},{17,25},{25,17},{2,10},{10... | collective-permute-start | bytes 786440 | tf_op jit(solution)/shard_map/ppermute | solution.py:41
  451.3 18.2 %collective-permute-start.74 = (bf16[256,512]{1,0:T(8,128)(2,1)S(1)}, bf16[256,512]{1,0:T(8,128)(2,1)S(1)}, u32[]{:S(2)}, u32[]{:S(2)}) collective-permute-start(bf16[256,512]{1,0:T(8,128)(2,1)S(1)} %add_convert_fusion.11.refs_4_), channel_id=1, source_target_pairs={{0,16},{8,24},{16,0},{24,8},{1,17},{9,25},{17,1},{25,9},{2,18},{10... | collective-permute-start | bytes 786440 | tf_op jit(solution)/shard_map/ppermute | solution.py:41
  451.7 17.8 %collective-permute-start.72 = (bf16[256,512]{1,0:T(8,128)(2,1)S(1)}, bf16[256,512]{1,0:T(8,128)(2,1)S(1)}, u32[]{:S(2)}, u32[]{:S(2)}) collective-permute-start(bf16[256,512]{1,0:T(8,128)(2,1)S(1)} %collective-permute-done.69.refs_1_), channel_id=1, source_target_pairs={{0,8},{8,0},{16,24},{24,16},{1,9},{9,1},{17,25},{25,17},{2,10},{10... | collective-permute-start | bytes 786440 | tf_op jit(solution)/shard_map/ppermute | solution.py:41
  453.2 16.3 %collective-permute-start.75 = (bf16[256,512]{1,0:T(8,128)(2,1)S(1)}, bf16[256,512]{1,0:T(8,128)(2,1)S(1)}, u32[]{:S(2)}, u32[]{:S(2)}) collective-permute-start(bf16[256,512]{1,0:T(8,128)(2,1)S(1)} %collective-permute-done.73.refs_5_), channel_id=1, source_target_pairs={{0,16},{8,24},{16,0},{24,8},{1,17},{9,25},{17,1},{25,9},{2,18},{10... | collective-permute-start | bytes 786440 | tf_op jit(solution)/shard_map/ppermute | solution.py:41
  (153 other events, 1647.9 us)
Sparse Core Ops, SparseCore 0:
  45.0 55.4 all-gather.1
  249.8 187.3 all-reduce.2
